TPU v7x, 32 devices: a whole 2x2x4 slice. The times are simulated.
32 devices in a mesh: dp: 2 (over core), expert: 4 (over y, x), tensor: 4 (over z).
Axes of the slice: x: 2, y: 2, z: 4, core: 2. Of those that a mesh axis runs over, the one named last changes fastest.
Arguments:
- tokens: bfloat16 [16384, 768], P(('dp', 'expert')), may hold values from -6 to 6
- prev_logits: float32 [16384, 12], P(('dp', 'expert')), may hold values from -3 to 3
- routes: int32 [16384, 2], P(('dp', 'expert')), may hold values from 0 to 11, all different within a row; in each aligned block of 2048 rows (0 to 2047, 2048 to 4095, ...) at most 480 rows name the same one
- segments: int32 [16384], P(('dp', 'expert')), may hold values from 0 to 15, as said below
- gain_one: float32 [768], P('dp'), may hold values from 0.5 to 1.5
- w_qkv: float32 [768, 3, 768], P('dp', None, 'tensor'), may hold values from -0.21875 to 0.21875
- w_out: float32 [768, 768], P('tensor', 'dp'), may hold values from -0.875 to 0.875
- gain_two: float32 [768], P('dp'), may hold values from 0.5 to 1.5
- router: float32 [768, 12], P('dp'), may hold values from -0.109375 to 0.109375
- const_proj: float32 [768, 4], P('dp'), may hold values from -0.21875 to 0.21875
- const_vec: float32 [2, 768], P(None, 'dp'), may hold values from -6 to 6
- w_gate_up: float32 [8, 768, 2, 2048], P('expert', 'dp', None, 'tensor'), may hold values from -0.21875 to 0.21875
- w_down: float32 [8, 2048, 768], P('expert', 'tensor', 'dp'), may hold values from -2 to 2
- cotangent: bfloat16 [16384, 768], P(('dp', 'expert')), may hold values from -6 to 6
Outputs:
- output: float32 [16384, 768], P(('dp', 'expert'))
- grad_tokens: float32 [16384, 768], P(('dp', 'expert'))
- grad_gain_one: float32 [768], P('dp')
- grad_w_qkv: float32 [768, 3, 768], P('dp', None, 'tensor')
- grad_w_out: float32 [768, 768], P('tensor', 'dp')
- grad_gain_two: float32 [768], P('dp')
- grad_router: float32 [768, 12], P('dp')
- grad_const_proj: float32 [768, 4], P('dp')
- grad_const_vec: float32 [2, 768], P(None, 'dp')
- grad_w_gate_up: float32 [8, 768, 2, 2048], P('expert', 'dp', None, 'tensor')
- grad_w_down: float32 [8, 2048, 768], P('expert', 'tensor', 'dp')
Inputs may be any that keep to these rules, and one draw needn't show every extreme that they name: `routes`: ids below 8 name expert networks, 8 the zero expert, 9 the copy expert, 10 and 11 the constant experts; a token's two ids differ; in the 2048 rows of one device no id is named more than 480 times. `segments`: within each sequence of 1024 tokens the numbers start at 0 and rise by one at each document start; documents start only at multiples of 64 and hold 64 to 768 tokens; the first sequence holds one of 768 tokens, and the last holds documents of 64 tokens only.
All inputs are finite; a program needn't handle non-finite values.
Results may differ from a plain program's by a relative error of at most 0.025.
Values may be sent and summed in bfloat16 or wider, within the bound.
No kernel may reach another device: no remote copies, remote signals or barrier semaphores. Data moves between devices by JAX's collectives and lax.ppermute only.
A program may use at most 256 MiB of HBM per device.

v0:
```python
import jax
import jax.numpy as jnp
from jax import lax
from jax.sharding import PartitionSpec as P

D = 768
HD = 64
EXPERTS = 8
ALL_EXPERTS = 12
SEQ_LEN = 1024
CAPACITY = 480


EPS = 1e-06
NEG = -1e30


def norm_rows(values, gain):
    factor = lax.rsqrt(jnp.mean(values * values, axis=-1, keepdims=True) + EPS)
    return (values * factor * gain, factor)


def norm_back(values, factor, gain, upstream):
    normed = values * factor
    weighted = upstream * gain
    inner = jnp.mean(weighted * normed, axis=-1, keepdims=True)
    return (factor * (weighted - normed * inner), jnp.sum(upstream * normed, axis=0))


def slot_tables(routes):
    flat_ids = routes.reshape(-1)
    entries = flat_ids.shape[0]
    one_hot = (flat_ids[:, None] == jnp.arange(EXPERTS, dtype=jnp.int32)[None, :]).astype(jnp.int32)
    places = jnp.sum(one_hot * (jnp.cumsum(one_hot, axis=0) - 1), axis=1)
    slot_ids = jnp.where(flat_ids < EXPERTS, flat_ids * CAPACITY + places, EXPERTS * CAPACITY)
    lookup = jnp.full((EXPERTS * CAPACITY + 1,), entries, jnp.int32)
    lookup = lookup.at[slot_ids].set(jnp.arange(entries, dtype=jnp.int32))
    return (slot_ids, lookup[: EXPERTS * CAPACITY])


def allowed_pairs(segment_ids, offset, span_len):
    total_len = segment_ids.shape[0]
    query_at = offset + jnp.arange(span_len, dtype=jnp.int32)
    key_at = jnp.arange(total_len, dtype=jnp.int32)
    same_doc = segment_ids[offset : offset + span_len][:, None] == segment_ids[None, :]
    return same_doc & (key_at[None, :] <= query_at[:, None])


def attend_forward(packed):
    queries, keys_in, values, segment_ids = packed
    total_len = queries.shape[0]
    span_len = min(512, total_len)
    scale = HD ** (-0.5)
    outputs = []
    log_sums = []
    for offset in range(0, total_len, span_len):
        scores = (
            jnp.einsum(
                "qhd,khd->hqk",
                queries[offset : offset + span_len],
                keys_in,
                preferred_element_type=jnp.float32,
            )
            * scale
        )
        scores = jnp.where(allowed_pairs(segment_ids, offset, span_len)[None], scores, NEG)
        highest = jnp.max(scores, axis=-1, keepdims=True)
        totals = jnp.sum(jnp.exp(scores - highest), axis=-1, keepdims=True)
        log_total = highest + jnp.log(totals)
        weights = jnp.exp(scores - log_total).astype(jnp.bfloat16)
        outputs.append(
            jnp.einsum("hqk,khd->qhd", weights, values, preferred_element_type=jnp.float32).astype(
                jnp.bfloat16
            )
        )
        log_sums.append(log_total[:, :, 0])
    return (jnp.concatenate(outputs, axis=0), jnp.concatenate(log_sums, axis=1))


def attend_backward(packed):
    queries, keys_in, values, segment_ids, log_sums, grad_out = packed
    total_len = queries.shape[0]
    span_len = min(512, total_len)
    scale = HD ** (-0.5)
    grad_keys = jnp.zeros(keys_in.shape, jnp.float32)
    grad_values = jnp.zeros(values.shape, jnp.float32)
    grad_queries = []
    for offset in range(0, total_len, span_len):
        chosen = queries[offset : offset + span_len]
        scores = (
            jnp.einsum("qhd,khd->hqk", chosen, keys_in, preferred_element_type=jnp.float32) * scale
        )
        scores = jnp.where(allowed_pairs(segment_ids, offset, span_len)[None], scores, NEG)
        weights = jnp.exp(scores - log_sums[:, offset : offset + span_len, None])
        grad_here = grad_out[offset : offset + span_len]
        grad_values = grad_values + jnp.einsum(
            "hqk,qhd->khd",
            weights.astype(jnp.bfloat16),
            grad_here,
            preferred_element_type=jnp.float32,
        )
        grad_weights = jnp.einsum(
            "qhd,khd->hqk", grad_here, values, preferred_element_type=jnp.float32
        )
        grad_scores = (
            weights * (grad_weights - jnp.sum(weights * grad_weights, axis=-1, keepdims=True))
        ).astype(jnp.bfloat16)
        grad_queries.append(
            (
                jnp.einsum("hqk,khd->qhd", grad_scores, keys_in, preferred_element_type=jnp.float32)
                * scale
            ).astype(jnp.bfloat16)
        )
        grad_keys = (
            grad_keys
            + jnp.einsum("hqk,qhd->khd", grad_scores, chosen, preferred_element_type=jnp.float32)
            * scale
        )
    return (
        jnp.concatenate(grad_queries, axis=0),
        grad_keys.astype(jnp.bfloat16),
        grad_values.astype(jnp.bfloat16),
    )


def on_device(
    tokens,
    prev_logits,
    routes,
    segments,
    gain_one,
    w_qkv,
    w_out,
    gain_two,
    router,
    const_proj,
    const_vec,
    w_gate_up,
    w_down,
    cotangent,
):
    row_count = tokens.shape[0]
    seq_count = row_count // SEQ_LEN
    ranks = lax.axis_size("expert")
    local_experts = EXPERTS // ranks
    (
        norm_gain_a,
        in_weights,
        out_weights,
        norm_gain_b,
        route_weights,
        mix_weights,
        const_rows,
        gate_up,
        down_proj,
    ) = (
        lax.all_gather(gain_one.astype(jnp.bfloat16), "dp", axis=0, tiled=True),
        lax.all_gather(w_qkv.astype(jnp.bfloat16), "dp", axis=0, tiled=True),
        lax.all_gather(w_out.astype(jnp.bfloat16), "dp", axis=1, tiled=True),
        lax.all_gather(gain_two.astype(jnp.bfloat16), "dp", axis=0, tiled=True),
        lax.all_gather(router.astype(jnp.bfloat16), "dp", axis=0, tiled=True),
        lax.all_gather(const_proj.astype(jnp.bfloat16), "dp", axis=0, tiled=True),
        lax.all_gather(const_vec.astype(jnp.bfloat16), "dp", axis=1, tiled=True),
        lax.all_gather(w_gate_up.astype(jnp.bfloat16), "dp", axis=1, tiled=True),
        lax.all_gather(w_down.astype(jnp.bfloat16), "dp", axis=2, tiled=True),
    )
    gain_a_full = norm_gain_a.astype(jnp.float32)
    gain_b_full = norm_gain_b.astype(jnp.float32)
    width = out_weights.shape[0]
    heads_here = width // HD
    in_flat = in_weights.reshape(D, 3 * width)
    inputs = tokens.astype(jnp.float32)
    normed_a, factor_a = norm_rows(inputs, gain_a_full)
    normed_low = normed_a.astype(jnp.bfloat16)
    projected = jnp.dot(normed_low, in_flat, preferred_element_type=jnp.float32).astype(
        jnp.bfloat16
    )
    projected = projected.reshape(seq_count, SEQ_LEN, 3, heads_here, HD)
    seg_rows = segments.reshape(seq_count, SEQ_LEN)
    attended, log_sums = lax.map(
        attend_forward, (projected[:, :, 0], projected[:, :, 1], projected[:, :, 2], seg_rows)
    )
    attended = attended.reshape(row_count, width)
    attn_total = lax.psum(
        jnp.dot(attended, out_weights, preferred_element_type=jnp.float32).astype(jnp.bfloat16),
        "tensor",
    ).astype(jnp.float32)
    after_attn = inputs + attn_total
    normed_b, factor_b = norm_rows(after_attn, gain_b_full)
    routed_low = normed_b.astype(jnp.bfloat16)
    logits = jnp.dot(routed_low, route_weights, preferred_element_type=jnp.float32) + prev_logits
    chances = jax.nn.softmax(logits, axis=-1)
    route_hot = (
        routes[:, :, None] == jnp.arange(ALL_EXPERTS, dtype=jnp.int32)[None, None, :]
    ).astype(jnp.float32)
    gate_values = jnp.sum(route_hot * chances[:, None, :], axis=-1)
    kinds = (
        routes[:, :, None] == (EXPERTS + jnp.arange(4, dtype=jnp.int32))[None, None, :]
    ).astype(jnp.float32)
    mixing = jax.nn.softmax(
        jnp.dot(routed_low, mix_weights, preferred_element_type=jnp.float32).reshape(
            row_count, 2, 2
        ),
        axis=-1,
    )
    const_values = const_rows.astype(jnp.float32)
    constants = (
        mixing[:, :, 0:1] * normed_b[:, None, :] + mixing[:, :, 1:2] * const_values[None, :, :]
    )
    others = (
        kinds[:, :, 1:2] * normed_b[:, None, :]
        + kinds[:, :, 2:3] * constants[:, None, 0, :]
        + kinds[:, :, 3:4] * constants[:, None, 1, :]
    )
    slot_ids, lookup = slot_tables(routes)
    padded_rows = jnp.concatenate([routed_low, jnp.zeros((1, D), jnp.bfloat16)], axis=0)
    outgoing = padded_rows[lookup // 2].reshape(ranks, local_experts, CAPACITY, D)
    incoming = lax.all_to_all(outgoing, "expert", split_axis=0, concat_axis=0, tiled=True)
    gate_up_flat = gate_up.reshape(local_experts, D, -1)
    hidden_here = down_proj.shape[1]

    def expert_front(received):
        both_parts = jnp.einsum(
            "secd,edf->secf", received, gate_up_flat, preferred_element_type=jnp.float32
        )
        active = (
            jax.nn.silu(both_parts[..., :hidden_here]) * both_parts[..., hidden_here:]
        ).astype(jnp.bfloat16)
        return (both_parts, active)

    both_kept, act_kept = expert_front(incoming)
    partial_out = jnp.einsum(
        "secf,efd->secd", act_kept, down_proj, preferred_element_type=jnp.float32
    )
    expert_out = lax.psum(partial_out.astype(jnp.bfloat16), "tensor")
    returned = lax.all_to_all(expert_out, "expert", split_axis=0, concat_axis=0, tiled=True)
    returned_pad = jnp.concatenate(
        [returned.reshape(EXPERTS * CAPACITY, D), jnp.zeros((1, D), jnp.bfloat16)], axis=0
    )
    picked = returned_pad[slot_ids].reshape(row_count, 2, D).astype(jnp.float32)
    branch_out = picked + others
    output = after_attn + jnp.sum(gate_values[:, :, None] * branch_out, axis=1)
    upstream = cotangent.astype(jnp.float32)
    grad_gates = jnp.sum(branch_out * upstream[:, None, :], axis=-1)
    copy_weight = jnp.sum(gate_values * kinds[:, :, 1], axis=1)
    const_weight = jnp.sum(gate_values[:, :, None] * kinds[:, :, 2:], axis=1)
    grad_normed = (copy_weight + jnp.sum(const_weight * mixing[:, :, 0], axis=1))[
        :, None
    ] * upstream
    dot_normed = jnp.sum(upstream * normed_b, axis=1)
    dot_const = jnp.dot(upstream, const_values.T, precision=lax.Precision.HIGHEST)
    grad_mixing = const_weight[:, :, None] * jnp.stack(
        [jnp.broadcast_to(dot_normed[:, None], (row_count, 2)), dot_const], axis=-1
    )
    grad_mix_logits = (
        (mixing * (grad_mixing - jnp.sum(mixing * grad_mixing, axis=-1, keepdims=True)))
        .reshape(row_count, 4)
        .astype(jnp.bfloat16)
    )
    grad_const_vec = jnp.dot(
        (const_weight * mixing[:, :, 1]).T, upstream, precision=lax.Precision.HIGHEST
    )
    grad_routed = jnp.dot(grad_mix_logits, mix_weights.T, preferred_element_type=jnp.float32)
    grad_mix_w = jnp.dot(routed_low.T, grad_mix_logits, preferred_element_type=jnp.float32)
    grad_chances = jnp.sum(route_hot * grad_gates[:, :, None], axis=1)
    grad_logits = (
        chances * (grad_chances - jnp.sum(chances * grad_chances, axis=-1, keepdims=True))
    ).astype(jnp.bfloat16)
    grad_routed = grad_routed + jnp.dot(
        grad_logits, route_weights.T, preferred_element_type=jnp.float32
    )
    grad_route_w = jnp.dot(routed_low.T, grad_logits, preferred_element_type=jnp.float32)
    scaled_up = (
        (gate_values[:, :, None] * upstream[:, None, :])
        .reshape(2 * row_count, D)
        .astype(jnp.bfloat16)
    )
    padded_grad = jnp.concatenate([scaled_up, jnp.zeros((1, D), jnp.bfloat16)], axis=0)
    grad_outgoing = padded_grad[lookup].reshape(ranks, local_experts, CAPACITY, D)
    grad_incoming = lax.all_to_all(grad_outgoing, "expert", split_axis=0, concat_axis=0, tiled=True)
    both_now, act_now = expert_front(incoming)
    grad_act = jnp.einsum(
        "secd,efd->secf", grad_incoming, down_proj, preferred_element_type=jnp.float32
    )
    gate_part = both_now[..., :hidden_here]
    up_part = both_now[..., hidden_here:]
    sigmoid_gate = jax.nn.sigmoid(gate_part)
    grad_gate = grad_act * up_part * sigmoid_gate * (1.0 + gate_part * (1.0 - sigmoid_gate))
    grad_up = grad_act * gate_part * sigmoid_gate
    grad_both = jnp.concatenate([grad_gate, grad_up], axis=-1).astype(jnp.bfloat16)
    grad_gate_up = jnp.einsum(
        "secd,secf->edf", incoming, grad_both, preferred_element_type=jnp.float32
    ).reshape(local_experts, D, 2, hidden_here)
    grad_down = jnp.einsum(
        "secf,secd->efd", act_now, grad_incoming, preferred_element_type=jnp.float32
    )
    row_terms = jnp.einsum(
        "secf,edf->secd", grad_both, gate_up_flat, preferred_element_type=jnp.float32
    )
    grad_rows = lax.psum(row_terms.astype(jnp.bfloat16), "tensor")
    grad_back = lax.all_to_all(grad_rows, "expert", split_axis=0, concat_axis=0, tiled=True)
    grad_pad = jnp.concatenate(
        [grad_back.reshape(EXPERTS * CAPACITY, D), jnp.zeros((1, D), jnp.bfloat16)], axis=0
    )
    grad_picked = grad_pad[slot_ids]
    grad_routed = grad_routed + jnp.sum(
        grad_picked.reshape(row_count, 2, D).astype(jnp.float32), axis=1
    )
    grad_mid, grad_gain_b = norm_back(after_attn, factor_b, gain_b_full, grad_normed + grad_routed)
    grad_after = upstream + grad_mid
    grad_after_low = grad_after.astype(jnp.bfloat16)
    grad_out_w = jnp.dot(attended.T, grad_after_low, preferred_element_type=jnp.float32)
    grad_attended = jnp.dot(
        grad_after_low, out_weights.T, preferred_element_type=jnp.float32
    ).astype(jnp.bfloat16)
    grad_attended = grad_attended.reshape(seq_count, SEQ_LEN, heads_here, HD)
    grad_query, grad_key, grad_value = lax.map(
        attend_backward,
        (
            projected[:, :, 0],
            projected[:, :, 1],
            projected[:, :, 2],
            seg_rows,
            log_sums,
            grad_attended,
        ),
    )
    grad_proj = jnp.stack([grad_query, grad_key, grad_value], axis=2).reshape(row_count, 3 * width)
    grad_in_w = jnp.dot(normed_low.T, grad_proj, preferred_element_type=jnp.float32).reshape(
        D, 3, width
    )
    grad_normed_a = lax.psum(
        jnp.dot(grad_proj, in_flat.T, preferred_element_type=jnp.float32).astype(jnp.bfloat16),
        "tensor",
    ).astype(jnp.float32)
    grad_input_mid, grad_gain_a = norm_back(inputs, factor_a, gain_a_full, grad_normed_a)
    grad_tokens = grad_after + grad_input_mid
    grad_gain_a, grad_in_w, grad_out_w, grad_gain_b, grad_route_w, grad_mix_w, grad_const_vec = (
        lax.psum(grad_gain_a.astype(jnp.bfloat16), "expert").astype(jnp.float32),
        lax.psum(grad_in_w.astype(jnp.bfloat16), "expert").astype(jnp.float32),
        lax.psum(grad_out_w.astype(jnp.bfloat16), "expert").astype(jnp.float32),
        lax.psum(grad_gain_b.astype(jnp.bfloat16), "expert").astype(jnp.float32),
        lax.psum(grad_route_w.astype(jnp.bfloat16), "expert").astype(jnp.float32),
        lax.psum(grad_mix_w.astype(jnp.bfloat16), "expert").astype(jnp.float32),
        lax.psum(grad_const_vec.astype(jnp.bfloat16), "expert").astype(jnp.float32),
    )
    reduced = (
        lax.psum_scatter(
            grad_gain_a.astype(jnp.bfloat16), "dp", scatter_dimension=0, tiled=True
        ).astype(jnp.float32),
        lax.psum_scatter(
            grad_in_w.astype(jnp.bfloat16), "dp", scatter_dimension=0, tiled=True
        ).astype(jnp.float32),
        lax.psum_scatter(
            grad_out_w.astype(jnp.bfloat16), "dp", scatter_dimension=1, tiled=True
        ).astype(jnp.float32),
        lax.psum_scatter(
            grad_gain_b.astype(jnp.bfloat16), "dp", scatter_dimension=0, tiled=True
        ).astype(jnp.float32),
        lax.psum_scatter(
            grad_route_w.astype(jnp.bfloat16), "dp", scatter_dimension=0, tiled=True
        ).astype(jnp.float32),
        lax.psum_scatter(
            grad_mix_w.astype(jnp.bfloat16), "dp", scatter_dimension=0, tiled=True
        ).astype(jnp.float32),
        lax.psum_scatter(
            grad_const_vec.astype(jnp.bfloat16), "dp", scatter_dimension=1, tiled=True
        ).astype(jnp.float32),
        lax.psum_scatter(
            grad_gate_up.astype(jnp.bfloat16), "dp", scatter_dimension=1, tiled=True
        ).astype(jnp.float32),
        lax.psum_scatter(
            grad_down.astype(jnp.bfloat16), "dp", scatter_dimension=2, tiled=True
        ).astype(jnp.float32),
    )
    dense_part = reduced[:7]
    return (
        output,
        grad_tokens,
        dense_part[0],
        dense_part[1],
        dense_part[2],
        dense_part[3],
        dense_part[4],
        dense_part[5],
        dense_part[6],
        reduced[7],
        reduced[8],
    )


def solution(mesh):
    placed = (
        P(("dp", "expert"), None),
        P(("dp", "expert"), None),
        P(("dp", "expert"), None),
        P(("dp", "expert")),
        P("dp"),
        P("dp", None, "tensor"),
        P("tensor", "dp"),
        P("dp"),
        P("dp", None),
        P("dp", None),
        P(None, "dp"),
        P("expert", "dp", None, "tensor"),
        P("expert", "tensor", "dp"),
        P(("dp", "expert"), None),
    )
    return jax.shard_map(
        on_device,
        mesh=mesh,
        in_specs=placed,
        out_specs=(
            P(("dp", "expert"), None),
            P(("dp", "expert"), None),
            P("dp"),
            P("dp", None, "tensor"),
            P("tensor", "dp"),
            P("dp"),
            P("dp", None),
            P("dp", None),
            P(None, "dp"),
            P("expert", "dp", None, "tensor"),
            P("expert", "tensor", "dp"),
        ),
        check_vma=False,
    )
```

profile of v0, /device:TPU:0, one launch (start us, length us, event | category | flops | bytes accessed | tf_op | source)
XLA Modules:
  0.0 1401.0 jit_solution(1164781175936519515)
XLA Ops:
  33.4 23.3 %while.26 = (s32[]{:T(128)}, bf16[2,1024,3,64]{1,3,2,0:T(8,128)(2,1)S(1)}, f32[2,3,1024]{2,1,0:T(4,128)S(1)}, bf16[2,1024,3,64]{1,3,2,0:T(8,128)(2,1)S(1)}, s32[...) while((s32[]{:T(128)}, ...), condition=%wide.region_6.7_spmd, body=%wide.region_1.6_spmd.sunk | while | flops 844038656 | bytes 45242512 | solution.py:180
  85.3 15.5 %scatter_custom_fusion = s32[3841]{0:T(1024)S(1)} fusion(s32[4096]{0:T(1024)S(1)} %bitcast.392, s32[4096]{0:T(1024)S(1)} %iota.72, s32[]{:T(128)} %constant.103.clone.1), kind=kCustom, calls=%fused_computation.254 | custom fusion | bytes 15368 | tf_op jit(solution)/shard_map/scatter | solution.py:37
  100.9 87.5 %all-reduce.15.cloned.1.call-done = bf16[2048,768]{1,0:T(8,128)(2,1)} async-done(((bf16[2048,768]{1,0:T(8,128)(2,1)}), bf16[2048,768]{1,0:T(8,128)(2,1)}) %all-reduce.15.cloned.1.call-update) | async-done | bytes 3145744 | tf_op jit(solution)/shard_map/psum | solution.py:184
  199.0 12.1 gather_fusion
  221.2 8.5 mul.424
  229.6 16.1 %mul.432 = f32[4096,768]{1,0:T(8,128)} reshape(f32[2048,2,768]{2,1,0:T(2,128)} %mul.424) | data formatting | bytes 25165824 | tf_op jit(solution)/shard_map/mul | solution.py:244
  263.2 18.4 %gather_fusion.2 = bf16[3840,768]{1,0:T(8,128)(2,1)} fusion(bf16[4097,768]{1,0:T(8,128)(2,1)} %concatenate.27, s32[4096]{0:T(1024)S(1)} %get-tuple-element.257), kind=kCustom, calls=%fused_computation.2 | custom fusion | bytes 11811840 | tf_op jit(solution)/shard_map/gather | solution.py:279
  296.4 13.1 convolution_bitcast_fusion
  309.5 43.8 %all-to-all-done.2 = bf16[4,2,480,768]{3,2,1,0:T(8,128)(2,1)} async-done(((bf16[4,2,480,768]{3,2,1,0:T(8,128)(2,1)}), bf16[4,2,480,768]{3,2,1,0:T(8,128)(2,1)}, u32[]{:S(2)}, u32[]{:S(2)}) %all-to-all-start.2) | async-done | bytes 5898272 | tf_op jit(solution)/shard_map/all_to_all | solution.py:280
  353.3 13.7 fusion.100
  367.1 10.5 convert_bitcast_fusion
  400.6 381.6 %all-reduce.19.cloned.1.call-done = (bf16[4,2,480,768]{3,2,0,1:T(8,128)(2,1)}, bf16[4,2,480,768]{3,2,0,1:T(8,128)(2,1)}) async-done(((bf16[4,2,480,768]{3,2,0,1:T(8,128)(2,1)}, bf16[4,2,480,768]{3,2,0,1:T(8,128)(2,1)}), (bf16[4,2,480,768]{3,2,0,1:T(8,128)(2,1)}, bf16[4,2,480,768]{3,2,0,1:T(8,128)(2,1)})) %all-reduce.19.cloned.1.call-update) | async-done | bytes 11796496 | tf_op jit(solution)/shard_map/psum | solution.py:235
  792.9 10.6 multiply_add_fusion
  803.5 9.9 fusion.156
  829.3 29.6 %all-to-all-done.1 = bf16[4,2,480,768]{3,2,1,0:T(8,128)(2,1)} async-done(((bf16[4,2,480,768]{3,2,1,0:T(8,128)(2,1)}), bf16[4,2,480,768]{3,2,1,0:T(8,128)(2,1)}, u32[]{:S(2)}, u32[]{:S(2)}) %all-to-all-start.1) | async-done | bytes 5898272 | tf_op jit(solution)/shard_map/all_to_all | solution.py:236
  869.7 22.9 %gather_fusion.1 = bf16[4096,768]{1,0:T(8,128)(2,1)} fusion(bf16[3841,768]{1,0:T(8,128)(2,1)} %concatenate.26, s32[4096]{0:T(1024)S(1)} %broadcast_clamp_fusion), kind=kCustom, calls=%fused_computation.1 | custom fusion | bytes 12599296 | tf_op jit(solution)/shard_map/gather | solution.py:240
  892.5 14.3 %reshape.492 = f32[2048,2,768]{2,1,0:T(2,128)} reshape(bf16[4096,768]{1,0:T(8,128)(2,1)} %gather_fusion.1) | data formatting | bytes 18874368 | tf_op jit(solution)/shard_map/convert_element_type | solution.py:240
  906.9 46.1 %multiply_reduce_fusion.2 = (f32[2048,2]{1,0:T(8,128)}, f32[2048,768]{1,0:T(8,128)}) fusion(f32[2048,768]{1,0:T(8,128)} %convert_element_type.270, f32[2048,2]{1,0:T(8,128)} %copy.117, f32[2048,2,768]{2,1,0:T(2,128)} %reshape.492, f32[2048,768]{1,0:T(8,128)} %bitcast.361, f32[2048,2]{1,0:T(8,128)} %copy.129, f32[2048,768]{1,0:T(8,128)} %bitcast.362, ...), kind=kLoop, calls=%fused_computation.127 | loop fusion | flops 29880320 | bytes 44122112 | tf_op jit(solution)/shard_map/reduce_sum | solution.py:244
  960.6 22.5 %gather_fusion.3 = bf16[4096,768]{1,0:T(8,128)(2,1)} fusion(bf16[3841,768]{1,0:T(8,128)(2,1)} %concatenate.29, s32[4096]{0:T(1024)S(1)} %broadcast_clamp_fusion), kind=kCustom, calls=%fused_computation.3 | custom fusion | bytes 12599296 | tf_op jit(solution)/shard_map/gather | solution.py:305
  983.1 14.3 %reshape.493 = f32[2048,2,768]{2,1,0:T(2,128)} reshape(bf16[4096,768]{1,0:T(8,128)(2,1)} %gather_fusion.3) | data formatting | bytes 18874368 | tf_op jit(solution)/shard_map/convert_element_type | solution.py:307
  997.4 36.5 %reduce_sum.234 = f32[2048,768]{1,0:T(8,128)} reduce(f32[2048,2,768]{2,1,0:T(2,128)} %reshape.493, f32[]{:T(128)} %constant.99.clone.1), dimensions={1}, to_apply=%region_29.30 | reduce | flops 1572864 | bytes 18874372 | tf_op jit(solution)/shard_map/reduce_sum | solution.py:306
  1034.0 10.8 multiply_reduce_fusion.4
  1044.8 7.6 multiply_add_fusion.1
  1063.3 65.8 %while.27 = (s32[]{:T(128)}, bf16[2,1024,3,64]{1,3,2,0:T(8,128)(2,1)}, bf16[2,1024,3,64]{1,3,2,0:T(8,128)(2,1)}, bf16[2,1024,3,64]{1,3,2,0:T(8,128)(2,1)}, bf16[...) while((s32[]{:T(128)}, ...), condition=%wide.region_34.35_spmd, body=%wide.region_31.34_spmd.sunk | while | flops 2065757696 | bytes 136076128 | solution.py:317
  1077.2 7.6 multiply_convert_fusion.7
  1109.9 7.6 multiply_convert_fusion.7
  1147.6 7.5 bitcast_convert_fusion.1
  1158.4 13.5 bitcast_convert_fusion
  1180.4 6.6 reshape.548
  1218.3 20.0 %all-reduce.21.cloned.1.call-done = (bf16[384,3,192]{0,2,1:T(8,128)(2,1)}, bf16[192,384]{1,0:T(8,128)(2,1)}) async-done(((bf16[384,3,192]{0,2,1:T(8,128)(2,1)}, bf16[192,384]{1,0:T(8,128)(2,1)}), (bf16[384,3,192]{0,2,1:T(8,128)(2,1)}, bf16[192,384]{1,0:T(8,128)(2,1)})) %all-reduce.21.cloned.1.call-update) | async-done | bytes 589840 | tf_op jit(solution)/shard_map/psum | solution.py:340
  1241.9 119.8 %all-reduce.17.cloned.1.call-done = bf16[2048,768]{1,0:T(8,128)(2,1)} async-done(((bf16[2048,768]{1,0:T(8,128)(2,1)}), bf16[2048,768]{1,0:T(8,128)(2,1)}) %all-reduce.17.cloned.1.call-update) | async-done | bytes 3145744 | tf_op jit(solution)/shard_map/psum | solution.py:332
  1368.1 16.1 %all-reduce.7 = (bf16[384]{0:T(512)(128)(2,1)S(1)}, bf16[384]{0:T(512)(128)(2,1)S(1)}, bf16[384,12]{0,1:T(8,128)(2,1)S(1)}, bf16[384,4]{0,1:T(4,128)(2,1)S(1)}, bf16[2,384]{1,0:T(2,128)(2,1)S(1)}) all-reduce(bf16[384]{0:T(512)(128)(2,1)S(1)} %dynamic-slice.1, ...), channel_id=1, replica_groups=mesh['dp'=2,'expert'=4,'tensor'=4] {'expert'}, use_global_device_ids=true, to_apply=%region_38.39 | all-reduce | flops 7680 | bytes 30720 | tf_op jit(solution)/shard_map/psum | solution.py:339
  (413 shorter events, 337.8 us)
Async XLA Ops:
  8.0 180.4 %all-reduce.15.cloned.1.call-start = ((), (), s32[]{:S(2)}) async-start(), calls=%async_computation.11 | async-start | bytes 6291456 | tf_op jit(solution)/shard_map/psum | solution.py:184
  66.0 126.5 %copy-start.3 = (bf16[2048,768]{1,0:T(8,128)(2,1)S(1)}, bf16[2048,768]{1,0:T(8,128)(2,1)}, u32[]{:S(2)}) copy-start(bf16[2048,768]{1,0:T(8,128)(2,1)} %param.31) | copy-start | bytes 9437188
  82.9 109.6 %copy-start.57 = (f32[768]{0:T(1024)S(1)}, f32[768]{0:T(1024)}, u32[]{:S(2)}) copy-start(f32[768]{0:T(1024)} %reshape.541) | copy-start | bytes 9220
  211.1 71.3 %all-to-all-start = ((bf16[4,2,480,768]{3,2,1,0:T(8,128)(2,1)}), bf16[4,2,480,768]{3,2,1,0:T(8,128)(2,1)}, u32[]{:S(2)}, u32[]{:S(2)}) async-start(bf16[4,2,480,768]{3,2,1,0:T(8,128)(2,1)} %bitcast.363), calls=%async_computation | async-start | bytes 11796480 | tf_op jit(solution)/shard_map/all_to_all | solution.py:218
  216.5 73.7 %all-gather.5.cloned.1.call-start = ((), (), s32[]{:S(2)}) async-start(), calls=%async_computation.12 | async-start | bytes 4718592 | tf_op jit(solution)/shard_map/all_gather | solution.py:164
  229.6 17.9 %copy-start.40 = (f32[2048,12]{0,1:T(8,128)S(1)}, f32[2048,12]{0,1:T(8,128)}, u32[]{:S(2)}) copy-start(f32[2048,12]{0,1:T(8,128)} %param.19) | copy-start | bytes 294916
  282.4 70.9 %all-to-all-start.2 = ((bf16[4,2,480,768]{3,2,1,0:T(8,128)(2,1)}), bf16[4,2,480,768]{3,2,1,0:T(8,128)(2,1)}, u32[]{:S(2)}, u32[]{:S(2)}) async-start(bf16[4,2,480,768]{3,2,1,0:T(8,128)(2,1)} %bitcast.364), calls=%async_computation.2 | async-start | bytes 11796480 | tf_op jit(solution)/shard_map/all_to_all | solution.py:280
  287.6 21.9 %all-gather.7.cloned.1.call-start = ((), (), s32[]{:S(2)}) async-start(), calls=%async_computation.13 | async-start | bytes 2359296 | tf_op jit(solution)/shard_map/all_gather | solution.py:165
  290.0 492.1 %all-reduce.19.cloned.1.call-start = ((), (), s32[]{:S(2)}) async-start(), calls=%async_computation.22 | async-start | bytes 23592960 | tf_op jit(solution)/shard_map/psum | solution.py:235
  353.3 13.8 copy-start.26
  397.7 422.1 %copy-start.38 = (f32[2048,2]{0,1:T(2,128)}, f32[2048,2]{0,1:T(2,128)S(1)}, u32[]{:S(2)}) copy-start(f32[2048,2]{0,1:T(2,128)S(1)} %fusion.146) | copy-start | bytes 49156
  397.9 421.9 %copy-start.41 = (f32[2048,2,2]{0,1,2:T(2,128)}, f32[2048,2,2]{0,1,2:T(2,128)S(1)}, u32[]{:S(2)}) copy-start(f32[2048,2,2]{0,1,2:T(2,128)S(1)} %get-tuple-element.210) | copy-start | bytes 98308
  787.7 71.1 %all-to-all-start.1 = ((bf16[4,2,480,768]{3,2,1,0:T(8,128)(2,1)}), bf16[4,2,480,768]{3,2,1,0:T(8,128)(2,1)}, u32[]{:S(2)}, u32[]{:S(2)}) async-start(bf16[4,2,480,768]{3,2,1,0:T(8,128)(2,1)} %copy.123), calls=%async_computation.1 | async-start | bytes 11796480 | tf_op jit(solution)/shard_map/all_to_all | solution.py:236
  858.9 96.1 %all-to-all-start.3 = ((bf16[4,2,480,768]{3,2,1,0:T(8,128)(2,1)}), bf16[4,2,480,768]{3,2,1,0:T(8,128)(2,1)}, u32[]{:S(2)}, u32[]{:S(2)}) async-start(bf16[4,2,480,768]{3,2,1,0:T(8,128)(2,1)} %copy.136), calls=%async_computation.3 | async-start | bytes 11796480 | tf_op jit(solution)/shard_map/all_to_all | solution.py:301
  864.0 324.6 %reduce-scatter.29.cloned.1.call-start = ((), (), s32[]{:S(2)}) async-start(), calls=%async_computation.18 | async-start | bytes 589824
  906.9 48.0 %copy-start.25 = (f32[2048,12]{0,1:T(8,128)S(1)}, f32[2048,12]{0,1:T(8,128)}, u32[]{:S(2)}) copy-start(f32[2048,12]{0,1:T(8,128)} %copy-done.24) | copy-start | bytes 294916
  906.9 48.0 %copy-start.46 = (f32[2048]{0:T(1024)S(1)}, f32[2048]{0:T(1024)}, u32[]{:S(2)}) copy-start(f32[2048]{0:T(1024)} %copy-done.45) | copy-start | bytes 24580
  906.9 48.0 %copy-start.52 = (f32[2048]{0:T(1024)S(1)}, f32[2048]{0:T(1024)}, u32[]{:S(2)}) copy-start(f32[2048]{0:T(1024)} %copy-done.51) | copy-start | bytes 24580
  955.0 79.0 %copy-start.35 = (bf16[2048,12]{0,1:T(8,128)(2,1)}, bf16[2048,12]{0,1:T(8,128)(2,1)S(1)}, u32[]{:S(2)}) copy-start(bf16[2048,12]{0,1:T(8,128)(2,1)S(1)} %multiply_convert_fusion.4) | copy-start | bytes 147460
  997.4 36.6 %copy-start.44 = (bf16[768,12]{0,1:T(8,128)(2,1)S(1)}, bf16[768,12]{0,1:T(8,128)(2,1)}, u32[]{:S(2)}) copy-start(bf16[768,12]{0,1:T(8,128)(2,1)} %copy-done.43) | copy-start | bytes 55300
  997.4 36.6 %copy-start.54 = (f32[2048]{0:T(1024)S(1)}, f32[2048]{0:T(1024)}, u32[]{:S(2)}) copy-start(f32[2048]{0:T(1024)} %copy-done.53) | copy-start | bytes 24580
  997.4 36.6 %copy-start.58 = (f32[768]{0:T(1024)S(1)}, f32[768]{0:T(1024)}, u32[]{:S(2)}) copy-start(f32[768]{0:T(1024)} %reshape.541) | copy-start | bytes 9220
  1131.0 59.3 %reduce-scatter.27.cloned.1.call-start = ((), (), s32[]{:S(2)}) async-start(), calls=%async_computation.17 | async-start | bytes 1474560
  1141.9 58.4 %reduce-scatter.35.cloned.1.call-start = ((), (), s32[]{:S(2)}) async-start(), calls=%async_computation.21 | async-start | bytes 294912
  1144.2 57.1 %reduce-scatter.33.cloned.1.call-start = ((), (), s32[]{:S(2)}) async-start(), calls=%async_computation.20 | async-start | bytes 294912
  1147.5 54.8 %reduce-scatter.25.cloned.1.call-start = ((), (), s32[]{:S(2)}) async-start(), calls=%async_computation.16 | async-start | bytes 2359296
  1158.3 50.9 %reduce-scatter.23.cloned.1.call-start = ((), (), s32[]{:S(2)}) async-start(), calls=%async_computation.15 | async-start | bytes 4718592
  1187.1 30.2 %reduce-scatter.31.cloned.1.call-start = ((), (), s32[]{:S(2)}) async-start(), calls=%async_computation.19 | async-start | bytes 294912
  1188.5 49.7 %all-reduce.21.cloned.1.call-start = ((), (), s32[]{:S(2)}) async-start(), calls=%async_computation.23 | async-start | bytes 1179648 | tf_op jit(solution)/shard_map/psum | solution.py:340
  1192.4 169.3 %all-reduce.17.cloned.1.call-start = ((), (), s32[]{:S(2)}) async-start(), calls=%async_computation.14 | async-start | bytes 6291456 | tf_op jit(solution)/shard_map/psum | solution.py:332
  1206.7 155.0 %copy-start.11 = (bf16[2048,768]{1,0:T(8,128)(2,1)S(1)}, bf16[2048,768]{1,0:T(8,128)(2,1)}, u32[]{:S(2)}) copy-start(bf16[2048,768]{1,0:T(8,128)(2,1)} %param.18) | copy-start | bytes 9437188
  1213.1 152.4 %copy-start.62 = (bf16[768]{0:T(1024)(128)(2,1)S(1)}, bf16[768]{0:T(1024)(128)(2,1)}, u32[]{:S(2)}) copy-start(bf16[768]{0:T(1024)(128)(2,1)} %get-tuple-element.158) | copy-start | bytes 4612
  (61 other events, 343.4 us)
Sparse Core Ops, SparseCore 0:
  64.8 123.6 all-reduce.14
  382.8 399.3 all-reduce.18
  1192.5 45.7 all-reduce.20
  1240.6 121.0 all-reduce.16
Sparse Core Ops, SparseCore 1:
  221.2 11.4 all-gather.4
  290.2 9.2 all-gather.6
  1131.1 7.1 reduce-scatter.28
  1142.0 8.2 reduce-scatter.26
  1152.5 8.6 reduce-scatter.34
  1163.6 8.6 reduce-scatter.32
  1175.0 10.1 reduce-scatter.24
  1187.3 11.9 reduce-scatter.22
  1202.0 8.7 reduce-scatter.30
where the time goes:
time: 1410 us; the launch traced here: 1400 us
  waiting for transfers between devices  683 us (48%)
  local copies, waits for them, and re-layouts  287 us (20%)
  other arithmetic  188 us (13%)
  matrix products  169 us (12%)
  blocking collectives  32.6 us (2%)
  starting transfers between devices  22.2 us (2%)
  between operations  17.6 us (1%)
    psum x1, waiting for transfers between devices, on_device(): expert_out = lax.psum(partial_out.astype(jnp.bfloat16), 'tensor')  382 us
    psum x1, waiting for transfers between devices, on_device(): lax.psum(jnp.dot(grad_proj, in_flat.T, preferred_element_type=jnp.float32...  120 us
    psum x1, waiting for transfers between devices, on_device(): lax.psum(jnp.dot(attended, out_weights, preferred_element_type=jnp.float3...  87.5 us
    unnamed x156, local copies, waits for them, and re-layouts  52.2 us
    reduce_sum x1, other arithmetic, on_device(): grad_gates = jnp.sum(branch_out * upstream[:, None, :], axis=-1)  46.1 us
    all_to_all x1, waiting for transfers between devices, on_device(): lax.all_to_all(grad_outgoing, 'expert', split_axis=0, concat_axis=0, tile...  43.8 us
    reduce_sum x1, other arithmetic, on_device(): jnp.sum(grad_picked.reshape(row_count, 2, D).astype(jnp.float32), axis=1)  36.5 us
    all_to_all x1, waiting for transfers between devices, on_device(): lax.all_to_all(expert_out, 'expert', split_axis=0, concat_axis=0, tiled=T...  29.6 us
  transfers between devices with their start and end apart: 17, of which 7 were waited for; matrix products, arithmetic and copies ran while one was open for 25% of the time, Pallas kernels for 0%

commit v1 on v0

v1 whole, which is shorter than its diff:
```python
import functools
import jax
import jax.numpy as jnp
from jax import lax
from jax.experimental import pallas as pl
from jax.experimental.pallas import tpu as pltpu
from jax.sharding import PartitionSpec as P

D = 768
HD = 64
HEADS = 12
EXPERTS = 8
ALL_EXPERTS = 12
SEQ_LEN = 1024
CAPACITY = 480
DOC_BLOCK = 64
EPS = 1e-06
NEG = -1e30

LANES = 128
BLK = 256
WIN = BLK + 16
QBLOCKS = SEQ_LEN // BLK
PAIRS = HEADS // 2
NT = (((1,), (1,)), ((), ()))
TN = (((0,), (0,)), ((), ()))
F32 = jnp.float32
BF16 = jnp.bfloat16
MB = 1 << 20


def nn(a, b):
    return jnp.dot(a, b, preferred_element_type=F32)


def nt(a, b):
    return lax.dot_general(a, b, NT, preferred_element_type=F32)


def tn(a, b):
    return lax.dot_general(a, b, TN, preferred_element_type=F32)


def call(body, name, grid, in_specs, out_specs, out_shape, scratch=(), prefetch=0, flops=0, nbytes=0, vmem=48):
    return pl.pallas_call(
        body,
        name=name,
        out_shape=out_shape,
        grid_spec=pltpu.PrefetchScalarGridSpec(
            num_scalar_prefetch=prefetch,
            grid=grid,
            in_specs=in_specs,
            out_specs=out_specs,
            scratch_shapes=list(scratch),
        ),
        compiler_params=pltpu.CompilerParams(
            dimension_semantics=("arbitrary",) * len(grid), vmem_limit_bytes=vmem * MB
        ),
        cost_estimate=pl.CostEstimate(flops=flops, bytes_accessed=nbytes, transcendentals=0),
    )


def rows_spec(cols, rows=BLK):
    return pl.BlockSpec((rows, cols), lambda i, *_: (i, 0))


def full_spec(*shape):
    return pl.BlockSpec(shape, lambda *_: (0,) * len(shape))


def project_body(x_ref, gain_ref, w_ref, low_ref, out_ref):
    x = x_ref[...].astype(F32)
    factor = lax.rsqrt(jnp.mean(x * x, axis=-1, keepdims=True) + EPS)
    low = (x * factor * gain_ref[...]).astype(BF16)
    low_ref[...] = low
    out_ref[...] = nn(low, w_ref[...]).astype(BF16)


def project(tokens, gain, weights):
    rows = tokens.shape[0]
    cols = weights.shape[1]
    return call(
        project_body,
        "norm_project",
        (rows // BLK,),
        [rows_spec(D), full_spec(1, D), full_spec(D, cols)],
        [rows_spec(D), rows_spec(cols)],
        [jax.ShapeDtypeStruct((rows, D), BF16), jax.ShapeDtypeStruct((rows, cols), BF16)],
        flops=2 * rows * D * cols,
        nbytes=rows * (D + D + cols) * 2 + D * cols * 2,
    )(tokens, gain, weights)


def split_heads(v):
    first = lax.broadcasted_iota(jnp.int32, v.shape, 1) < HD
    zero = jnp.zeros_like(v)
    return (jnp.where(first, v, zero), jnp.where(first, zero, v))


def pair_mask(key_block, query_block, starts, diagonal):
    key_at = lax.broadcasted_iota(jnp.int32, (BLK, BLK), 0)
    mask = key_at >= starts - key_block * BLK
    if diagonal:
        mask = mask & (key_at <= lax.broadcasted_iota(jnp.int32, (BLK, BLK), 1))
    return mask


def attend_body(low_ref, q_ref, k_ref, v_ref, start_ref, o_ref, lse_ref, vt_ref):
    seq = pl.program_id(0)
    for kb in range(QBLOCKS):
        vt_ref[kb] = v_ref[kb * BLK : (kb + 1) * BLK, :].T
    for qb in range(QBLOCKS):
        here = slice(qb * BLK, (qb + 1) * BLK)
        queries = split_heads(q_ref[here, :] * jnp.asarray(HD**-0.5, BF16))
        starts = start_ref[0, :, here]

        def step(kb, carry, diagonal):
            keys = k_ref[pl.ds(pl.multiple_of(kb * BLK, BLK), BLK), :]
            mask = pair_mask(kb, qb, starts, diagonal)
            out = []
            for h in range(2):
                highest, total, acc = carry[3 * h : 3 * h + 3]
                scores = jnp.where(mask, nt(keys, queries[h]), NEG)
                now = jnp.maximum(highest, jnp.max(scores, axis=0, keepdims=True))
                weights = jnp.exp(scores - now)
                fade = jnp.exp(highest - now)
                total = total * fade + jnp.sum(weights, axis=0, keepdims=True)
                acc = acc * fade + nn(vt_ref[kb, h * HD : (h + 1) * HD, :], weights.astype(BF16))
                out += [now, total, acc]
            return tuple(out)

        empty = (jnp.full((1, BLK), NEG, F32), jnp.zeros((1, BLK), F32), jnp.zeros((HD, BLK), F32))
        carry = step(qb, empty + empty, True)
        if qb > 0:
            carry = lax.fori_loop(
                low_ref[seq * QBLOCKS + qb], qb, lambda kb, c: step(kb, c, False), carry
            )
        both = jnp.concatenate([carry[2] / carry[1], carry[5] / carry[4]], axis=0)
        o_ref[here, :] = both.T.astype(BF16)
        lse_ref[0, 0, 0:1, here] = carry[0] + jnp.log(carry[1])
        lse_ref[0, 0, 1:2, here] = carry[3] + jnp.log(carry[4])


def head_spec(offset):
    return pl.BlockSpec((SEQ_LEN, 2 * HD), lambda s, p, *_: (s, p + offset))


def attend(qkv, starts, lowest):
    rows = qkv.shape[0]
    seqs = rows // SEQ_LEN
    return call(
        attend_body,
        "attend",
        (seqs, PAIRS),
        [
            head_spec(0),
            head_spec(PAIRS),
            head_spec(2 * PAIRS),
            pl.BlockSpec((1, 1, SEQ_LEN), lambda s, p, *_: (s, 0, 0)),
        ],
        [head_spec(0), pl.BlockSpec((1, 1, 2, SEQ_LEN), lambda s, p, *_: (s, p, 0, 0))],
        [
            jax.ShapeDtypeStruct((rows, D), BF16),
            jax.ShapeDtypeStruct((seqs, PAIRS, 2, SEQ_LEN), F32),
        ],
        scratch=[pltpu.VMEM((QBLOCKS, 2 * HD, BLK), BF16)],
        prefetch=1,
        flops=4 * rows * SEQ_LEN * D,
        nbytes=rows * D * 8,
    )(lowest, qkv, qkv, qkv, starts)


def attend_back_body(low_ref, q_ref, k_ref, v_ref, start_ref, do_ref, o_ref, lse_ref, g_ref, kt_ref, dk_ref, dv_ref):
    seq = pl.program_id(0)
    pick = (
        lax.broadcasted_iota(jnp.int32, (8, 2 * HD), 1) // HD
        == lax.broadcasted_iota(jnp.int32, (8, 2 * HD), 0)
    ).astype(F32)
    for kb in range(QBLOCKS):
        kt_ref[kb] = k_ref[kb * BLK : (kb + 1) * BLK, :].T
    for qb in range(QBLOCKS):
        here = slice(qb * BLK, (qb + 1) * BLK)
        queries = split_heads(q_ref[here, :] * jnp.asarray(HD**-0.5, BF16))
        upstream = do_ref[here, :]
        ups = split_heads(upstream)
        deltas = lax.dot_general(
            pick,
            upstream.astype(F32) * o_ref[here, :].astype(F32),
            NT,
            precision=lax.Precision.HIGHEST,
            preferred_element_type=F32,
        )
        starts = start_ref[0, :, here]

        def step(kb, carry, diagonal):
            at = pl.ds(pl.multiple_of(kb * BLK, BLK), BLK)
            keys = k_ref[at, :]
            values = v_ref[at, :]
            mask = pair_mask(kb, qb, starts, diagonal)
            out = []
            dk = dv = None
            for h in range(2):
                scores = jnp.where(mask, nt(keys, queries[h]), NEG)
                weights = jnp.exp(scores - lse_ref[0, 0, h : h + 1, here])
                slopes = (weights * (nt(values, ups[h]) - deltas[h : h + 1, :])).astype(BF16)
                dv_h = nn(weights.astype(BF16), ups[h])
                dk_h = nn(slopes, queries[h])
                dv = dv_h if dv is None else dv + dv_h
                dk = dk_h if dk is None else dk + dk_h
                out.append(carry[h] + nn(kt_ref[kb, h * HD : (h + 1) * HD, :], slopes))
            if diagonal:
                dk_ref[at, :] = dk
                dv_ref[at, :] = dv
            else:
                dk_ref[at, :] += dk
                dv_ref[at, :] += dv
            return tuple(out)

        zero = jnp.zeros((HD, BLK), F32)
        carry = step(qb, (zero, zero), True)
        if qb > 0:
            carry = lax.fori_loop(
                low_ref[seq * QBLOCKS + qb], qb, lambda kb, c: step(kb, c, False), carry
            )
        both = jnp.concatenate(carry, axis=0) * (HD**-0.5)
        g_ref[0, here, :] = both.T.astype(BF16)
    g_ref[1] = dk_ref[...].astype(BF16)
    g_ref[2] = dv_ref[...].astype(BF16)


def attend_back(qkv, starts, lowest, grad_out, attended, log_sums):
    rows = qkv.shape[0]
    seqs = rows // SEQ_LEN
    return call(
        attend_back_body,
        "attend_back",
        (seqs, PAIRS),
        [
            head_spec(0),
            head_spec(PAIRS),
            head_spec(2 * PAIRS),
            pl.BlockSpec((1, 1, SEQ_LEN), lambda s, p, *_: (s, 0, 0)),
            head_spec(0),
            head_spec(0),
            pl.BlockSpec((1, 1, 2, SEQ_LEN), lambda s, p, *_: (s, p, 0, 0)),
        ],
        pl.BlockSpec((3, SEQ_LEN, 2 * HD), lambda s, p, *_: (0, s, p)),
        jax.ShapeDtypeStruct((3, rows, D), BF16),
        scratch=[
            pltpu.VMEM((QBLOCKS, 2 * HD, BLK), BF16),
            pltpu.VMEM((SEQ_LEN, 2 * HD), F32),
            pltpu.VMEM((SEQ_LEN, 2 * HD), F32),
        ],
        prefetch=1,
        flops=10 * rows * SEQ_LEN * D,
        nbytes=rows * D * 16,
    )(lowest, qkv, qkv, qkv, starts, grad_out, attended, log_sums)


def lane_of(shape):
    return lax.broadcasted_iota(jnp.int32, shape, 1)


def members_of(routes):
    lane = lane_of((routes.shape[0], LANES))
    return ((lane == routes[:, 0:1]) | (lane == routes[:, 1:2])).astype(F32)


def middle_body(att_ref, w_ref, x_ref, gain_ref, rw_ref, cv_ref, cot_ref, prev_ref, after_ref, low_ref, info_ref):
    after = x_ref[...].astype(F32) + nn(att_ref[...], w_ref[...])
    after_ref[...] = after
    factor = lax.rsqrt(jnp.mean(after * after, axis=-1, keepdims=True) + EPS)
    normed = after * factor * gain_ref[...]
    low = normed.astype(BF16)
    low_ref[...] = low
    products = nt(low, rw_ref[...])
    mine, swapped = products[:, :LANES], products[:, LANES:]
    cot = cot_ref[...]
    dots = nt(cot, cv_ref[...])
    dot_normed = jnp.sum(cot.astype(F32) * normed, axis=-1, keepdims=True)
    lane = lane_of(mine.shape)
    logits = jnp.where(lane < ALL_EXPERTS, mine + prev_ref[...], NEG)
    grown = jnp.exp(logits - jnp.max(logits, axis=-1, keepdims=True))
    chances = grown / jnp.sum(grown, axis=-1, keepdims=True)
    mixing = 1.0 / (1.0 + jnp.exp(swapped - mine))
    info = jnp.where(lane < 12, chances, jnp.where(lane < 16, mixing, dots))
    info_ref[...] = jnp.where(lane == 18, dot_normed, info)


def middle(attended, w_out, tokens, gain, rw, cv, cot, prev):
    rows = tokens.shape[0]
    return call(
        middle_body,
        "out_norm_route",
        (rows // BLK,),
        [
            rows_spec(D),
            full_spec(D, D),
            rows_spec(D),
            full_spec(1, D),
            full_spec(2 * LANES, D),
            full_spec(LANES, D),
            rows_spec(D),
            rows_spec(LANES),
        ],
        [rows_spec(D), rows_spec(D), rows_spec(LANES)],
        [
            jax.ShapeDtypeStruct((rows, D), F32),
            jax.ShapeDtypeStruct((rows, D), BF16),
            jax.ShapeDtypeStruct((rows, LANES), F32),
        ],
        flops=2 * rows * D * (D + 3 * LANES),
        nbytes=rows * D * 12 + rows * LANES * 8,
    )(attended, w_out, tokens, gain, rw, cv, cot, prev)


def dispatch_body(start_ref, rows_ref, rank_ref, out_ref, acc_ref):
    expert = pl.program_id(0)
    acc_ref[...] = jnp.zeros_like(acc_ref)
    blocks = rows_ref.shape[0] // BLK
    for tb in range(blocks):
        here = slice(tb * BLK, (tb + 1) * BLK)
        first = pl.multiple_of(start_ref[expert * blocks + tb] // 16 * 16, 16)
        slot = lax.broadcasted_iota(jnp.int32, (WIN, BLK), 0)
        chosen = jnp.where(rank_ref[0, :, here] - first == slot, 1.0, 0.0).astype(BF16)
        acc_ref[pl.ds(first, WIN), :] += nn(chosen, rows_ref[here, :]).astype(acc_ref.dtype)
    out_ref[0] = acc_ref[:CAPACITY, :]


def dispatch(rows, ranks, starts, dtype, name):
    count, cols = rows.shape
    experts = ranks.shape[0]
    return call(
        dispatch_body,
        name,
        (experts,),
        [full_spec(count, cols), pl.BlockSpec((1, 1, count), lambda e, *_: (e, 0, 0))],
        pl.BlockSpec((1, CAPACITY, cols), lambda e, *_: (e, 0, 0)),
        jax.ShapeDtypeStruct((experts, CAPACITY, cols), dtype),
        scratch=[pltpu.VMEM((CAPACITY + WIN, cols), dtype)],
        prefetch=1,
        flops=2 * experts * count * WIN * cols,
        nbytes=(count + experts * CAPACITY) * cols * 2,
    )(starts, rows, ranks)


def combine_body(start_ref, first_ref, second_ref, rank_ref, info_ref, *rest, blocks):
    if len(rest) == 1:
        (out_ref,) = rest
        dg_ref = None
    else:
        dg_ref, out_ref, pick_ref = rest
    tb = pl.program_id(0)
    ranks = rank_ref[...]
    info = info_ref[...]
    slot = lax.broadcasted_iota(jnp.int32, (BLK, WIN), 1)
    lane = lane_of((BLK, LANES))
    acc = jnp.zeros((BLK, D), F32)
    picked = jnp.zeros((BLK, LANES), F32)
    for expert in range(EXPERTS):
        rows_ref = (first_ref, second_ref)[expert % 2]
        first = jnp.minimum(start_ref[expert * blocks + tb] // 16 * 16, CAPACITY - WIN)
        first = pl.multiple_of(first, 16)
        chosen = jnp.where(ranks[:, expert : expert + 1] - first == slot, 1.0, 0.0).astype(BF16)
        acc += info[:, expert : expert + 1] * nn(chosen, rows_ref[expert // 2, pl.ds(first, WIN), :])
        if dg_ref is not None:
            mine = (lane % 16 == expert) & (lane < 48)
            picked += jnp.where(mine, nn(chosen, dg_ref[pl.ds(first, WIN), :]), 0.0)
    out_ref[...] = acc.astype(BF16)
    if dg_ref is not None:
        pick_ref[...] = picked + pltpu.roll(picked, LANES - 16, 1) + pltpu.roll(picked, LANES - 32, 1)


def combine(first, second, rank_cols, info, starts, dg, name):
    count = rank_cols.shape[0]
    blocks = count // BLK
    owners = first.shape[0]
    extra = [] if dg is None else [dg]
    outs = [jax.ShapeDtypeStruct((count, D), BF16)]
    out_specs = [rows_spec(D)]
    if dg is not None:
        outs.append(jax.ShapeDtypeStruct((count, LANES), F32))
        out_specs.append(rows_spec(LANES))
    return call(
        functools.partial(combine_body, blocks=blocks),
        name,
        (blocks,),
        [
            full_spec(owners, CAPACITY, D),
            full_spec(owners, CAPACITY, D),
            rows_spec(LANES),
            rows_spec(LANES),
        ]
        + [full_spec(CAPACITY, LANES)] * len(extra),
        out_specs,
        outs,
        prefetch=1,
        flops=2 * EXPERTS * count * WIN * D,
        nbytes=(count + EXPERTS * CAPACITY) * D * 2,
    )(starts, first, second, rank_cols, info, *extra)


def expert_body(x_ref, c_ref, gu_ref, dn_ref, act_ref, both_ref, dx_ref, dg_ref):
    hidden = dn_ref.shape[0]
    both = nn(x_ref[0], gu_ref[...])
    gate, up = both[:, :hidden], both[:, hidden:]
    sig = jax.nn.sigmoid(gate)
    act = (gate * sig * up).astype(BF16)
    act_ref[0] = act
    grad_act = nt(c_ref[0], dn_ref[...])
    dg_ref[0] = jnp.sum(act.astype(F32) * grad_act, axis=-1, keepdims=True)
    grad_gate = grad_act * up * sig * (1.0 + gate * (1.0 - sig))
    grad_up = grad_act * (gate * sig)
    grad_both = jnp.concatenate([grad_gate, grad_up], axis=-1).astype(BF16)
    both_ref[0] = grad_both
    dx_ref[0] = nt(grad_both, gu_ref[...]).astype(BF16)


def expert_core(x, cot, gate_up, down):
    sources = x.shape[0]
    hidden = down.shape[0]

    def block(cols):
        return pl.BlockSpec((1, CAPACITY, cols), lambda s: (s, 0, 0))

    return call(
        expert_body,
        "expert",
        (sources,),
        [block(D), block(D), full_spec(D, 2 * hidden), full_spec(hidden, D)],
        [block(hidden), block(2 * hidden), block(D), block(1)],
        [
            jax.ShapeDtypeStruct((sources, CAPACITY, hidden), BF16),
            jax.ShapeDtypeStruct((sources, CAPACITY, 2 * hidden), BF16),
            jax.ShapeDtypeStruct((sources, CAPACITY, D), BF16),
            jax.ShapeDtypeStruct((sources, CAPACITY, 1), F32),
        ],
        flops=2 * sources * CAPACITY * D * hidden * 5,
        nbytes=sources * CAPACITY * (3 * D + 3 * hidden) * 2 + 3 * D * hidden * 2,
    )(x, cot, gate_up, down)


def output_body(after_ref, moe_ref, info_ref, routes_ref, gain_ref, cv_ref, out_ref):
    after = after_ref[...]
    factor = lax.rsqrt(jnp.mean(after * after, axis=-1, keepdims=True) + EPS)
    info = info_ref[...]
    gates = info * members_of(routes_ref[...])
    coef = gates[:, 9:10] + gates[:, 10:11] * info[:, 12:13] + gates[:, 11:12] * info[:, 14:15]
    out = after * (1.0 + coef * factor * gain_ref[...]) + moe_ref[...].astype(F32)
    out = out + (gates[:, 10:11] * info[:, 13:14]) * cv_ref[0:1, :]
    out_ref[...] = out + (gates[:, 11:12] * info[:, 15:16]) * cv_ref[1:2, :]


def finish_output(after, moe, info, routes, gain, cv):
    rows = after.shape[0]
    return call(
        output_body,
        "output",
        (rows // BLK,),
        [rows_spec(D), rows_spec(D), rows_spec(LANES), rows_spec(2), full_spec(1, D), full_spec(2, D)],
        rows_spec(D),
        jax.ShapeDtypeStruct((rows, D), F32),
        nbytes=rows * D * 10,
    )(after, moe, info, routes, gain, cv)


def back_body(after_ref, cot_ref, moe_ref, info_ref, dg_ref, routes_ref, gain_ref, rw_ref, low_ref, w_ref, grad_ref, glow_ref, datt_ref, small_ref):
    after = after_ref[...]
    factor = lax.rsqrt(jnp.mean(after * after, axis=-1, keepdims=True) + EPS)
    xhat = after * factor
    gain = gain_ref[...]
    cot = cot_ref[...].astype(F32)
    info = info_ref[...]
    members = members_of(routes_ref[...])
    gates = info * members
    lane = lane_of(info.shape)
    dot_normed = info[:, 18:19]

    grad = jnp.where(lane < EXPERTS, dg_ref[...], 0.0)
    grad = grad + jnp.where(lane == 9, dot_normed, 0.0)
    grad_mix = jnp.zeros_like(grad)
    coef = gates[:, 9:10]
    spare = []
    for c in range(2):
        first, second = info[:, 12 + 2 * c : 13 + 2 * c], info[:, 13 + 2 * c : 14 + 2 * c]
        dot_const = info[:, 16 + c : 17 + c]
        weight = gates[:, 10 + c : 11 + c]
        inner = first * dot_normed + second * dot_const
        grad = grad + jnp.where(lane == 10 + c, inner, 0.0)
        grad_mix = grad_mix + jnp.where(lane == 12 + 2 * c, first * weight * (dot_normed - inner), 0.0)
        grad_mix = grad_mix + jnp.where(lane == 13 + 2 * c, second * weight * (dot_const - inner), 0.0)
        coef = coef + weight * first
        spare.append(weight * second)
    grad = grad * members
    chances = jnp.where(lane < ALL_EXPERTS, info, 0.0)
    grad_logits = chances * (grad - jnp.sum(chances * grad, axis=-1, keepdims=True))
    slopes = (grad_logits + grad_mix).astype(BF16)

    grad_normed = coef * cot + nn(slopes, rw_ref[...]) + moe_ref[...].astype(F32)
    weighted = grad_normed * gain
    inner = jnp.mean(weighted * xhat, axis=-1, keepdims=True)
    grad_after = cot + factor * (weighted - xhat * inner)
    grad_ref[...] = grad_after
    low = grad_after.astype(BF16)
    glow_ref[...] = low
    datt_ref[...] = nt(low, w_ref[...]).astype(BF16)

    @pl.when(pl.program_id(0) == 0)
    def _():
        small_ref[...] = jnp.zeros_like(small_ref)

    small_ref[0:16, :] += tn(slopes, low_ref[...])[:16, :]
    small_ref[16:17, :] += jnp.sum(grad_normed * xhat, axis=0, keepdims=True)
    small_ref[17:18, :] += jnp.sum(spare[0] * cot, axis=0, keepdims=True)
    small_ref[18:19, :] += jnp.sum(spare[1] * cot, axis=0, keepdims=True)


def back(after, cot, moe, info, dg, routes, gain, rw, low, w_out):
    rows = after.shape[0]
    return call(
        back_body,
        "route_norm_back",
        (rows // BLK,),
        [
            rows_spec(D),
            rows_spec(D),
            rows_spec(D),
            rows_spec(LANES),
            rows_spec(LANES),
            rows_spec(2),
            full_spec(1, D),
            full_spec(LANES, D),
            rows_spec(D),
            full_spec(D, D),
        ],
        [rows_spec(D), rows_spec(D), rows_spec(D), full_spec(24, D)],
        [
            jax.ShapeDtypeStruct((rows, D), F32),
            jax.ShapeDtypeStruct((rows, D), BF16),
            jax.ShapeDtypeStruct((rows, D), BF16),
            jax.ShapeDtypeStruct((24, D), F32),
        ],
        flops=2 * rows * D * (D + 2 * LANES),
        nbytes=rows * D * 18,
    )(after, cot, moe, info, dg, routes, gain, rw, low, w_out)


def final_body(g_ref, w_ref, x_ref, gain_ref, after_ref, out_ref, small_ref):
    grad = nt(g_ref[0], w_ref[:, :D]) + nt(g_ref[1], w_ref[:, D : 2 * D]) + nt(g_ref[2], w_ref[:, 2 * D :])
    x = x_ref[...].astype(F32)
    factor = lax.rsqrt(jnp.mean(x * x, axis=-1, keepdims=True) + EPS)
    xhat = x * factor
    weighted = grad * gain_ref[...]
    inner = jnp.mean(weighted * xhat, axis=-1, keepdims=True)
    out_ref[...] = after_ref[...] + factor * (weighted - xhat * inner)

    @pl.when(pl.program_id(0) == 0)
    def _():
        small_ref[...] = jnp.zeros_like(small_ref)

    small_ref[0:1, :] += jnp.sum(grad * xhat, axis=0, keepdims=True)


def final(grads, weights, tokens, gain, grad_after):
    rows = tokens.shape[0]
    return call(
        final_body,
        "norm_back",
        (rows // BLK,),
        [
            pl.BlockSpec((3, BLK, D), lambda i: (0, i, 0)),
            full_spec(D, 3 * D),
            rows_spec(D),
            full_spec(1, D),
            rows_spec(D),
        ],
        [rows_spec(D), full_spec(8, D)],
        [jax.ShapeDtypeStruct((rows, D), F32), jax.ShapeDtypeStruct((8, D), F32)],
        flops=6 * rows * D * D,
        nbytes=rows * D * 16,
    )(grads, weights, tokens, gain, grad_after)


def gather_dp(x, axis):
    n = lax.axis_size("dp")
    if n != 2:
        return lax.all_gather(x, "dp", axis=axis, tiled=True)
    other = lax.ppermute(x, "dp", [(0, 1), (1, 0)])
    here = lax.axis_index("dp") == 0
    return jnp.concatenate([jnp.where(here, x, other), jnp.where(here, other, x)], axis=axis)


def scatter_dp(x, axis):
    n = lax.axis_size("dp")
    if n != 2:
        return lax.psum_scatter(x.astype(BF16), "dp", scatter_dimension=axis, tiled=True).astype(F32)
    half = x.shape[axis] // 2
    me = lax.axis_index("dp")
    keep = lax.dynamic_slice_in_dim(x, me * half, half, axis)
    send = lax.dynamic_slice_in_dim(x, (1 - me) * half, half, axis).astype(BF16)
    return keep.astype(F32) + lax.ppermute(send, "dp", [(0, 1), (1, 0)]).astype(F32)


def sum_over(x, axis_name):
    n = lax.axis_size(axis_name)
    if n & (n - 1):
        return lax.psum(x.astype(BF16), axis_name).astype(F32)
    step = 1
    while step < n:
        low = x.astype(BF16)
        other = lax.ppermute(low, axis_name, [(i, i ^ step) for i in range(n)])
        x = low.astype(F32) + other.astype(F32)
        step *= 2
    return x


def gather_groups(x):
    n = lax.axis_size("tensor")
    me = lax.axis_index("tensor")
    parts = [x] + [
        lax.ppermute(x, "tensor", [(i, (i + k) % n) for i in range(n)]) for k in range(1, n)
    ]
    stacked = jnp.stack(parts)
    return jnp.take(stacked, (me - jnp.arange(n)) % n, axis=0)


def sum_tensor(x, pieces):
    n = lax.axis_size("tensor")
    if n != 4:
        return lax.psum(x, "tensor")
    me = lax.axis_index("tensor")
    outer = (me == 0) | (me == n - 1)
    size = x.shape[0] // pieces
    done = []
    for c in range(pieces):
        part = x[c * size : (c + 1) * size]
        other = lax.ppermute(part, "tensor", [(0, 1), (3, 2)])
        part = (part.astype(F32) + other.astype(F32)).astype(BF16)
        other = lax.ppermute(part, "tensor", [(1, 2), (2, 1)])
        part = (part.astype(F32) + other.astype(F32)).astype(BF16)
        other = lax.ppermute(part, "tensor", [(1, 0), (2, 3)])
        done.append(jnp.where(outer, other, part))
    return jnp.concatenate(done, axis=0)


def exchange(x):
    return lax.all_to_all(x, "expert", split_axis=0, concat_axis=0, tiled=True)


def route_tables(routes):
    count = routes.shape[0]
    blocks = count // BLK
    ids = jnp.arange(EXPERTS, dtype=jnp.int32)[:, None]
    member = (routes[:, 0][None, :] == ids) | (routes[:, 1][None, :] == ids)
    ones = member.astype(BF16).reshape(EXPERTS, blocks, BLK)
    earlier = (jnp.arange(BLK)[:, None] < jnp.arange(BLK)[None, :]).astype(BF16)
    inside = jnp.einsum("ebt,tu->ebu", ones, earlier, preferred_element_type=F32)
    counts = jnp.sum(ones.astype(F32), axis=-1)
    starts = jnp.cumsum(counts, axis=1) - counts
    ranks = (inside + starts[:, :, None]).astype(jnp.int32).reshape(EXPERTS, count)
    ranks = jnp.where(member, ranks, -(1 << 20))
    return (ranks, starts.astype(jnp.int32))


def document_tables(segments):
    seqs = segments.shape[0] // SEQ_LEN
    marks = segments.reshape(seqs, SEQ_LEN // DOC_BLOCK, DOC_BLOCK)[:, :, 0]
    begin = DOC_BLOCK * jnp.sum((marks[:, None, :] < marks[:, :, None]).astype(jnp.int32), axis=-1)
    starts = jnp.broadcast_to(begin[:, :, None], begin.shape + (DOC_BLOCK,)).reshape(seqs, 1, SEQ_LEN)
    lowest = begin[:, :: BLK // DOC_BLOCK] // BLK
    return (starts, lowest.reshape(-1))


def three_parts(x):
    high = x.astype(BF16)
    rest = x - high.astype(F32)
    mid = rest.astype(BF16)
    return (high, mid, (rest - mid.astype(F32)).astype(BF16))


def on_device(
    tokens,
    prev_logits,
    routes,
    segments,
    gain_one,
    w_qkv,
    w_out,
    gain_two,
    router,
    const_proj,
    const_vec,
    w_gate_up,
    w_down,
    cotangent,
):
    rows = tokens.shape[0]
    owners = lax.axis_size("expert")
    groups = lax.axis_size("tensor")
    group = lax.axis_index("tensor")
    local_experts = EXPERTS // owners
    width = w_out.shape[0]
    slice_rows = w_qkv.shape[0]

    in_mine = gather_groups(w_qkv.astype(BF16).reshape(slice_rows, 3 * width))
    in_mine = in_mine.reshape(groups, slice_rows, 3, width).transpose(1, 2, 0, 3)
    in_all = gather_dp(in_mine.reshape(slice_rows, 3 * D), 0)
    out_mine = gather_groups(w_out.astype(BF16)).reshape(D, slice_rows)
    out_all = gather_dp(out_mine, 1)
    small = jnp.concatenate(
        [router.T, const_proj.T, gain_one[None], gain_two[None], const_vec], axis=0
    ).astype(BF16)
    small = gather_dp(small, 1)
    gain_a = small[16:17].astype(F32)
    gain_b = small[17:18].astype(F32)
    const_rows = small[18:20].astype(F32)
    mains = jnp.pad(small[:16], ((0, LANES - 16), (0, 0)))
    swaps = jnp.stack([small[13], small[12], small[15], small[14]])
    routing = jnp.concatenate([mains, jnp.pad(swaps, ((12, LANES - 16), (0, 0)))], axis=0)
    const_low = jnp.pad(small[18:20], ((16, LANES - 18), (0, 0)))

    ranks, block_starts = route_tables(routes)
    rank_cols = jnp.pad(ranks.T, ((0, 0), (0, LANES - EXPERTS)))
    per_expert = ranks.reshape(owners, local_experts, 1, rows)
    per_start = block_starts.reshape(owners, local_experts, -1)
    table = [
        (per_expert[:, j], per_start[:, j].reshape(-1)) for j in range(local_experts)
    ]
    cot_in = [
        exchange(dispatch(cotangent, r, s, BF16, "send_cot")) for r, s in table
    ]
    all_starts = block_starts.reshape(-1)

    hidden = w_down.shape[1]
    gate_up = gather_dp(w_gate_up.astype(BF16).reshape(local_experts, slice_rows, 2 * hidden), 1)
    down = gather_dp(w_down.astype(BF16), 2)

    starts, lowest = document_tables(segments)
    normed_low, qkv = project(tokens, gain_a, in_all)
    attended, log_sums = attend(qkv, starts, lowest)
    prev = jnp.pad(prev_logits, ((0, 0), (0, LANES - ALL_EXPERTS)))
    after_attn, routed_low, info = middle(
        attended, out_all, tokens, gain_b, routing, const_low, cotangent, prev
    )

    rows_in = [exchange(dispatch(routed_low, r, s, BF16, "send_rows")) for r, s in table]
    acts, boths, back_rows, back_dots = [], [], [], []
    for j in range(local_experts):
        act, both, grad_rows, dots = expert_core(rows_in[j], cot_in[j], gate_up[j], down[j])
        acts.append(act)
        boths.append(both)
        back_rows.append(exchange(grad_rows))
        back_dots.append(dots.reshape(owners, CAPACITY))
    dots = exchange(jnp.stack(back_dots, axis=1)).reshape(EXPERTS, CAPACITY)
    dots = jnp.concatenate(
        [jnp.pad(p, ((0, 8), (0, 0))) for p in three_parts(dots)], axis=0
    )
    dots = jnp.pad(dots.T, ((0, 0), (0, LANES - 48)))
    grad_part, dots_part = combine(
        back_rows[0], back_rows[1], rank_cols, info, all_starts, dots, "combine_grads"
    )
    grad_moe = sum_tensor(grad_part, 4)
    dot_sums = lax.psum(dots_part[:, :EXPERTS].T, "tensor").T
    dot_sums = jnp.pad(dot_sums, ((0, 0), (0, LANES - EXPERTS)))

    outs_back = [
        exchange(
            jnp.einsum("scf,fd->scd", acts[j], down[j], preferred_element_type=F32).astype(BF16)
        )
        for j in range(local_experts)
    ]
    (out_part,) = combine(
        outs_back[0], outs_back[1], rank_cols, info, all_starts, None, "combine_out"
    )
    output = finish_output(
        after_attn, sum_tensor(out_part, 4), info, routes, gain_b, const_rows
    )

    grad_after, grad_low, grad_att, small_grads = back(
        after_attn, cotangent, grad_moe, info, dot_sums, routes, gain_b, mains, routed_low, out_all
    )
    grad_qkv = attend_back(qkv, starts, lowest, grad_att, attended, log_sums)
    grad_tokens, gain_grads = final(grad_qkv, in_all, tokens, gain_a, grad_after)

    chance_parts = jnp.concatenate(
        [jnp.pad(p, ((0, 0), (0, 8))) for p in three_parts(info[:, :EXPERTS])], axis=1
    )
    chance_parts = jnp.pad(chance_parts, ((0, 0), (0, LANES - 48)))
    grad_gate_up, grad_down = [], []
    for j in range(local_experts):
        sent = dispatch(chance_parts, *table[j], F32, "send_gates")
        ids = local_experts * jnp.arange(owners)[:, None] + j
        mine = (jnp.arange(LANES)[None, :] % 16 == ids) & (jnp.arange(LANES)[None, :] < 48)
        gates = exchange(jnp.sum(jnp.where(mine[:, None, :], sent, 0.0), axis=-1))
        gated = (gates[:, :, None] * boths[j].astype(F32)).astype(BF16)
        gated_cot = (gates[:, :, None] * cot_in[j].astype(F32)).astype(BF16)
        grad_gate_up.append(
            jnp.einsum("scd,scf->df", rows_in[j], gated, preferred_element_type=F32)
        )
        grad_down.append(
            jnp.einsum("scf,scd->fd", acts[j], gated_cot, preferred_element_type=F32)
        )
    grad_gate_up = scatter_dp(jnp.stack(grad_gate_up), 1).reshape(w_gate_up.shape)
    grad_down = scatter_dp(jnp.stack(grad_down), 2)

    own = lax.dynamic_slice_in_dim(grad_qkv, group * width, width, 2)
    grad_in_w = jnp.einsum("td,ctm->dcm", normed_low, own, preferred_element_type=F32)
    grad_in_w = sum_over(scatter_dp(grad_in_w.reshape(D, 3 * width), 0), "expert")
    own_att = lax.dynamic_slice_in_dim(attended, group * width, width, 1)
    grad_out_w = jnp.einsum("tm,td->md", own_att, grad_low, preferred_element_type=F32)
    grad_out_w = sum_over(scatter_dp(grad_out_w, 1), "expert")
    small_grads = sum_over(scatter_dp(small_grads, 1), "expert")
    gain_grads = sum_over(scatter_dp(gain_grads, 1), "expert")
    return (
        output,
        grad_tokens,
        gain_grads[0],
        grad_in_w.reshape(w_qkv.shape),
        grad_out_w,
        small_grads[16],
        small_grads[:12].T,
        small_grads[12:16].T,
        small_grads[17:19],
        grad_gate_up,
        grad_down,
    )


def solution(mesh):
    token_spec = P(("dp", "expert"), None)
    weight_specs = (
        P("dp"),
        P("dp", None, "tensor"),
        P("tensor", "dp"),
        P("dp"),
        P("dp", None),
        P("dp", None),
        P(None, "dp"),
        P("expert", "dp", None, "tensor"),
        P("expert", "tensor", "dp"),
    )
    return jax.shard_map(
        on_device,
        mesh=mesh,
        in_specs=(token_spec, token_spec, token_spec, P(("dp", "expert"))) + weight_specs + (token_spec,),
        out_specs=(token_spec, token_spec) + weight_specs,
        check_vma=False,
    )
```

time: 1410 us -> 968 us (0.69)
  waiting for transfers between devices: 683 us -> 324 us
  Pallas kernels: 0 us -> 293 us
  local copies, waits for them, and re-layouts: 287 us -> 82.1 us
  matrix products: 169 us -> 40.1 us
  other arithmetic: 188 us -> 76.8 us
  starting transfers between devices: 22.2 us -> 117 us
  blocking collectives: 32.6 us -> 7.73 us
    psum x4 -> x1, waiting for transfers between devices: 609 us -> 70.2 us  [on_device(): dot_sums = lax.psum(dots_part[:, :EXPERTS].T, 'tensor').T]
    pallas_call x0 -> x17, Pallas kernels: none -> 293 us  [the longest x1 61.4 us: attend_back(): call(attend_back_body, 'attend_back', (seqs, PAIRS), [head_spec(0), head_...]
    ppermute x0 -> x49, waiting for transfers between devices: none -> 169 us  [the longest x8 119 us: sum_tensor(): other = lax.ppermute(part, 'tensor', [(1, 0), (2, 3)])]
    dot_general x48 -> x8, matrix products: 169 us -> 35.3 us  [the longest x2 13.9 us: on_device(): jnp.einsum('scd,scf->df', rows_in[j], gated, preferred_element_type=F32)]
    reduce_sum x18 -> x4, other arithmetic: 104 us -> 0.99 us  [the longest x2 0.71 us: on_device(): gates = exchange(jnp.sum(jnp.where(mine[:, None, :], sent, 0.0), axis=-1))]
    gather x4 -> x2, local copies, waits for them, and re-layouts: 75.9 us -> 2.68 us  [gather_groups(): return jnp.take(stacked, (me - jnp.arange(n)) % n, axis=0)]
    ppermute x0 -> x49, starting transfers between devices: none -> 67.8 us  [the longest x8 27.4 us: sum_tensor(): other = lax.ppermute(part, 'tensor', [(0, 1), (3, 2)])]
    mul x12 -> x0, local copies, waits for them, and re-layouts: 36.8 us -> none  [the longest x2 24.6 us: on_device(): grad_gates = jnp.sum(branch_out * upstream[:, None, :], axis=-1)]
  transfers between devices with their start and end apart: 17 -> 60, of which waited for: 7 -> 23; matrix products, arithmetic and copies ran while one was open for 25% -> 18% of each run, Pallas kernels for 0% -> 31%
where the time goes in v1:
time: 968 us; the launch traced here: 956 us
  waiting for transfers between devices  324 us (33%)
  Pallas kernels  293 us (30%)
  starting transfers between devices  117 us (12%)
  local copies, waits for them, and re-layouts  82.1 us (8%)
  other arithmetic  76.8 us (8%)
  matrix products  40.1 us (4%)
  between operations  15.7 us (2%)
    ppermute x8, waiting for transfers between devices, sum_tensor(): other = lax.ppermute(part, 'tensor', [(1, 0), (2, 3)])  119 us
    all_to_all x10, waiting for transfers between devices, exchange(): return lax.all_to_all(x, 'expert', split_axis=0, concat_axis=0, tiled=True)  84.9 us
    psum x1, waiting for transfers between devices, on_device(): dot_sums = lax.psum(dots_part[:, :EXPERTS].T, 'tensor').T  70.2 us
    pallas_call x1, Pallas kernels, attend_back(): call(attend_back_body, 'attend_back', (seqs, PAIRS), [head_spec(0), head_...  61.4 us
    pallas_call x1, Pallas kernels, attend(): call(attend_body, 'attend', (seqs, PAIRS), [head_spec(0), head_spec(PAIRS...  52 us
    all_to_all x10, starting transfers between devices, exchange(): return lax.all_to_all(x, 'expert', split_axis=0, concat_axis=0, tiled=True)  48.5 us
    pallas_call x2, Pallas kernels, combine(): call(functools.partial(combine_body, blocks=blocks), name, (blocks,), [fu...  44.2 us
    pallas_call x1, Pallas kernels, back(): call(back_body, 'route_norm_back', (rows // BLK,), [rows_spec(D), rows_sp...  31.7 us
  transfers between devices with their start and end apart: 60, of which 23 were waited for; matrix products, arithmetic and copies ran while one was open for 18% of the time, Pallas kernels for 31%

profile of v1, /device:TPU:0, one launch (start us, length us, event | category | flops | bytes accessed | tf_op | source)
XLA Modules:
  0.0 955.7 jit_solution(16449853822712115801)
XLA Ops:
  23.4 6.4 send_cot.3
  89.0 12.9 %norm_project.1 = (bf16[2048,768]{1,0:T(8,128)(2,1)S(1)}, bf16[2048,2304]{1,0:T(8,128)(2,1)}) custom-call(bf16[2048,768]{1,0:T(8,128)(2,1)} %x_ref.5, f32[1,768]{1,0:T(1,128)S(1)} %get-tuple-element.102.gain_ref, bf16[768,2304]{1,0:T(8,128)(2,1)} %pad_maximum_fusion.w_ref), custom_call_target="tpu_custom_call" | custom-call | flops 7247757312 | bytes 19267584 | tf_op jit(solution)/shard_map/norm_project/pallas_call | solution.py:82
  103.6 52.0 %attend.1 = (bf16[2048,768]{1,0:T(8,128)(2,1)S(1)}, f32[2,6,2,1024]{3,2,1,0:T(2,128)S(1)}) custom-call(s32[8]{0:T(128)S(1)} %copy-done.25, bf16[2048,2304]{1,0:T(8,128)(2,1)} %get-tuple-element.34.q_ref.k_ref.v_ref, bf16[2048,2304]{1,0:T(8,128)(2,1)} %get-tuple-element.34.q_ref.k_ref.v_ref, bf16[2048,2304]{1,0:T(8,128)(2,1)} %get-tuple-element.34.q_ref.k_ref.v_ref, ...), custom_call_target="tpu_custom_call" | custom-call | flops 6442450944 | bytes 12582912 | tf_op jit(solution)/shard_map/attend/pallas_call | solution.py:151
  157.3 11.0 %out_norm_route.1 = (f32[2048,768]{1,0:T(8,128)}, bf16[2048,768]{1,0:T(8,128)(2,1)}, f32[2048,128]{1,0:T(8,128)S(1)}) custom-call(bf16[2048,768]{1,0:T(8,128)(2,1)} %copy-done.32, bf16[768,768]{1,0:T(8,128)(2,1)S(1)} %pad_maximum_fusion.5.w_ref, bf16[2048,768]{1,0:T(8,128)(2,1)} %x_ref.5, f32[1,768]{1,0:T(1,128)S(1)} %get-tuple-element.101.gain_ref, ...), custom_call_target="tpu_custom_call" | custom-call | flops 3623878656 | bytes 20971520 | tf_op jit(solution)/shard_map/out_norm_route/pallas_call | solution.py:292
  177.3 7.5 all-to-all-start.3
  207.5 9.4 all-to-all-done.3.x_ref
  233.7 12.6 %expert.3 = (bf16[4,480,512]{2,1,0:T(8,128)(2,1)S(1)}, bf16[4,480,1024]{2,1,0:T(8,128)(2,1)}, bf16[4,480,768]{2,1,0:T(8,128)(2,1)}, f32[4,480,1]{2,1,0:T(8,128)S(1)}) custom-call(bf16[4,480,768]{2,1,0:T(8,128)(2,1)} %all-to-all-done.3.x_ref, bf16[4,480,768]{2,1,0:T(8,128)(2,1)} %all-to-all-done.4.c_ref, bf16[768,1024]{1,0:T(8,128)(2,1)S(1)} %get-tuple-element.86.gu_ref, ...), custom_call_target="tpu_custom_call" | custom-call | flops 7549747200 | bytes 17104896 | tf_op jit(solution)/shard_map/expert/pallas_call | solution.py:426
  247.6 6.1 all-to-all-done.x_ref
  259.5 12.6 %expert.2 = (bf16[4,480,512]{2,1,0:T(8,128)(2,1)S(1)}, bf16[4,480,1024]{2,1,0:T(8,128)(2,1)}, bf16[4,480,768]{2,1,0:T(8,128)(2,1)}, f32[4,480,1]{2,1,0:T(8,128)S(1)}) custom-call(bf16[4,480,768]{2,1,0:T(8,128)(2,1)} %all-to-all-done.x_ref, bf16[4,480,768]{2,1,0:T(8,128)(2,1)} %all-to-all-done.1.c_ref, bf16[768,1024]{1,0:T(8,128)(2,1)S(1)} %copy-done.10, ...), custom_call_target="tpu_custom_call" | custom-call | flops 7549747200 | bytes 17104896 | tf_op jit(solution)/shard_map/expert/pallas_call | solution.py:426
  285.1 7.7 all_to_all.63
  302.6 25.7 %all-to-all-done.7.second_ref = bf16[4,480,768]{2,1,0:T(8,128)(2,1)} async-done(((bf16[4,480,768]{2,1,0:T(8,128)(2,1)}), bf16[4,480,768]{2,1,0:T(8,128)(2,1)}, u32[]{:S(2)}, u32[]{:S(2)}) %all-to-all-start.7) | async-done | bytes 2949152 | tf_op jit(solution)/shard_map/all_to_all | solution.py:647
  338.3 28.1 %all-to-all-done.5.second_ref = bf16[4,480,768]{2,1,0:T(8,128)(2,1)} async-done(((bf16[4,480,768]{2,1,0:T(8,128)(2,1)}), bf16[4,480,768]{2,1,0:T(8,128)(2,1)}, u32[]{:S(2)}, u32[]{:S(2)}) %all-to-all-start.5) | async-done | bytes 2949152 | tf_op jit(solution)/shard_map/all_to_all | solution.py:647
  386.9 7.1 fusion.12
  394.0 10.8 %all-to-all-done.2.first_ref = bf16[4,480,768]{2,1,0:T(8,128)(2,1)} async-done(((bf16[4,480,768]{2,1,0:T(8,128)(2,1)}), bf16[4,480,768]{2,1,0:T(8,128)(2,1)}, u32[]{:S(2)}, u32[]{:S(2)}) %all-to-all-start.2) | async-done | bytes 2949152 | tf_op jit(solution)/shard_map/all_to_all | solution.py:647
  409.7 6.8 fusion.13
  421.1 20.2 %combine_out.1 = bf16[2048,768]{1,0:T(8,128)(2,1)} custom-call(s32[64]{0:T(128)S(1)} %convert_element_type.389.start_ref, bf16[4,480,768]{2,1,0:T(8,128)(2,1)} %all-to-all-done.2.first_ref, bf16[4,480,768]{2,1,0:T(8,128)(2,1)} %all-to-all-done.5.second_ref, s32[2048,128]{1,0:T(8,128)S(1)} %pad.56.rank_ref, f32[2048,128]{1,0:T(8,128)S(1)} %get-tuple-element.40.info_ref), custom_call_target="tpu_custom_call" | custom-call | flops 6845104128 | bytes 9043968 | tf_op jit(solution)/shard_map/combine_out/pallas_call | solution.py:384
  457.9 24.0 %combine_grads.1 = (bf16[2048,768]{1,0:T(8,128)(2,1)}, f32[2048,128]{1,0:T(8,128)S(1)}) custom-call(s32[64]{0:T(128)S(1)} %convert_element_type.389.start_ref, bf16[4,480,768]{2,1,0:T(8,128)(2,1)} %all-to-all-done.6.first_ref, bf16[4,480,768]{2,1,0:T(8,128)(2,1)} %all-to-all-done.7.second_ref, s32[2048,128]{1,0:T(8,128)S(1)} %pad.56.rank_ref, ...), custom_call_target="tpu_custom_call" | custom-call | flops 6845104128 | bytes 9043968 | tf_op jit(solution)/shard_map/combine_grads/pallas_call | solution.py:384
  490.7 10.7 %collective-permute-done.17 = bf16[512,768]{1,0:T(8,128)(2,1)} collective-permute-done((bf16[512,768]{1,0:T(8,128)(2,1)}, bf16[512,768]{1,0:T(8,128)(2,1)}, u32[]{:S(2)}, u32[]{:S(2)}) %collective-permute-start.17) | collective-permute-done | bytes 786464 | tf_op jit(solution)/shard_map/ppermute | solution.py:637
  506.6 11.6 %collective-permute-done.14 = bf16[512,768]{1,0:T(8,128)(2,1)} collective-permute-done((bf16[512,768]{1,0:T(8,128)(2,1)}, bf16[512,768]{1,0:T(8,128)(2,1)}, u32[]{:S(2)}, u32[]{:S(2)}) %collective-permute-start.14) | collective-permute-done | bytes 786464 | tf_op jit(solution)/shard_map/ppermute | solution.py:637
  546.9 70.2 %all-reduce.16.cloned.1.call-done = f32[2048,8]{1,0:T(8,128)} async-done(((f32[2048,8]{1,0:T(8,128)}), f32[2048,8]{1,0:T(8,128)}) %all-reduce.16.cloned.1.call-update) | async-done | bytes 65552 | tf_op jit(solution)/shard_map/psum | solution.py:763
  641.1 71.9 %collective-permute-done.25 = bf16[512,768]{1,0:T(8,128)(2,1)S(1)} collective-permute-done((bf16[512,768]{1,0:T(8,128)(2,1)S(1)}, bf16[512,768]{1,0:T(8,128)(2,1)S(1)}, u32[]{:S(2)}, u32[]{:S(2)}) %collective-permute-start.25) | collective-permute-done | bytes 786464 | tf_op jit(solution)/shard_map/ppermute | solution.py:641
  714.4 15.5 %collective-permute-done.28 = bf16[512,768]{1,0:T(8,128)(2,1)S(1)} collective-permute-done((bf16[512,768]{1,0:T(8,128)(2,1)S(1)}, bf16[512,768]{1,0:T(8,128)(2,1)S(1)}, u32[]{:S(2)}, u32[]{:S(2)}) %collective-permute-start.28) | collective-permute-done | bytes 786464 | tf_op jit(solution)/shard_map/ppermute | solution.py:641
  731.2 16.4 %collective-permute-done.31 = bf16[512,768]{1,0:T(8,128)(2,1)S(1)} collective-permute-done((bf16[512,768]{1,0:T(8,128)(2,1)S(1)}, bf16[512,768]{1,0:T(8,128)(2,1)S(1)}, u32[]{:S(2)}, u32[]{:S(2)}) %collective-permute-start.31) | collective-permute-done | bytes 786464 | tf_op jit(solution)/shard_map/ppermute | solution.py:641
  749.0 15.5 %collective-permute-done.34 = bf16[512,768]{1,0:T(8,128)(2,1)S(1)} collective-permute-done((bf16[512,768]{1,0:T(8,128)(2,1)S(1)}, bf16[512,768]{1,0:T(8,128)(2,1)S(1)}, u32[]{:S(2)}, u32[]{:S(2)}) %collective-permute-start.34) | collective-permute-done | bytes 786464 | tf_op jit(solution)/shard_map/ppermute | solution.py:641
  766.4 31.7 %route_norm_back.1 = (f32[2048,768]{1,0:T(8,128)}, bf16[2048,768]{1,0:T(8,128)(2,1)}, bf16[2048,768]{1,0:T(8,128)(2,1)}, f32[24,768]{1,0:T(8,128)S(1)}) custom-call(f32[2048,768]{1,0:T(8,128)} %get-tuple-element.36.after_ref, bf16[2048,768]{1,0:T(8,128)(2,1)} %cot_ref.3, bf16[2048,768]{1,0:T(8,128)(2,1)} %pad_maximum_fusion.2.moe_ref, ...), custom_call_target="tpu_custom_call" | custom-call | flops 3221225472 | bytes 28311552 | tf_op jit(solution)/shard_map/route_norm_back/pallas_call | solution.py:520
  800.0 61.4 %attend_back.1.g_ref = bf16[3,2048,768]{2,1,0:T(8,128)(2,1)} custom-call(s32[8]{0:T(128)S(1)} %copy-done.26, bf16[2048,2304]{1,0:T(8,128)(2,1)} %get-tuple-element.34.q_ref.k_ref.v_ref, bf16[2048,2304]{1,0:T(8,128)(2,1)} %get-tuple-element.34.q_ref.k_ref.v_ref, bf16[2048,2304]{1,0:T(8,128)(2,1)} %get-tuple-element.34.q_ref.k_ref.v_ref, ...), custom_call_target="tpu_custom_call" | custom-call | flops 16106127360 | bytes 25165824 | tf_op jit(solution)/shard_map/attend_back/pallas_call | solution.py:234
  861.4 15.8 %norm_back.1 = (f32[2048,768]{1,0:T(8,128)}, f32[8,768]{1,0:T(8,128)S(1)}) custom-call(bf16[3,2048,768]{2,1,0:T(8,128)(2,1)} %attend_back.1.g_ref, bf16[768,2304]{1,0:T(8,128)(2,1)} %pad_maximum_fusion.w_ref, bf16[2048,768]{1,0:T(8,128)(2,1)S(1)} %copy-done.31, f32[1,768]{1,0:T(1,128)S(1)} %copy-done.24, f32[2048,768]{1,0:T(8,128)} %get-tuple-element.49.after_ref), custom_call_target="tpu_custom_call" | custom-call | flops 7247757312 | bytes 25165824 | tf_op jit(solution)/shard_map/norm_back/pallas_call | solution.py:566
  877.2 5.7 constant_dynamic-slice_fusion
  901.9 10.3 %output.1 = f32[2048,768]{1,0:T(8,128)} custom-call(f32[2048,768]{1,0:T(8,128)} %get-tuple-element.36.after_ref, bf16[2048,768]{1,0:T(8,128)(2,1)S(1)} %pad_maximum_fusion.1.moe_ref, f32[2048,128]{1,0:T(8,128)S(1)} %get-tuple-element.40.info_ref, s32[2048,2]{1,0:T(8,128)S(1)} %copy.87.routes_ref, f32[1,768]{1,0:T(1,128)S(1)} %copy-done.21, ...), custom_call_target="tpu_custom_call" | custom-call | bytes 15728640 | tf_op jit(solution)/shard_map/output/pallas_call | solution.py:456
  912.2 5.6 collective-permute-start.36
  932.5 6.1 collective-permute-done.39
  941.3 6.4 collective-permute-done.40
  (406 shorter events, 324.3 us)
Async XLA Ops:
  8.8 63.3 %collective-permute-start.6 = (bf16[192,384]{1,0:T(8,128)(2,1)}, bf16[192,384]{1,0:T(8,128)(2,1)S(1)}, u32[]{:S(2)}, u32[]{:S(2)}) collective-permute-start(bf16[192,384]{1,0:T(8,128)(2,1)} %convert_element_type.384), channel_id=1, source_target_pairs={{0,2},{1,3},{2,0},{3,1},{4,6},{5,7},{6,4},{7,5},{8,10},{9,11},{10,... | collective-permute-start | bytes 442376 | tf_op jit(solution)/shard_map/ppermute | solution.py:621
  12.9 59.2 %collective-permute-start.5 = (bf16[192,384]{1,0:T(8,128)(2,1)}, bf16[192,384]{1,0:T(8,128)(2,1)S(1)}, u32[]{:S(2)}, u32[]{:S(2)}) collective-permute-start(bf16[192,384]{1,0:T(8,128)(2,1)} %convert_element_type.384), channel_id=1, source_target_pairs={{0,1},{1,2},{2,3},{3,0},{4,5},{5,6},{6,7},{7,4},{8,9},{9,10},{10,1... | collective-permute-start | bytes 442376 | tf_op jit(solution)/shard_map/ppermute | solution.py:621
  16.4 40.5 %collective-permute-start.3 = (bf16[384,576]{0,1:T(8,128)(2,1)}, bf16[384,576]{0,1:T(8,128)(2,1)}, u32[]{:S(2)}, u32[]{:S(2)}) collective-permute-start(bf16[384,576]{0,1:T(8,128)(2,1)} %bitcast.3), channel_id=1, source_target_pairs={{0,3},{1,0},{2,1},{3,2},{4,7},{5,4},{6,5},{7,6},{8,11},{9,8},{10,9... | collective-permute-start | bytes 1327112 | tf_op jit(solution)/shard_map/ppermute | solution.py:621
  18.7 43.3 %collective-permute-start.2 = (bf16[384,576]{0,1:T(8,128)(2,1)}, bf16[384,576]{0,1:T(8,128)(2,1)}, u32[]{:S(2)}, u32[]{:S(2)}) collective-permute-start(bf16[384,576]{0,1:T(8,128)(2,1)} %bitcast.3), channel_id=1, source_target_pairs={{0,2},{1,3},{2,0},{3,1},{4,6},{5,7},{6,4},{7,5},{8,10},{9,11},{10,... | collective-permute-start | bytes 1327112 | tf_op jit(solution)/shard_map/ppermute | solution.py:621
  18.7 43.3 %collective-permute-start.1 = (bf16[384,576]{0,1:T(8,128)(2,1)}, bf16[384,576]{0,1:T(8,128)(2,1)}, u32[]{:S(2)}, u32[]{:S(2)}) collective-permute-start(bf16[384,576]{0,1:T(8,128)(2,1)} %bitcast.3), channel_id=1, source_target_pairs={{0,1},{1,2},{2,3},{3,0},{4,5},{5,6},{6,7},{7,4},{8,9},{9,10},{10,1... | collective-permute-start | bytes 1327112 | tf_op jit(solution)/shard_map/ppermute | solution.py:621
  29.8 50.7 %all-to-all-start.4 = ((bf16[4,480,768]{2,1,0:T(8,128)(2,1)}), bf16[4,480,768]{2,1,0:T(8,128)(2,1)}, u32[]{:S(2)}, u32[]{:S(2)}) async-start(bf16[4,480,768]{2,1,0:T(8,128)(2,1)} %send_cot.3), calls=%async_computation.4 | async-start | bytes 5898240 | tf_op jit(solution)/shard_map/all_to_all | solution.py:647
  80.5 96.8 %all-to-all-start.1 = ((bf16[4,480,768]{2,1,0:T(8,128)(2,1)}), bf16[4,480,768]{2,1,0:T(8,128)(2,1)}, u32[]{:S(2)}, u32[]{:S(2)}) async-start(bf16[4,480,768]{2,1,0:T(8,128)(2,1)} %copy-done.4), calls=%async_computation.1 | async-start | bytes 5898240 | tf_op jit(solution)/shard_map/all_to_all | solution.py:647
  177.3 39.6 %all-to-all-start.3 = ((bf16[4,480,768]{2,1,0:T(8,128)(2,1)}), bf16[4,480,768]{2,1,0:T(8,128)(2,1)}, u32[]{:S(2)}, u32[]{:S(2)}) async-start(bf16[4,480,768]{2,1,0:T(8,128)(2,1)} %copy-done.6), calls=%async_computation.3 | async-start | bytes 5898240 | tf_op jit(solution)/shard_map/all_to_all | solution.py:647
  328.3 38.1 %all-to-all-start.5 = ((bf16[4,480,768]{2,1,0:T(8,128)(2,1)}), bf16[4,480,768]{2,1,0:T(8,128)(2,1)}, u32[]{:S(2)}, u32[]{:S(2)}) async-start(bf16[4,480,768]{2,1,0:T(8,128)(2,1)} %convolution_convert_fusion), calls=%async_computation.5 | async-start | bytes 5898240 | tf_op jit(solution)/shard_map/all_to_all | solution.py:647
  366.5 38.3 %all-to-all-start.2 = ((bf16[4,480,768]{2,1,0:T(8,128)(2,1)}), bf16[4,480,768]{2,1,0:T(8,128)(2,1)}, u32[]{:S(2)}, u32[]{:S(2)}) async-start(bf16[4,480,768]{2,1,0:T(8,128)(2,1)} %convolution_convert_fusion.1), calls=%async_computation.2 | async-start | bytes 5898240 | tf_op jit(solution)/shard_map/all_to_all | solution.py:647
  385.4 69.5 %collective-permute-start.48 = (bf16[2,512,384]{2,1,0:T(8,128)(2,1)}, bf16[2,512,384]{2,1,0:T(8,128)(2,1)}, u32[]{:S(2)}, u32[]{:S(2)}) collective-permute-start(bf16[2,512,384]{2,1,0:T(8,128)(2,1)} %fusion.17), channel_id=1, source_target_pairs={{0,16},{16,0},{1,17},{17,1},{2,18},{18,2},{3,19},{19,3},{4,20},{20... | collective-permute-start | bytes 2359304 | tf_op jit(solution)/shard_map/ppermute | solution.py:601
  404.8 52.2 %all-to-all-start.6 = ((bf16[4,480,768]{2,1,0:T(8,128)(2,1)}), bf16[4,480,768]{2,1,0:T(8,128)(2,1)}, u32[]{:S(2)}, u32[]{:S(2)}) async-start(bf16[4,480,768]{2,1,0:T(8,128)(2,1)} %get-tuple-element.41), calls=%async_computation.6 | async-start | bytes 5898240 | tf_op jit(solution)/shard_map/all_to_all | solution.py:647
  409.5 207.6 %all-reduce.16.cloned.1.call-start = ((), (), s32[]{:S(2)}) async-start(), calls=%async_computation.11 | async-start | bytes 2097152 | tf_op jit(solution)/shard_map/psum | solution.py:763
  418.7 110.0 %collective-permute-start.47 = (bf16[2,384,1024]{2,1,0:T(8,128)(2,1)}, bf16[2,384,1024]{2,1,0:T(8,128)(2,1)}, u32[]{:S(2)}, u32[]{:S(2)}) collective-permute-start(bf16[2,384,1024]{2,1,0:T(8,128)(2,1)} %fusion.5), channel_id=1, source_target_pairs={{0,16},{16,0},{1,17},{17,1},{2,18},{18,2},{3,19},{19,3},{4,20},{20... | collective-permute-start | bytes 4718600 | tf_op jit(solution)/shard_map/ppermute | solution.py:601
  444.9 41.0 %collective-permute-start.11 = (bf16[512,768]{1,0:T(8,128)(2,1)}, bf16[512,768]{1,0:T(8,128)(2,1)}, u32[]{:S(2)}, u32[]{:S(2)}) collective-permute-start(bf16[512,768]{1,0:T(8,128)(2,1)} %get-tuple-element.82), channel_id=1, source_target_pairs={{0,1},{3,2},{4,5},{7,6},{8,9},{11,10},{12,13},{15,14},{16,17},{19,... | collective-permute-start | bytes 2359304 | tf_op jit(solution)/shard_map/ppermute | solution.py:637
  450.4 38.1 %collective-permute-start.20 = (bf16[512,768]{1,0:T(8,128)(2,1)}, bf16[512,768]{1,0:T(8,128)(2,1)}, u32[]{:S(2)}, u32[]{:S(2)}) collective-permute-start(bf16[512,768]{1,0:T(8,128)(2,1)} %get-tuple-element.83), channel_id=1, source_target_pairs={{0,1},{3,2},{4,5},{7,6},{8,9},{11,10},{12,13},{15,14},{16,17},{19,... | collective-permute-start | bytes 2359304 | tf_op jit(solution)/shard_map/ppermute | solution.py:637
  452.6 48.8 %collective-permute-start.17 = (bf16[512,768]{1,0:T(8,128)(2,1)}, bf16[512,768]{1,0:T(8,128)(2,1)}, u32[]{:S(2)}, u32[]{:S(2)}) collective-permute-start(bf16[512,768]{1,0:T(8,128)(2,1)} %get-tuple-element.84), channel_id=1, source_target_pairs={{0,1},{3,2},{4,5},{7,6},{8,9},{11,10},{12,13},{15,14},{16,17},{19,... | collective-permute-start | bytes 2359304 | tf_op jit(solution)/shard_map/ppermute | solution.py:637
  454.8 63.4 %collective-permute-start.14 = (bf16[512,768]{1,0:T(8,128)(2,1)}, bf16[512,768]{1,0:T(8,128)(2,1)}, u32[]{:S(2)}, u32[]{:S(2)}) collective-permute-start(bf16[512,768]{1,0:T(8,128)(2,1)} %get-tuple-element.85), channel_id=1, source_target_pairs={{0,1},{3,2},{4,5},{7,6},{8,9},{11,10},{12,13},{15,14},{16,17},{19,... | collective-permute-start | bytes 2359304 | tf_op jit(solution)/shard_map/ppermute | solution.py:637
  485.9 49.2 %collective-permute-start.23 = (bf16[512,768]{1,0:T(8,128)(2,1)}, bf16[512,768]{1,0:T(8,128)(2,1)}, u32[]{:S(2)}, u32[]{:S(2)}) collective-permute-start(bf16[512,768]{1,0:T(8,128)(2,1)} %get-tuple-element.74), channel_id=1, source_target_pairs={{0,1},{3,2},{4,5},{7,6},{8,9},{11,10},{12,13},{15,14},{16,17},{19,... | collective-permute-start | bytes 2359304 | tf_op jit(solution)/shard_map/ppermute | solution.py:637
  488.5 130.0 %collective-permute-start.32 = (bf16[512,768]{1,0:T(8,128)(2,1)}, bf16[512,768]{1,0:T(8,128)(2,1)}, u32[]{:S(2)}, u32[]{:S(2)}) collective-permute-start(bf16[512,768]{1,0:T(8,128)(2,1)} %get-tuple-element.75), channel_id=1, source_target_pairs={{0,1},{3,2},{4,5},{7,6},{8,9},{11,10},{12,13},{15,14},{16,17},{19,... | collective-permute-start | bytes 2359304 | tf_op jit(solution)/shard_map/ppermute | solution.py:637
  501.4 117.9 %collective-permute-start.29 = (bf16[512,768]{1,0:T(8,128)(2,1)}, bf16[512,768]{1,0:T(8,128)(2,1)}, u32[]{:S(2)}, u32[]{:S(2)}) collective-permute-start(bf16[512,768]{1,0:T(8,128)(2,1)} %get-tuple-element.76), channel_id=1, source_target_pairs={{0,1},{3,2},{4,5},{7,6},{8,9},{11,10},{12,13},{15,14},{16,17},{19,... | collective-permute-start | bytes 2359304 | tf_op jit(solution)/shard_map/ppermute | solution.py:637
  518.2 102.2 %collective-permute-start.26 = (bf16[512,768]{1,0:T(8,128)(2,1)}, bf16[512,768]{1,0:T(8,128)(2,1)}, u32[]{:S(2)}, u32[]{:S(2)}) collective-permute-start(bf16[512,768]{1,0:T(8,128)(2,1)} %get-tuple-element.77), channel_id=1, source_target_pairs={{0,1},{3,2},{4,5},{7,6},{8,9},{11,10},{12,13},{15,14},{16,17},{19,... | collective-permute-start | bytes 2359304 | tf_op jit(solution)/shard_map/ppermute | solution.py:637
  528.7 96.1 %collective-permute-start.12 = (bf16[512,768]{1,0:T(8,128)(2,1)}, bf16[512,768]{1,0:T(8,128)(2,1)}, u32[]{:S(2)}, u32[]{:S(2)}) collective-permute-start(bf16[512,768]{1,0:T(8,128)(2,1)} %get-tuple-element.78), channel_id=1, source_target_pairs={{1,2},{2,1},{5,6},{6,5},{9,10},{10,9},{13,14},{14,13},{17,18},{18,... | collective-permute-start | bytes 2359304 | tf_op jit(solution)/shard_map/ppermute | solution.py:639
  535.1 92.9 %collective-permute-start.15 = (bf16[512,768]{1,0:T(8,128)(2,1)}, bf16[512,768]{1,0:T(8,128)(2,1)}, u32[]{:S(2)}, u32[]{:S(2)}) collective-permute-start(bf16[512,768]{1,0:T(8,128)(2,1)} %get-tuple-element.79), channel_id=1, source_target_pairs={{1,2},{2,1},{5,6},{6,5},{9,10},{10,9},{13,14},{14,13},{17,18},{18,... | collective-permute-start | bytes 2359304 | tf_op jit(solution)/shard_map/ppermute | solution.py:639
  632.7 262.3 %collective-permute-start.13 = (bf16[512,768]{1,0:T(8,128)(2,1)}, bf16[512,768]{1,0:T(8,128)(2,1)}, u32[]{:S(2)}, u32[]{:S(2)}) collective-permute-start(bf16[512,768]{1,0:T(8,128)(2,1)} %add_convert_fusion.14), channel_id=1, source_target_pairs={{1,0},{2,3},{5,4},{6,7},{9,8},{10,11},{13,12},{14,15},{17,16},{18,... | collective-permute-start | bytes 2359304 | tf_op jit(solution)/shard_map/ppermute | solution.py:641
  635.1 261.8 %collective-permute-start.16 = (bf16[512,768]{1,0:T(8,128)(2,1)}, bf16[512,768]{1,0:T(8,128)(2,1)}, u32[]{:S(2)}, u32[]{:S(2)}) collective-permute-start(bf16[512,768]{1,0:T(8,128)(2,1)} %add_convert_fusion.12), channel_id=1, source_target_pairs={{1,0},{2,3},{5,4},{6,7},{9,8},{10,11},{13,12},{14,15},{17,16},{18,... | collective-permute-start | bytes 2359304 | tf_op jit(solution)/shard_map/ppermute | solution.py:641
  636.6 76.4 %collective-permute-start.25 = (bf16[512,768]{1,0:T(8,128)(2,1)S(1)}, bf16[512,768]{1,0:T(8,128)(2,1)S(1)}, u32[]{:S(2)}, u32[]{:S(2)}) collective-permute-start(bf16[512,768]{1,0:T(8,128)(2,1)S(1)} %add_convert_fusion.6), channel_id=1, source_target_pairs={{1,0},{2,3},{5,4},{6,7},{9,8},{10,11},{13,12},{14,15},{17,16},{18,... | collective-permute-start | bytes 2359304 | tf_op jit(solution)/shard_map/ppermute | solution.py:641
  638.1 91.8 %collective-permute-start.28 = (bf16[512,768]{1,0:T(8,128)(2,1)S(1)}, bf16[512,768]{1,0:T(8,128)(2,1)S(1)}, u32[]{:S(2)}, u32[]{:S(2)}) collective-permute-start(bf16[512,768]{1,0:T(8,128)(2,1)S(1)} %add_convert_fusion.4), channel_id=1, source_target_pairs={{1,0},{2,3},{5,4},{6,7},{9,8},{10,11},{13,12},{14,15},{17,16},{18,... | collective-permute-start | bytes 2359304 | tf_op jit(solution)/shard_map/ppermute | solution.py:641
  639.6 108.0 %collective-permute-start.31 = (bf16[512,768]{1,0:T(8,128)(2,1)S(1)}, bf16[512,768]{1,0:T(8,128)(2,1)S(1)}, u32[]{:S(2)}, u32[]{:S(2)}) collective-permute-start(bf16[512,768]{1,0:T(8,128)(2,1)S(1)} %add_convert_fusion.2), channel_id=1, source_target_pairs={{1,0},{2,3},{5,4},{6,7},{9,8},{10,11},{13,12},{14,15},{17,16},{18,... | collective-permute-start | bytes 2359304 | tf_op jit(solution)/shard_map/ppermute | solution.py:641
  713.0 51.5 %collective-permute-start.34 = (bf16[512,768]{1,0:T(8,128)(2,1)S(1)}, bf16[512,768]{1,0:T(8,128)(2,1)S(1)}, u32[]{:S(2)}, u32[]{:S(2)}) collective-permute-start(bf16[512,768]{1,0:T(8,128)(2,1)S(1)} %add_convert_fusion), channel_id=1, source_target_pairs={{1,0},{2,3},{5,4},{6,7},{9,8},{10,11},{13,12},{14,15},{17,16},{18,... | collective-permute-start | bytes 2359304 | tf_op jit(solution)/shard_map/ppermute | solution.py:641
  729.8 168.3 %collective-permute-start.19 = (bf16[512,768]{1,0:T(8,128)(2,1)}, bf16[512,768]{1,0:T(8,128)(2,1)}, u32[]{:S(2)}, u32[]{:S(2)}) collective-permute-start(bf16[512,768]{1,0:T(8,128)(2,1)} %add_convert_fusion.10), channel_id=1, source_target_pairs={{1,0},{2,3},{5,4},{6,7},{9,8},{10,11},{13,12},{14,15},{17,16},{18,... | collective-permute-start | bytes 2359304 | tf_op jit(solution)/shard_map/ppermute | solution.py:641
  747.6 152.4 %collective-permute-start.22 = (bf16[512,768]{1,0:T(8,128)(2,1)}, bf16[512,768]{1,0:T(8,128)(2,1)}, u32[]{:S(2)}, u32[]{:S(2)}) collective-permute-start(bf16[512,768]{1,0:T(8,128)(2,1)} %add_convert_fusion.8), channel_id=1, source_target_pairs={{1,0},{2,3},{5,4},{6,7},{9,8},{10,11},{13,12},{14,15},{17,16},{18,... | collective-permute-start | bytes 2359304 | tf_op jit(solution)/shard_map/ppermute | solution.py:641
  (101 other events, 1207.2 us)
Sparse Core Ops, SparseCore 0:
  532.8 84.2 all-reduce.15

commit v2 on v1

v2 whole, which is shorter than its diff:
```python
import functools
import jax
import jax.numpy as jnp
from jax import lax
from jax.experimental import pallas as pl
from jax.experimental.pallas import tpu as pltpu
from jax.sharding import PartitionSpec as P

D = 768
HD = 64
EXPERTS = 8
ALL_EXPERTS = 12
SEQ_LEN = 1024
CAPACITY = 480
DOC_BLOCK = 64
EPS = 1e-06
NEG = -1e30

LANES = 128
BLK = 256
SENT = CAPACITY + 16
WIN = BLK + 16
QBLOCKS = SEQ_LEN // BLK
CHUNK = 256
PAD = 256
HALF = D // 2
NT = (((1,), (1,)), ((), ()))
TN = (((0,), (0,)), ((), ()))
F32 = jnp.float32
BF16 = jnp.bfloat16
MB = 1 << 20


def nn(a, b):
    return jnp.dot(a, b, preferred_element_type=F32)


def nt(a, b):
    return lax.dot_general(a, b, NT, preferred_element_type=F32)


def tn(a, b):
    return lax.dot_general(a, b, TN, preferred_element_type=F32)


def call(body, name, grid, in_specs, out_specs, out_shape, scratch=(), prefetch=0, vmem=48, aliases={}):
    return pl.pallas_call(
        body,
        name=name,
        input_output_aliases=aliases,
        out_shape=out_shape,
        grid_spec=pltpu.PrefetchScalarGridSpec(
            num_scalar_prefetch=prefetch,
            grid=grid,
            in_specs=in_specs,
            out_specs=out_specs,
            scratch_shapes=list(scratch),
        ),
        compiler_params=pltpu.CompilerParams(
            dimension_semantics=("arbitrary",) * len(grid), vmem_limit_bytes=vmem * MB
        ),
        cost_estimate=pl.CostEstimate(flops=1000, bytes_accessed=1000, transcendentals=0),
    )


def rows_spec(cols, offset=0):
    return pl.BlockSpec((BLK, cols), lambda i, *_: (i + offset, 0))


def full_spec(*shape):
    return pl.BlockSpec(shape, lambda *_: (0,) * len(shape))


def by_rows(body):
    @pl.loop(0, BLK // CHUNK)
    def _(i):
        body(pl.ds(pl.multiple_of(i * CHUNK, CHUNK), CHUNK))


def group_spec(count, cols, offset=0):
    return pl.BlockSpec((count, BLK, cols), lambda i, *_: (0, i + offset, 0))


def half_at(index):
    return pl.ds(pl.multiple_of(index * HALF, HALF), HALF)


def place_heads(values, out_ref, g):
    width = values.shape[1] // 3
    rest = jnp.zeros((values.shape[0], PAD - width), BF16)
    for c in range(3):
        out_ref[g, :, c * PAD : c * PAD + width] = values[:, c * width : (c + 1) * width]
        out_ref[g, :, c * PAD + width : (c + 1) * PAD] = rest


def project_first_body(at_ref, x_ref, gain_ref, mine_ref, other_ref, low_ref, out_ref):
    gain = gain_ref[...]

    def norm(rows):
        x = x_ref[rows, :].astype(F32)
        factor = lax.rsqrt(jnp.mean(x * x, axis=-1, keepdims=True) + EPS)
        low_ref[rows, :] = (x * factor * gain).astype(BF16)

    by_rows(norm)
    here, there = half_at(at_ref[0]), half_at(1 - at_ref[0])
    found = nn(low_ref[:, here], mine_ref[...]) + nn(low_ref[:, there], other_ref[...])
    place_heads(found.astype(BF16), out_ref, 0)


def project_first(place, tokens, gain, mine, other):
    rows = tokens.shape[0]
    cols = mine.shape[1]
    return call(
        project_first_body,
        "norm_project",
        (rows // BLK,),
        [rows_spec(D), full_spec(1, D), full_spec(HALF, cols), full_spec(HALF, cols)],
        [rows_spec(D), group_spec(1, 3 * PAD)],
        [jax.ShapeDtypeStruct((rows, D), BF16), jax.ShapeDtypeStruct((1, rows, 3 * PAD), BF16)],
        prefetch=1,
    )(place, tokens, gain, mine, other)


def project_rest_body(at_ref, low_ref, *rest):
    out_ref = rest[-1]
    here, there = half_at(at_ref[0]), half_at(1 - at_ref[0])
    for g in range(out_ref.shape[0]):
        found = nn(low_ref[:, here], rest[2 * g][...]) + nn(low_ref[:, there], rest[2 * g + 1][...])
        place_heads(found.astype(BF16), out_ref, g)


def project_rest(place, low, weights):
    rows = low.shape[0]
    cols = weights[0].shape[1]
    count = len(weights) // 2
    return call(
        project_rest_body,
        "project_rest",
        (rows // BLK,),
        [rows_spec(D)] + [full_spec(HALF, cols)] * len(weights),
        group_spec(count, 3 * PAD),
        jax.ShapeDtypeStruct((count, rows, 3 * PAD), BF16),
        prefetch=1,
    )(place, low, *weights)


TILES = ((0, 0), (0, 1), (1, None))


def heads_of(wide):
    lane = lax.broadcasted_iota(jnp.int32, (wide.shape[0], LANES), 1) < HD
    zero = jnp.zeros((wide.shape[0], LANES), wide.dtype)
    first, second = wide[:, :LANES], wide[:, LANES:]
    return (jnp.where(lane, first, zero), jnp.where(lane, zero, first), second)


def pair_mask(key_block, starts, diagonal):
    key_at = lax.broadcasted_iota(jnp.int32, (BLK, BLK), 0)
    mask = key_at >= starts - key_block * BLK
    if diagonal:
        mask = mask & (key_at <= lax.broadcasted_iota(jnp.int32, (BLK, BLK), 1))
    return mask


def block_at(kb):
    return pl.ds(kb * BLK, BLK) if isinstance(kb, int) else pl.ds(pl.multiple_of(kb * BLK, BLK), BLK)


def tile_of(ref, rows, part, h):
    low = part * PAD + TILES[h][0] * LANES
    return ref[0, rows, low : low + LANES]


def attend_body(low_ref, x_ref, start_ref, o_ref, lse_ref, vt_ref):
    seq = pl.program_id(1)
    for kb in range(QBLOCKS):
        vt_ref[kb] = x_ref[0, kb * BLK : (kb + 1) * BLK, 2 * PAD :].T
    for qb in range(QBLOCKS):
        here = slice(qb * BLK, (qb + 1) * BLK)
        queries = heads_of(x_ref[0, here, :PAD] * jnp.asarray(HD**-0.5, BF16))
        starts = start_ref[0, :, here]

        def scores_of(kb, diagonal):
            mask = pair_mask(kb, starts, diagonal)
            rows = block_at(kb)
            return [
                jnp.where(mask, nt(tile_of(x_ref, rows, 1, h), queries[h]), NEG) for h in range(3)
            ]

        def values_of(kb, h):
            return vt_ref[kb, h * HD : (h + 1) * HD, :]

        blocks = [(qb, scores_of(qb, True))]
        if qb:
            blocks.append((qb - 1, scores_of(qb - 1, False)))
        carry = []
        for h in range(3):
            highest = functools.reduce(
                jnp.maximum, [jnp.max(sc[h], axis=0, keepdims=True) for _, sc in blocks]
            )
            weights = [jnp.exp(sc[h] - highest) for _, sc in blocks]
            total = sum(jnp.sum(w, axis=0, keepdims=True) for w in weights)
            acc = sum(nn(values_of(kb, h), w.astype(BF16)) for (kb, _), w in zip(blocks, weights))
            carry += [highest, total, acc]

        def step(kb, carry):
            scores = scores_of(kb, False)
            out = []
            for h in range(3):
                highest, total, acc = carry[3 * h : 3 * h + 3]
                now = jnp.maximum(highest, jnp.max(scores[h], axis=0, keepdims=True))
                weights = jnp.exp(scores[h] - now)
                fade = jnp.exp(highest - now)
                total = total * fade + jnp.sum(weights, axis=0, keepdims=True)
                out += [now, total, acc * fade + nn(values_of(kb, h), weights.astype(BF16))]
            return tuple(out)

        if qb > 1:
            carry = lax.fori_loop(low_ref[seq * QBLOCKS + qb], qb - 1, step, tuple(carry))
        parts = [carry[3 * h + 2] / carry[3 * h + 1] for h in range(3)]
        parts.append(jnp.zeros((PAD - 3 * HD, BLK), F32))
        o_ref[0, here, :] = jnp.concatenate(parts, axis=0).T.astype(BF16)
        for h in range(3):
            lse_ref[0, 0, h : h + 1, here] = carry[3 * h] + jnp.log(carry[3 * h + 1])


def attend(qkv, starts, lowest):
    groups, rows = qkv.shape[:2]
    seqs = rows // SEQ_LEN
    return call(
        attend_body,
        "attend",
        (groups, seqs),
        [
            pl.BlockSpec((1, SEQ_LEN, 3 * PAD), lambda g, s, *_: (g, s, 0)),
            pl.BlockSpec((1, 1, SEQ_LEN), lambda g, s, *_: (s, 0, 0)),
        ],
        [
            pl.BlockSpec((1, SEQ_LEN, PAD), lambda g, s, *_: (g, s, 0)),
            pl.BlockSpec((1, 1, 3, SEQ_LEN), lambda g, s, *_: (g, s, 0, 0)),
        ],
        [
            jax.ShapeDtypeStruct((groups, rows, PAD), BF16),
            jax.ShapeDtypeStruct((groups, seqs, 3, SEQ_LEN), F32),
        ],
        scratch=[pltpu.VMEM((QBLOCKS, PAD, BLK), BF16)],
        prefetch=1,
    )(lowest, qkv, starts)


def attend_back_body(seq, low_ref, x_ref, start_ref, do_ref, o_ref, lse_ref, g_ref, kt_ref, dk_ref, dv_ref):
    pick = (
        lax.broadcasted_iota(jnp.int32, (8, PAD), 1) // HD
        == lax.broadcasted_iota(jnp.int32, (8, PAD), 0)
    ).astype(F32)
    for kb in range(QBLOCKS):
        kt_ref[kb] = x_ref[0, kb * BLK : (kb + 1) * BLK, PAD : 2 * PAD].T
    for qb in range(QBLOCKS):
        here = slice(qb * BLK, (qb + 1) * BLK)
        queries = heads_of(x_ref[0, here, :PAD] * jnp.asarray(HD**-0.5, BF16))
        upstream = do_ref[0, here, :]
        ups = heads_of(upstream)
        deltas = lax.dot_general(
            pick,
            upstream.astype(F32) * o_ref[0, here, :].astype(F32),
            NT,
            precision=lax.Precision.HIGHEST,
            preferred_element_type=F32,
        )
        starts = start_ref[0, :, here]

        def step(kb, carry, diagonal):
            at = block_at(kb)
            mask = pair_mask(kb, starts, diagonal)
            out, dks, dvs = [], [], []
            for h in range(3):
                scores = jnp.where(mask, nt(tile_of(x_ref, at, 1, h), queries[h]), NEG)
                weights = jnp.exp(scores - lse_ref[0, 0, h : h + 1, here])
                slopes = weights * (nt(tile_of(x_ref, at, 2, h), ups[h]) - deltas[h : h + 1, :])
                slopes = slopes.astype(BF16)
                dvs.append(nn(weights.astype(BF16), ups[h]))
                dks.append(nn(slopes, queries[h]))
                out.append(carry[h] + nn(kt_ref[kb, h * HD : (h + 1) * HD, :], slopes))
            for ref, grads in ((dk_ref, dks), (dv_ref, dvs)):
                if diagonal:
                    ref[at, :LANES] = grads[0] + grads[1]
                    ref[at, LANES:] = grads[2]
                else:
                    ref[at, :LANES] += grads[0] + grads[1]
                    ref[at, LANES:] += grads[2]
            return tuple(out)

        zero = jnp.zeros((HD, BLK), F32)
        carry = step(qb, (zero, zero, zero), True)
        if qb:
            carry = step(qb - 1, carry, False)
        if qb > 1:
            carry = lax.fori_loop(
                low_ref[seq * QBLOCKS + qb], qb - 1, lambda kb, c: step(kb, c, False), carry
            )
        parts = list(carry) + [jnp.zeros((PAD - 3 * HD, BLK), F32)]
        g_ref[0, here, :PAD] = (jnp.concatenate(parts, axis=0) * (HD**-0.5)).T.astype(BF16)
    g_ref[0, :, PAD : 2 * PAD] = dk_ref[...].astype(BF16)
    g_ref[0, :, 2 * PAD :] = dv_ref[...].astype(BF16)


def attend_back(seq, qkv, starts, lowest, grad_out, attended, log_sums):
    groups = qkv.shape[0]

    def block(cols, row):
        return pl.BlockSpec((1, SEQ_LEN, cols), lambda g, *_: (g, row, 0))

    return call(
        functools.partial(attend_back_body, seq),
        "attend_back",
        (groups,),
        [
            block(3 * PAD, seq),
            pl.BlockSpec((1, 1, SEQ_LEN), lambda g, *_: (seq, 0, 0)),
            block(PAD, 0),
            block(PAD, seq),
            pl.BlockSpec((1, 1, 3, SEQ_LEN), lambda g, *_: (g, seq, 0, 0)),
        ],
        block(3 * PAD, 0),
        jax.ShapeDtypeStruct((groups, SEQ_LEN, 3 * PAD), BF16),
        scratch=[
            pltpu.VMEM((QBLOCKS, PAD, BLK), BF16),
            pltpu.VMEM((SEQ_LEN, PAD), F32),
            pltpu.VMEM((SEQ_LEN, PAD), F32),
        ],
        prefetch=1,
    )(lowest, qkv, starts, grad_out, attended, log_sums)


def lane_of(shape):
    return lax.broadcasted_iota(jnp.int32, shape, 1)


def members_of(routes):
    lane = lane_of((routes.shape[0], LANES))
    return ((lane == routes[:, 0:1]) | (lane == routes[:, 1:2])).astype(F32)


def sum_groups(part_ref, rows):
    total = part_ref[0, rows, :]
    for g in range(1, part_ref.shape[0]):
        total = total + part_ref[g, rows, :]
    return total


def group_slot(at_ref, k, groups):
    return lax.rem(at_ref[1] - k + groups, groups)


def middle_body(groups, at_ref, first_ref, rest_ref, x_ref, gain_ref, rw_ref, cv_ref, cot_ref, prev_ref, *refs):
    weights = refs[: 2 * groups]
    after_ref, low_ref, info_ref, part_ref, dot_ref = refs[2 * groups :]
    here, there = half_at(at_ref[0]), half_at(1 - at_ref[0])
    for k in range(groups):
        width = weights[2 * k].shape[0]
        heads = (rest_ref[k - 1] if k else first_ref[0])[:, :width]
        slot = group_slot(at_ref, k, groups)
        part_ref[slot, :, here] = nn(heads, weights[2 * k][...])
        part_ref[slot, :, there] = nn(heads, weights[2 * k + 1][...])
    gain = gain_ref[...]

    def norm(rows):
        after = x_ref[rows, :].astype(F32) + sum_groups(part_ref, rows)
        after_ref[rows, :] = after
        factor = lax.rsqrt(jnp.mean(after * after, axis=-1, keepdims=True) + EPS)
        normed = after * factor * gain
        low_ref[rows, :] = normed.astype(BF16)
        dot = jnp.sum(cot_ref[rows, :].astype(F32) * normed, axis=-1, keepdims=True)
        dot_ref[rows, :] = jnp.broadcast_to(dot, (CHUNK, LANES))

    by_rows(norm)
    products = nt(low_ref[...], rw_ref[...])
    mine, swapped = products[:, :LANES], products[:, LANES:]
    dots = nt(cot_ref[...], cv_ref[...])
    lane = lane_of(mine.shape)
    logits = jnp.where(lane < ALL_EXPERTS, mine + prev_ref[...], NEG)
    grown = jnp.exp(logits - jnp.max(logits, axis=-1, keepdims=True))
    chances = grown / jnp.sum(grown, axis=-1, keepdims=True)
    mixing = 1.0 / (1.0 + jnp.exp(swapped - mine))
    info = jnp.where(lane < 12, chances, jnp.where(lane < 16, mixing, dots))
    info_ref[...] = jnp.where(lane == 18, dot_ref[...], info)


def middle(place, first, rest, weights, tokens, gain, rw, cv, cot, prev):
    rows = tokens.shape[0]
    groups = len(weights) // 2
    return call(
        functools.partial(middle_body, groups),
        "out_norm_route",
        (rows // BLK,),
        [
            group_spec(1, PAD),
            group_spec(groups - 1, PAD),
            rows_spec(D),
            full_spec(1, D),
            full_spec(2 * LANES, D),
            full_spec(LANES, D),
            rows_spec(D),
            rows_spec(LANES),
        ]
        + [full_spec(*w.shape) for w in weights],
        [rows_spec(D), rows_spec(D), rows_spec(LANES)],
        [
            jax.ShapeDtypeStruct((rows, D), F32),
            jax.ShapeDtypeStruct((rows, D), BF16),
            jax.ShapeDtypeStruct((rows, LANES), F32),
        ],
        scratch=[pltpu.VMEM((groups, BLK, D), F32), pltpu.VMEM((BLK, LANES), F32)],
        prefetch=1,
    )(place, first, rest, tokens, gain, rw, cv, cot, prev, *weights)


def dispatch_body(start_ref, rows_ref, rank_ref, out_ref, acc_ref):
    expert = pl.program_id(0)
    acc_ref[...] = jnp.zeros_like(acc_ref)
    blocks = rows_ref.shape[0] // BLK
    for tb in range(blocks):
        here = slice(tb * BLK, (tb + 1) * BLK)
        at = expert * (blocks + 1) + tb
        first = pl.multiple_of(start_ref[at] // 16 * 16, 16)
        slot = lax.broadcasted_iota(jnp.int32, (WIN, BLK), 0)
        chosen = jnp.where(rank_ref[0, :, here] - first == slot, 1.0, 0.0).astype(BF16)
        acc_ref[pl.ds(first, WIN), :] += nn(chosen, rows_ref[here, :]).astype(acc_ref.dtype)
    out_ref[0] = acc_ref[:CAPACITY, :]


def dispatch(rows, ranks, starts, dtype, name):
    count, cols = rows.shape
    experts = ranks.shape[0]
    return call(
        dispatch_body,
        name,
        (experts,),
        [full_spec(count, cols), pl.BlockSpec((1, 1, count), lambda e, *_: (e, 0, 0))],
        pl.BlockSpec((1, CAPACITY, cols), lambda e, *_: (e, 0, 0)),
        jax.ShapeDtypeStruct((experts, CAPACITY, cols), dtype),
        scratch=[pltpu.VMEM((CAPACITY + WIN, cols), dtype)],
        prefetch=1,
    )(starts, rows, ranks)


def combine_body(seq, blocks, start_ref, first_ref, second_ref, rank_ref, info_ref, *rest):
    block = pl.program_id(0)
    out_ref = rest[0]
    dg_ref = rest[1] if len(rest) == 2 else None
    if dg_ref is not None:

        @pl.when(block == 0)
        def _():
            refs = [(first_ref, second_ref)[e % 2].at[e // 2] for e in range(EXPERTS)]
            lines = []
            for r in range(2):
                lines += [ref[CAPACITY + r : CAPACITY + r + 1, :CAPACITY].astype(F32) for ref in refs]
            lines.append(jnp.zeros((LANES - 2 * EXPERTS, CAPACITY), F32))
            dg_ref[...] = jnp.concatenate(lines, axis=0).T.astype(BF16)

    tb = seq * QBLOCKS + pl.program_id(0)
    slot = lax.broadcasted_iota(jnp.int32, (BLK, WIN), 1)
    lane = lane_of((BLK, LANES))
    acc = jnp.zeros((BLK, D), F32)
    picked = jnp.zeros((BLK, LANES), F32)
    for expert in range(EXPERTS):
        rows_ref = (first_ref, second_ref)[expert % 2]
        low = start_ref[expert * (blocks + 1) + tb] // 16 * 16
        first = pl.multiple_of(jnp.minimum(low, CAPACITY - WIN), 16)
        chosen = jnp.where(rank_ref[:, expert : expert + 1] - first == slot, 1.0, 0.0).astype(BF16)
        acc += info_ref[:, expert : expert + 1] * nn(chosen, rows_ref[expert // 2, pl.ds(first, WIN), :])
        if dg_ref is not None:
            mine = (lane == expert) | (lane == EXPERTS + expert)
            got = jnp.where(mine, nn(chosen, dg_ref[pl.ds(first, WIN), :]), 0.0)
            picked += jnp.where(lane == expert, jnp.sum(got, axis=-1, keepdims=True), 0.0)
    if dg_ref is None:
        out_ref[...] = acc.astype(BF16)
    else:
        out_ref[pl.ds(pl.multiple_of(block * BLK, BLK), BLK), :] = acc.astype(BF16)
        dots = picked.T[:EXPERTS].astype(BF16)
        for i in range(QBLOCKS):

            @pl.when(block == i)
            def _():
                row = SEQ_LEN + i // 2 * EXPERTS
                out_ref[row : row + EXPERTS, i % 2 * BLK : (i % 2 + 1) * BLK] = dots

        @pl.when(block == 0)
        def _():
            out_ref[SEQ_LEN:, 2 * BLK :] = jnp.zeros((2 * EXPERTS, D - 2 * BLK), BF16)


def combine(seq, seqs, first, second, rank_cols, info, starts, dots, name):
    count = rank_cols.shape[0]
    blocks = count // BLK
    owners = first.shape[0]
    at = seq * QBLOCKS
    if not dots:
        out, out_spec = jax.ShapeDtypeStruct((seqs * SEQ_LEN, D), BF16), rows_spec(D)
    else:
        out = jax.ShapeDtypeStruct((SEQ_LEN + 2 * EXPERTS, D), BF16)
        out_spec = full_spec(*out.shape)
    return call(
        functools.partial(combine_body, seq, blocks),
        name,
        (seqs * QBLOCKS,),
        [
            full_spec(owners, first.shape[1], D),
            full_spec(owners, first.shape[1], D),
            rows_spec(LANES, at),
            rows_spec(LANES, at),
        ],
        out_spec,
        out,
        scratch=[pltpu.VMEM((CAPACITY, LANES), BF16)] if dots else [],
        prefetch=1,
    )(starts, first, second, rank_cols, info)


def expert_body(x_ref, c_ref, gu_ref, dn_ref, act_ref, both_ref, dx_ref):
    hidden = dn_ref.shape[0]
    both = nn(x_ref[0], gu_ref[...])
    gate, up = both[:, :hidden], both[:, hidden:]
    sig = jax.nn.sigmoid(gate)
    act = (gate * sig * up).astype(BF16)
    act_ref[0] = act
    grad_act = nt(c_ref[0], dn_ref[...])
    dots = jnp.sum(act.astype(F32) * grad_act, axis=-1, keepdims=True)
    dots = jnp.broadcast_to(dots, (CAPACITY, LANES)).T[:16]
    high = dots.astype(BF16).astype(F32)
    dots = jnp.where(lax.broadcasted_iota(jnp.int32, dots.shape, 0) == 0, high, dots - high)
    grad_gate = grad_act * up * sig * (1.0 + gate * (1.0 - sig))
    grad_up = grad_act * (gate * sig)
    grad_both = jnp.concatenate([grad_gate, grad_up], axis=-1).astype(BF16)
    both_ref[0] = grad_both
    dx_ref[0, :CAPACITY, :] = nt(grad_both, gu_ref[...]).astype(BF16)
    dots = jnp.concatenate([dots, jnp.zeros((16, D - CAPACITY), F32)], axis=1)
    dx_ref[0, CAPACITY:, :] = dots.astype(BF16)


def expert_core(x, cot, gate_up, down):
    sources = x.shape[0]
    hidden = down.shape[0]

    def block(cols):
        return pl.BlockSpec((1, CAPACITY, cols), lambda s: (s, 0, 0))

    return call(
        expert_body,
        "expert",
        (sources,),
        [block(D), block(D), full_spec(D, 2 * hidden), full_spec(hidden, D)],
        [block(hidden), block(2 * hidden), pl.BlockSpec((1, SENT, D), lambda s: (s, 0, 0))],
        [
            jax.ShapeDtypeStruct((sources, CAPACITY, hidden), BF16),
            jax.ShapeDtypeStruct((sources, CAPACITY, 2 * hidden), BF16),
            jax.ShapeDtypeStruct((sources, SENT, D), BF16),
        ],
    )(x, cot, gate_up, down)


def output_body(after_ref, moe_ref, info_ref, routes_ref, gain_ref, cv_ref, out_ref):
    gain = gain_ref[...]

    def finish(rows):
        after = after_ref[rows, :]
        factor = lax.rsqrt(jnp.mean(after * after, axis=-1, keepdims=True) + EPS)
        info = info_ref[rows, :]
        gates = info * members_of(routes_ref[rows, :])
        coef = gates[:, 9:10] + gates[:, 10:11] * info[:, 12:13] + gates[:, 11:12] * info[:, 14:15]
        out = after * (1.0 + (coef * factor) * gain) + moe_ref[rows, :].astype(F32)
        out = out + (gates[:, 10:11] * info[:, 13:14]) * cv_ref[0:1, :]
        out_ref[rows, :] = out + (gates[:, 11:12] * info[:, 15:16]) * cv_ref[1:2, :]

    by_rows(finish)


def finish_output(after, moe, info, routes, gain, cv):
    rows = after.shape[0]
    return call(
        output_body,
        "output",
        (rows // BLK,),
        [rows_spec(D), rows_spec(D), rows_spec(LANES), rows_spec(2), full_spec(1, D), full_spec(2, D)],
        rows_spec(D),
        jax.ShapeDtypeStruct((rows, D), F32),
    )(after, moe, info, routes, gain, cv)


def back_body(groups, at_ref, after_ref, cot_ref, moe_ref, info_ref, dg_ref, routes_ref, gain_ref, rw_ref, low_ref, *refs):
    weights = refs[: 2 * groups]
    grad_ref, glow_ref, first_ref, rest_ref, small_ref, routed_ref, coef_ref, sum_ref = refs[2 * groups :]
    block = pl.program_id(0)

    @pl.when(block == 0)
    def _():
        small_ref[...] = jnp.zeros_like(small_ref)
        sum_ref[...] = jnp.zeros_like(sum_ref)

    info = info_ref[...]
    members = members_of(routes_ref[...])
    gates = info * members
    lane = lane_of(info.shape)
    dot_normed = info[:, 18:19]
    dots = dg_ref[:, pl.ds(pl.multiple_of(block % 2 * BLK, BLK), BLK)].astype(F32)
    dots = jnp.where(block < 2, dots[:EXPERTS], dots[EXPERTS:])
    dots = jnp.concatenate([dots, jnp.zeros((LANES - EXPERTS, BLK), F32)], axis=0).T
    grad = jnp.where(lane < EXPERTS, dots, 0.0)
    grad = grad + jnp.where(lane == 9, dot_normed, 0.0)
    grad_mix = jnp.zeros_like(grad)
    coef = gates[:, 9:10]
    coefs = jnp.zeros_like(grad)
    for c in range(2):
        first, second = info[:, 12 + 2 * c : 13 + 2 * c], info[:, 13 + 2 * c : 14 + 2 * c]
        dot_const = info[:, 16 + c : 17 + c]
        weight = gates[:, 10 + c : 11 + c]
        inner = first * dot_normed + second * dot_const
        grad = grad + jnp.where(lane == 10 + c, inner, 0.0)
        grad_mix = grad_mix + jnp.where(lane == 12 + 2 * c, first * weight * (dot_normed - inner), 0.0)
        grad_mix = grad_mix + jnp.where(lane == 13 + 2 * c, second * weight * (dot_const - inner), 0.0)
        coef = coef + weight * first
        coefs = coefs + jnp.where(lane == 1 + c, weight * second, 0.0)
    coef_ref[...] = coefs + jnp.where(lane == 0, coef, 0.0)
    grad = grad * members
    chances = jnp.where(lane < ALL_EXPERTS, info, 0.0)
    grad_logits = chances * (grad - jnp.sum(chances * grad, axis=-1, keepdims=True))
    slopes = (grad_logits + grad_mix).astype(BF16)
    routed_ref[...] = nn(slopes, rw_ref[...])
    small_ref[0:16, :] += tn(slopes, low_ref[...])[:16, :]
    gain = gain_ref[...]

    def norm(rows):
        after = after_ref[rows, :]
        cot = cot_ref[rows, :].astype(F32)
        columns = coef_ref[rows, :]
        factor = lax.rsqrt(jnp.mean(after * after, axis=-1, keepdims=True) + EPS)
        xhat = after * factor
        grad_normed = columns[:, 0:1] * cot + routed_ref[rows, :] + moe_ref[rows, :].astype(F32)
        weighted = grad_normed * gain
        inner = jnp.mean(weighted * xhat, axis=-1, keepdims=True)
        grad_after = cot + factor * (weighted - xhat * inner)
        grad_ref[rows, :] = grad_after
        glow_ref[rows, :] = grad_after.astype(BF16)
        for i, value in enumerate((grad_normed * xhat, columns[:, 1:2] * cot, columns[:, 2:3] * cot)):
            total = value[0:8]
            for r in range(8, CHUNK, 8):
                total = total + value[r : r + 8]
            sum_ref[i] += total

    by_rows(norm)
    here, there = half_at(at_ref[0]), half_at(1 - at_ref[0])
    for k in range(groups):
        grad_heads = nt(glow_ref[:, here], weights[2 * k][...]) + nt(glow_ref[:, there], weights[2 * k + 1][...])
        width = grad_heads.shape[1]
        ref, g = (rest_ref, k - 1) if k else (first_ref, 0)
        ref[g, :, :width] = grad_heads.astype(BF16)
        ref[g, :, width:] = jnp.zeros((BLK, PAD - width), BF16)

    @pl.when(block == pl.num_programs(0) - 1)
    def _():
        for i in range(3):
            small_ref[16 + i : 17 + i, :] = jnp.sum(sum_ref[i], axis=0, keepdims=True)


def back(seq, place, after, cot, moe, info, routes, gain, rw, low, weights):
    at = seq * QBLOCKS
    groups = len(weights) // 2
    return call(
        functools.partial(back_body, groups),
        "route_norm_back",
        (QBLOCKS,),
        [
            rows_spec(D, at),
            rows_spec(D, at),
            rows_spec(D),
            rows_spec(LANES, at),
            pl.BlockSpec((2 * EXPERTS, D), lambda i, *_: (SEQ_LEN // (2 * EXPERTS), 0)),
            rows_spec(2, at),
            full_spec(1, D),
            full_spec(LANES, D),
            rows_spec(D, at),
        ]
        + [full_spec(*w.shape) for w in weights],
        [rows_spec(D), rows_spec(D), group_spec(1, PAD), group_spec(groups - 1, PAD), full_spec(24, D)],
        [
            jax.ShapeDtypeStruct((SEQ_LEN, D), F32),
            jax.ShapeDtypeStruct((SEQ_LEN, D), BF16),
            jax.ShapeDtypeStruct((1, SEQ_LEN, PAD), BF16),
            jax.ShapeDtypeStruct((groups - 1, SEQ_LEN, PAD), BF16),
            jax.ShapeDtypeStruct((24, D), F32),
        ],
        scratch=[pltpu.VMEM((BLK, D), F32), pltpu.VMEM((BLK, LANES), F32), pltpu.VMEM((3, 8, D), F32)],
        prefetch=1,
    )(place, after, cot, moe, info, moe, routes, gain, rw, low, *weights)


def final_body(groups, at_ref, first_ref, rest_ref, x_ref, gain_ref, after_ref, *refs):
    weights = refs[: 2 * groups]
    out_ref, small_ref, part_ref, sum_ref = refs[-4:]
    here, there = half_at(at_ref[0]), half_at(1 - at_ref[0])
    for k in range(groups):
        wide = rest_ref[k - 1] if k else first_ref[0]
        width = weights[2 * k].shape[1] // 3
        packed = jnp.concatenate([wide[:, c * PAD : c * PAD + width] for c in range(3)], axis=1)
        slot = group_slot(at_ref, k, groups)
        part_ref[slot, :, here] = nt(packed, weights[2 * k][...])
        part_ref[slot, :, there] = nt(packed, weights[2 * k + 1][...])

    @pl.when(pl.program_id(0) == 0)
    def _():
        sum_ref[...] = jnp.zeros_like(sum_ref)

    gain = gain_ref[...]

    def norm(rows):
        grad = sum_groups(part_ref, rows)
        x = x_ref[rows, :].astype(F32)
        factor = lax.rsqrt(jnp.mean(x * x, axis=-1, keepdims=True) + EPS)
        xhat = x * factor
        weighted = grad * gain
        inner = jnp.mean(weighted * xhat, axis=-1, keepdims=True)
        out_ref[rows, :] = after_ref[rows, :] + factor * (weighted - xhat * inner)
        value = grad * xhat
        total = value[0:8]
        for r in range(8, CHUNK, 8):
            total = total + value[r : r + 8]
        sum_ref[...] += total

    by_rows(norm)
    small_ref[...] = sum_ref[...]


def final(seq, place, first, rest, weights, tokens, gain, grad_after, earlier):
    rows = tokens.shape[0]
    at = seq * QBLOCKS
    groups = len(weights) // 2
    extra = [] if earlier is None else [earlier]
    return call(
        functools.partial(final_body, groups),
        "norm_back",
        (QBLOCKS,),
        [
            group_spec(1, 3 * PAD),
            group_spec(groups - 1, 3 * PAD),
            rows_spec(D, at),
            full_spec(1, D),
            rows_spec(D),
        ]
        + [full_spec(*w.shape) for w in weights]
        + [pl.BlockSpec(memory_space=pl.ANY)] * len(extra),
        [rows_spec(D, at), full_spec(8, D)],
        [jax.ShapeDtypeStruct((rows, D), F32), jax.ShapeDtypeStruct((8, D), F32)],
        scratch=[pltpu.VMEM((groups, BLK, D), F32), pltpu.VMEM((8, D), F32)],
        prefetch=1,
        aliases={6 + len(weights): 0} if extra else {},
    )(place, first, rest, tokens, gain, grad_after, *weights, *extra)


def gather_dp(x, axis):
    n = lax.axis_size("dp")
    if n != 2:
        return lax.all_gather(x, "dp", axis=axis, tiled=True)
    other = lax.ppermute(x, "dp", [(0, 1), (1, 0)])
    here = lax.axis_index("dp") == 0
    return jnp.concatenate([jnp.where(here, x, other), jnp.where(here, other, x)], axis=axis)


def scatter_dp(x, axis):
    n = lax.axis_size("dp")
    if n != 2:
        return lax.psum_scatter(x.astype(BF16), "dp", scatter_dimension=axis, tiled=True).astype(F32)
    half = x.shape[axis] // 2
    me = lax.axis_index("dp")
    keep = lax.dynamic_slice_in_dim(x, me * half, half, axis)
    send = lax.dynamic_slice_in_dim(x, (1 - me) * half, half, axis).astype(BF16)
    return keep.astype(F32) + lax.ppermute(send, "dp", [(0, 1), (1, 0)]).astype(F32)


def sum_over(x, axis_name):
    n = lax.axis_size(axis_name)
    if n & (n - 1):
        return lax.psum(x.astype(BF16), axis_name).astype(F32)
    step = 1
    while step < n:
        low = x.astype(BF16)
        other = lax.ppermute(low, axis_name, [(i, i ^ step) for i in range(n)])
        x = low.astype(F32) + other.astype(F32)
        step *= 2
    return x


def shifted(x):
    n = lax.axis_size("tensor")
    return [lax.ppermute(x, "tensor", [(i, (i + k) % n) for i in range(n)]) for k in range(1, n)]


def halves(x, axis):
    if lax.axis_size("dp") == 2:
        return [x, lax.ppermute(x, "dp", [(0, 1), (1, 0)])]
    return jnp.split(lax.all_gather(x, "dp", axis=axis, tiled=True), 2, axis=axis)


def join(part, other):
    return (part.astype(F32) + other.astype(F32)).astype(BF16)


def to_inner(part):
    return join(part, lax.ppermute(part, "tensor", [(0, 1), (3, 2)]))


def between_inner(part):
    return join(part, lax.ppermute(part, "tensor", [(1, 2), (2, 1)]))


def to_outer(part):
    me = lax.axis_index("tensor")
    other = lax.ppermute(part, "tensor", [(1, 0), (2, 3)])
    return jnp.where((me == 0) | (me == 3), other, part)


def exchange_small(x):
    n = lax.axis_size("expert")
    me = lax.axis_index("expert")
    return jnp.stack(
        [
            lax.ppermute(
                lax.dynamic_index_in_dim(x, me ^ k, 0, keepdims=False),
                "expert",
                [(i, i ^ k) for i in range(n)],
            )
            if k
            else lax.dynamic_index_in_dim(x, me, 0, keepdims=False)
            for k in range(n)
        ]
    )


def exchange(x):
    return lax.all_to_all(x, "expert", split_axis=0, concat_axis=0, tiled=True)


def route_tables(routes):
    count = routes.shape[0]
    blocks = count // BLK
    ids = jnp.arange(EXPERTS, dtype=jnp.int32)[:, None]
    member = (routes[:, 0][None, :] == ids) | (routes[:, 1][None, :] == ids)
    ones = member.astype(BF16).reshape(EXPERTS, blocks, BLK)
    earlier = (jnp.arange(BLK)[:, None] < jnp.arange(BLK)[None, :]).astype(BF16)
    inside = jnp.einsum("ebt,tu->ebu", ones, earlier, preferred_element_type=F32)
    counts = jnp.sum(ones.astype(F32), axis=-1)
    ends = jnp.cumsum(counts, axis=1)
    starts = ends - counts
    ranks = (inside + starts[:, :, None]).astype(jnp.int32).reshape(EXPERTS, count)
    ranks = jnp.where(member, ranks, -(1 << 20))
    bounds = jnp.concatenate([starts, ends[:, -1:]], axis=1)
    return (ranks, bounds.astype(jnp.int32))


def document_tables(segments):
    seqs = segments.shape[0] // SEQ_LEN
    marks = segments.reshape(seqs, SEQ_LEN // DOC_BLOCK, DOC_BLOCK)[:, :, 0]
    begin = DOC_BLOCK * jnp.sum((marks[:, None, :] < marks[:, :, None]).astype(jnp.int32), axis=-1)
    starts = jnp.broadcast_to(begin[:, :, None], begin.shape + (DOC_BLOCK,)).reshape(seqs, 1, SEQ_LEN)
    lowest = begin[:, :: BLK // DOC_BLOCK] // BLK
    return (starts, lowest.reshape(-1))


def three_parts(x):
    high = x.astype(BF16)
    rest = x - high.astype(F32)
    mid = rest.astype(BF16)
    return (high, mid, (rest - mid.astype(F32)).astype(BF16))


def on_device(
    tokens,
    prev_logits,
    routes,
    segments,
    gain_one,
    w_qkv,
    w_out,
    gain_two,
    router,
    const_proj,
    const_vec,
    w_gate_up,
    w_down,
    cotangent,
):
    rows = tokens.shape[0]
    owners = lax.axis_size("expert")
    groups = lax.axis_size("tensor")
    group = lax.axis_index("tensor")
    local_experts = EXPERTS // owners
    width = w_out.shape[0]
    slice_rows = w_qkv.shape[0]

    own_in = w_qkv.astype(BF16).reshape(slice_rows, 3 * width)
    rest_in = shifted(own_in)
    in_first = halves(own_in, 0)
    dp_at = lax.axis_index("dp") if lax.axis_size("dp") == 2 else jnp.int32(0)
    place = jnp.stack([dp_at, group]).astype(jnp.int32)
    small = jnp.concatenate(
        [router.T, const_proj.T, gain_one[None], gain_two[None], const_vec], axis=0
    ).astype(BF16)
    small = gather_dp(small, 1)
    gain_a = small[16:17].astype(F32)
    gain_b = small[17:18].astype(F32)
    const_rows = small[18:20].astype(F32)
    mains = jnp.pad(small[:16], ((0, LANES - 16), (0, 0)))
    swaps = jnp.stack([small[13], small[12], small[15], small[14]])
    routing = jnp.concatenate([mains, jnp.pad(swaps, ((12, LANES - 16), (0, 0)))], axis=0)
    const_low = jnp.pad(small[18:20], ((16, LANES - 18), (0, 0)))

    ranks, block_starts = route_tables(routes)
    rank_cols = jnp.pad(ranks.T, ((0, 0), (0, LANES - EXPERTS)))
    per_expert = ranks.reshape(owners, local_experts, 1, rows)
    per_start = block_starts.reshape(owners, local_experts, -1)
    table = [
        (per_expert[:, j], per_start[:, j].reshape(-1)) for j in range(local_experts)
    ]
    cot_in = [exchange(dispatch(cotangent, *table[0], BF16, "send_cot"))]
    me = lax.axis_index("expert")
    all_starts = block_starts.reshape(-1)

    hidden = w_down.shape[1]
    gate_up = gather_dp(w_gate_up.astype(BF16).reshape(local_experts, slice_rows, 2 * hidden), 1)
    down = gather_dp(w_down.astype(BF16), 2)

    starts, lowest = document_tables(segments)
    normed_low, qkv_first = project_first(place, tokens, gain_a, *in_first)
    attended_first, sums_first = attend(qkv_first, starts, lowest)
    out_master = w_out.astype(BF16)
    cot_late, attended_first, rest_in, out_master = lax.optimization_barrier(
        (cotangent, attended_first, rest_in, out_master)
    )
    in_rest = sum([halves(w, 0) for w in rest_in], [])
    in_all = in_first + in_rest
    out_all = sum([halves(w, 1) for w in [out_master] + shifted(out_master)], [])
    for j in range(1, local_experts):
        cot_in.append(exchange(dispatch(cot_late, *table[j], BF16, "send_cot")))
    qkv_rest = project_rest(place, normed_low, in_rest)
    attended_rest, sums_rest = attend(qkv_rest, starts, lowest)
    prev = jnp.pad(prev_logits, ((0, 0), (0, LANES - ALL_EXPERTS)))
    after_attn, routed_low, info = middle(
        place,
        attended_first,
        attended_rest,
        out_all,
        tokens,
        gain_b,
        routing,
        const_low,
        cotangent,
        prev,
    )

    routed_low, cot_in = lax.optimization_barrier((routed_low, cot_in))

    rows_in = [exchange(dispatch(routed_low, r, s, BF16, "send_rows")) for r, s in table]
    acts, boths, back_rows = [], [], []
    for j in range(local_experts):
        act, both, grad_rows = expert_core(rows_in[j], cot_in[j], gate_up[j], down[j])
        acts.append(act)
        boths.append(both)
        back_rows.append(exchange(grad_rows))
    seqs = rows // SEQ_LEN

    chance_parts = jnp.concatenate(
        [jnp.pad(p, ((0, 0), (0, 8))) for p in three_parts(info[:, :EXPERTS])], axis=1
    )
    chance_parts = jnp.pad(chance_parts, ((0, 0), (0, LANES - 48)))
    gates = []
    for j in range(local_experts):
        sent = dispatch(chance_parts, *table[j], F32, "send_gates")
        ids = local_experts * jnp.arange(owners)[:, None] + j
        mine = (jnp.arange(LANES)[None, :] % 16 == ids) & (jnp.arange(LANES)[None, :] < 48)
        gates.append(jnp.sum(jnp.where(mine[:, None, :], sent, 0.0), axis=-1))
    outs = [
        jnp.einsum("scf,fd->scd", acts[j], down[j], preferred_element_type=F32).astype(BF16)
        for j in range(local_experts)
    ]
    gates = jnp.stack(gates, axis=1)
    gates, back_rows = lax.optimization_barrier((gates, back_rows))
    gates = exchange_small(gates)
    gates = jnp.take(gates, me ^ jnp.arange(owners), axis=0)
    outs, back_rows = lax.optimization_barrier((outs, back_rows))
    grad_moe = []
    for seq in range(seqs):
        grad_part = combine(
            seq, 1, back_rows[0], back_rows[1], rank_cols, info, all_starts, True, "combine_grads"
        )
        half = SEQ_LEN // 2
        parts = [to_inner(p) for p in (grad_part[:half], grad_part[half:])]
        parts = [to_outer(between_inner(p)) for p in parts]
        grad_moe.append(jnp.concatenate(parts, axis=0))
    outs_back = [exchange(o) for o in outs]
    out_part = combine(
        0, seqs, outs_back[0], outs_back[1], rank_cols, info, all_starts, False, "combine_out"
    )

    out_sums = jnp.split(out_part, 4)

    grad_tokens = None
    grad_dense = small_grads = gain_grads = 0.0
    waiting = []
    grad_qkv = outs_back[0]
    for seq in range(seqs):
        if seq == 0:
            grad_moe[seq], grad_qkv = lax.optimization_barrier((grad_moe[seq], grad_qkv))
        else:
            grad_moe[seq], grad_qkv, out_sums[:2] = lax.optimization_barrier((grad_moe[seq], grad_qkv, out_sums[:2]))
            out_sums[:2] = [between_inner(p) for p in out_sums[:2]]
        grad_after, grad_low, att_first, att_rest, small_part = back(
            seq, place, after_attn, cotangent, grad_moe[seq], info, routes, gain_b, mains, routed_low, out_all
        )
        if seq == 0:
            att_first, att_rest, out_sums = lax.optimization_barrier((att_first, att_rest, out_sums))
            out_sums = [to_inner(p) for p in out_sums]
        here = slice(seq * SEQ_LEN, (seq + 1) * SEQ_LEN)
        grad_first = attend_back(seq, qkv_first, starts, lowest, att_first, attended_first, sums_first)
        grad_dense = grad_dense + jnp.concatenate(
            [
                jnp.einsum("td,tm->dm", normed_low[here], grad_first[0], preferred_element_type=F32),
                jnp.einsum("td,tm->dm", grad_low, attended_first[0, here], preferred_element_type=F32),
            ],
            axis=1,
        )
        small_grads = small_grads + small_part
        if seq == seqs - 1:
            grad_dense, att_rest, out_sums[0], out_sums[2] = lax.optimization_barrier(
                (grad_dense, att_rest, out_sums[0], out_sums[2])
            )
            out_sums[0] = to_outer(out_sums[0])
            out_sums[2] = between_inner(out_sums[2])
        grad_qkv = attend_back(seq, qkv_rest, starts, lowest, att_rest, attended_rest, sums_rest)
        waiting.append((grad_first, grad_qkv, grad_after))

    pieces = [grad_dense[:, c * PAD : c * PAD + width] for c in range(4)]
    grad_dense = scatter_dp(jnp.concatenate(pieces, axis=1), 0)
    small_grads = scatter_dp(small_grads, 1)
    for seq in range(seqs):
        if seq == 0:
            waiting[0], grad_dense, small_grads, out_sums[1:] = lax.optimization_barrier(
                (waiting[0], grad_dense, small_grads, out_sums[1:])
            )
            out_sums[3] = between_inner(out_sums[3])
            out_sums[1:3] = [to_outer(p) for p in out_sums[1:3]]
        if seq == seqs - 1:
            waiting[seq], out_sums[3] = lax.optimization_barrier((waiting[seq], out_sums[3]))
            out_sums[3] = to_outer(out_sums[3])
        grad_first, grad_qkv, grad_after = waiting[seq]
        grad_tokens, gain_part = final(
            seq, place, grad_first, grad_qkv, in_all, tokens, gain_a, grad_after, grad_tokens
        )
        gain_grads = gain_grads + gain_part
    grad_dense = sum_over(grad_dense, "expert")
    small_grads = sum_over(small_grads, "expert")

    output = finish_output(
        after_attn, jnp.concatenate(out_sums, axis=0), info, routes, gain_b, const_rows
    )

    grad_gate_up, grad_down = [], []
    for j in range(local_experts):
        gate = gates[:, j, :, None]
        gated = (gate * boths[j].astype(F32)).astype(BF16)
        gated_cot = (gate * cot_in[j].astype(F32)).astype(BF16)
        grad_gate_up.append(
            jnp.einsum("scd,scf->df", rows_in[j], gated, preferred_element_type=F32)
        )
        grad_down.append(
            jnp.einsum("scf,scd->fd", acts[j], gated_cot, preferred_element_type=F32)
        )
    grad_gate_up = scatter_dp(jnp.stack(grad_gate_up), 1).reshape(w_gate_up.shape)
    grad_down = scatter_dp(jnp.stack(grad_down), 2)

    gain_grads = sum_over(scatter_dp(jnp.sum(gain_grads, axis=0, keepdims=True), 1), "expert")
    return (
        output,
        grad_tokens,
        gain_grads[0],
        grad_dense[:, : 3 * width].reshape(w_qkv.shape),
        grad_dense[:, 3 * width :].T,
        small_grads[16],
        small_grads[:12].T,
        small_grads[12:16].T,
        small_grads[17:19],
        grad_gate_up,
        grad_down,
    )


def solution(mesh):
    token_spec = P(("dp", "expert"), None)
    weight_specs = (
        P("dp"),
        P("dp", None, "tensor"),
        P("tensor", "dp"),
        P("dp"),
        P("dp", None),
        P("dp", None),
        P(None, "dp"),
        P("expert", "dp", None, "tensor"),
        P("expert", "tensor", "dp"),
    )
    return jax.shard_map(
        on_device,
        mesh=mesh,
        in_specs=(token_spec, token_spec, token_spec, P(("dp", "expert"))) + weight_specs + (token_spec,),
        out_specs=(token_spec, token_spec) + weight_specs,
        check_vma=False,
    )
```

time: 968 us -> 771 us (0.80)
  waiting for transfers between devices: 324 us -> 165 us
  other arithmetic: 76.8 us -> 58.8 us
  local copies, waits for them, and re-layouts: 82.1 us -> 64.7 us
  starting transfers between devices: 117 us -> 131 us
  between operations: 15.7 us -> 3.14 us
    psum x1 -> x0, waiting for transfers between devices: 70.2 us -> none  [on_device(): dot_sums = lax.psum(dots_part[:, :EXPERTS].T, 'tensor').T]
    ppermute x30 -> x41, waiting for transfers between devices: 146 us -> 104 us  [the longest x8 62.4 us: to_outer(): other = lax.ppermute(part, 'tensor', [(1, 0), (2, 3)])]
    ppermute x30 -> x41, starting transfers between devices: 57.2 us -> 84.6 us  [the longest x8 42 us: to_inner(): return join(part, lax.ppermute(part, 'tensor', [(0, 1), (3, 2)]))]
    all_to_all x10 -> x8, waiting for transfers between devices: 84.9 us -> 58.7 us  [exchange(): return lax.all_to_all(x, 'expert', split_axis=0, concat_axis=0, tiled=True)]
    ppermute x8 -> x6, waiting for transfers between devices: 23.3 us -> 0.02 us  [sum_over(): other = lax.ppermute(low, axis_name, [(i, i ^ step) for i in range(n)])]
    dynamic_slice x2 -> x1, local copies, waits for them, and re-layouts: 10.4 us -> 0.01 us  [exchange_small(): lax.dynamic_index_in_dim(x, me, 0, keepdims=False)]
    all_to_all x10 -> x8, starting transfers between devices: 48.5 us -> 38.7 us  [exchange(): return lax.all_to_all(x, 'expert', split_axis=0, concat_axis=0, tiled=True)]
    unnamed x150 -> x242, local copies, waits for them, and re-layouts: 29.1 us -> 38.1 us
  transfers between devices with their start and end apart: 60 -> 63, of which waited for: 23 -> 17; matrix products, arithmetic and copies ran while one was open for 18% -> 16% of each run, Pallas kernels for 31% -> 37%
where the time goes in v2:
time: 771 us; the launch traced here: 761 us
  Pallas kernels  302 us (39%)
  waiting for transfers between devices  165 us (21%)
  starting transfers between devices  131 us (17%)
  local copies, waits for them, and re-layouts  64.7 us (8%)
  other arithmetic  58.8 us (8%)
  matrix products  36 us (5%)
    pallas_call x4, Pallas kernels, attend_back(): call(functools.partial(attend_back_body, seq), 'attend_back', (groups,),...  69 us
    ppermute x8, waiting for transfers between devices, to_outer(): other = lax.ppermute(part, 'tensor', [(1, 0), (2, 3)])  62.4 us
    all_to_all x8, waiting for transfers between devices, exchange(): return lax.all_to_all(x, 'expert', split_axis=0, concat_axis=0, tiled=True)  58.7 us
    pallas_call x3, Pallas kernels, combine(): call(functools.partial(combine_body, seq, blocks), name, (seqs * QBLOCKS,...  47.3 us
    ppermute x8, starting transfers between devices, to_inner(): return join(part, lax.ppermute(part, 'tensor', [(0, 1), (3, 2)]))  42 us
    all_to_all x8, starting transfers between devices, exchange(): return lax.all_to_all(x, 'expert', split_axis=0, concat_axis=0, tiled=True)  38.7 us
    unnamed x242, local copies, waits for them, and re-layouts  38.1 us
    pallas_call x2, Pallas kernels, back(): call(functools.partial(back_body, groups), 'route_norm_back', (QBLOCKS,),...  31.6 us
  transfers between devices with their start and end apart: 63, of which 17 were waited for; matrix products, arithmetic and copies ran while one was open for 16% of the time, Pallas kernels for 37%

profile of v2, /device:TPU:0, one launch (start us, length us, event | category | flops | bytes accessed | tf_op | source)
XLA Modules:
  0.0 761.4 jit_solution(5470460100804016362)
XLA Ops:
  24.8 9.6 %norm_project.1 = (bf16[2048,768]{1,0:T(8,128)(2,1)S(1)}, bf16[1,2048,768]{2,1,0:T(8,128)(2,1)}) custom-call(s32[2]{0:T(128)S(1)} %pad_add_fusion.at_ref, bf16[2048,768]{1,0:T(8,128)(2,1)} %x_ref.7, f32[1,768]{1,0:T(1,128)S(1)} %get-tuple-element.184.gain_ref, bf16[384,576]{1,0:T(8,128)(2,1)S(1)} %copy.90.mine_ref.refs_0_, ...), custom_call_target="tpu_custom_call" | custom-call | flops 1000 | bytes 1000 | tf_op jit(solution)/shard_map/norm_project/pallas_call | solution.py:113
  38.1 6.9 attend.2
  45.0 9.4 %collective-permute-done.3.rest_2_.refs_4_ = bf16[384,576]{1,0:T(8,128)(2,1)S(1)} collective-permute-done((bf16[384,576]{1,0:T(8,128)(2,1)S(1)}, bf16[384,576]{1,0:T(8,128)(2,1)S(1)}, u32[]{:S(2)}, u32[]{:S(2)}) %collective-permute-start.3) | collective-permute-done | bytes 442400 | tf_op jit(solution)/shard_map/ppermute | solution.py:795
  66.1 11.1 %collective-permute-start.9 = (bf16[192,384]{1,0:T(8,128)(2,1)S(1)}, bf16[192,384]{1,0:T(8,128)(2,1)}, u32[]{:S(2)}, u32[]{:S(2)}) collective-permute-start(bf16[192,384]{1,0:T(8,128)(2,1)S(1)} %convert_element_type.339.refs_0_), channel_id=1, source_target_pairs={{0,1},{1,2},{2,3},{3,0},{4,5},{5,6},{6,7},{7,4},{8,9},{9,10},{10,1... | collective-permute-start | bytes 442376 | tf_op jit(solution)/shard_map/ppermute | solution.py:795
  82.7 6.9 collective-permute-done.11.refs_4_
  91.6 13.7 %project_rest.1.x_ref = bf16[3,2048,768]{2,1,0:T(8,128)(2,1)} custom-call(s32[2]{0:T(128)S(1)} %pad_add_fusion.at_ref, bf16[2048,768]{1,0:T(8,128)(2,1)S(1)} %copy-done.37, bf16[384,576]{1,0:T(8,128)(2,1)S(1)} %collective-permute-done.2.rest_0_.refs_2_, bf16[384,576]{1,0:T(8,128)(2,1)S(1)} %collective-permute-done.5.rest_1_.refs_3_, ...), custom_call_target="tpu_custom_call" | custom-call | flops 1000 | bytes 1000 | tf_op jit(solution)/shard_map/project_rest/pallas_call | solution.py:136
  105.3 20.9 %attend.3 = (bf16[3,2048,256]{2,1,0:T(8,128)(2,1)S(1)}, f32[3,2,3,1024]{3,2,1,0:T(4,128)S(1)}) custom-call(s32[8]{0:T(128)S(1)} %reshape.276.low_ref, bf16[3,2048,768]{2,1,0:T(8,128)(2,1)} %project_rest.1.x_ref, s32[2,1,1024]{2,1,0:T(1,128)S(1)} %reshape.278.start_ref), custom_call_target="tpu_custom_call" | custom-call | flops 1000 | bytes 1000 | tf_op jit(solution)/shard_map/attend/pallas_call | solution.py:230
  128.7 14.3 %out_norm_route.1 = (f32[2048,768]{1,0:T(8,128)}, bf16[2048,768]{1,0:T(8,128)(2,1)}, f32[2048,128]{1,0:T(8,128)S(1)}) custom-call(s32[2]{0:T(128)S(1)} %pad_add_fusion.at_ref, bf16[1,2048,256]{2,1,0:T(8,128)(2,1)S(1)} %get-tuple-element.84.first_ref.o_ref, bf16[3,2048,256]{2,1,0:T(8,128)(2,1)} %copy-done.4, bf16[2048,768]{1,0:T(8,128)(2,1)} %x_ref.7, ...), custom_call_target="tpu_custom_call" | custom-call | flops 1000 | bytes 1000 | tf_op jit(solution)/shard_map/out_norm_route/pallas_call | solution.py:392
  168.3 24.3 %all-to-all-done.3.x_ref = bf16[4,480,768]{2,1,0:T(8,128)(2,1)} async-done(((bf16[4,480,768]{2,1,0:T(8,128)(2,1)}), bf16[4,480,768]{2,1,0:T(8,128)(2,1)}, u32[]{:S(2)}, u32[]{:S(2)}) %all-to-all-start.3) | async-done | bytes 2949152 | tf_op jit(solution)/shard_map/all_to_all | solution.py:840
  214.2 12.6 %expert.3 = (bf16[4,480,512]{2,1,0:T(8,128)(2,1)S(1)}, bf16[4,480,1024]{2,1,0:T(8,128)(2,1)}, bf16[4,496,768]{2,1,0:T(8,128)(2,1)}) custom-call(bf16[4,480,768]{2,1,0:T(8,128)(2,1)} %all-to-all-done.3.x_ref, bf16[4,480,768]{2,1,0:T(8,128)(2,1)} %all-to-all-done.1.c_ref, bf16[768,1024]{1,0:T(8,128)(2,1)S(1)} %get-tuple-element.170.gu_ref, ...), custom_call_target="tpu_custom_call" | custom-call | flops 1000 | bytes 1000 | tf_op jit(solution)/shard_map/expert/pallas_call | solution.py:549
  243.8 12.7 %expert.2 = (bf16[4,480,512]{2,1,0:T(8,128)(2,1)S(1)}, bf16[4,480,1024]{2,1,0:T(8,128)(2,1)}, bf16[4,496,768]{2,1,0:T(8,128)(2,1)}) custom-call(bf16[4,480,768]{2,1,0:T(8,128)(2,1)} %all-to-all-done.2.x_ref, bf16[4,480,768]{2,1,0:T(8,128)(2,1)} %all-to-all-done.c_ref, bf16[768,1024]{1,0:T(8,128)(2,1)S(1)} %copy-done.18, bf16[512,768]{1,0:T(8,128)(2,1)S(1)} %copy-done.39), custom_call_target="tpu_custom_call" | custom-call | flops 1000 | bytes 1000 | tf_op jit(solution)/shard_map/expert/pallas_call | solution.py:549
  257.8 12.6 %all-to-all-done.5.second_ref = bf16[4,496,768]{2,1,0:T(8,128)(2,1)} async-done(((bf16[4,496,768]{2,1,0:T(8,128)(2,1)}), bf16[4,496,768]{2,1,0:T(8,128)(2,1)}, u32[]{:S(2)}, u32[]{:S(2)}) %all-to-all-start.5) | async-done | bytes 3047456 | tf_op jit(solution)/shard_map/all_to_all | solution.py:840
  291.1 18.9 %all-to-all-done.4.first_ref = bf16[4,496,768]{2,1,0:T(8,128)(2,1)} async-done(((bf16[4,496,768]{2,1,0:T(8,128)(2,1)}), bf16[4,496,768]{2,1,0:T(8,128)(2,1)}, u32[]{:S(2)}, u32[]{:S(2)}) %all-to-all-start.4) | async-done | bytes 3047456 | tf_op jit(solution)/shard_map/all_to_all | solution.py:840
  318.5 13.8 %combine_grads.2 = bf16[1040,768]{1,0:T(8,128)(2,1)S(1)} custom-call(s32[72]{0:T(128)S(1)} %copy-done.77, bf16[4,496,768]{2,1,0:T(8,128)(2,1)} %all-to-all-done.4.first_ref, bf16[4,496,768]{2,1,0:T(8,128)(2,1)} %all-to-all-done.5.second_ref, s32[2048,128]{1,0:T(8,128)S(1)} %pad.42.rank_ref, f32[2048,128]{1,0:T(8,128)S(1)} %get-tuple-element.99.info_ref), custom_call_target="tpu_custom_call" | custom-call | flops 1000 | bytes 1000 | tf_op jit(solution)/shard_map/combine_grads/pallas_call | solution.py:504
  332.3 13.5 %combine_grads.3 = bf16[1040,768]{1,0:T(8,128)(2,1)S(1)} custom-call(s32[72]{0:T(128)S(1)} %copy-done.77, bf16[4,496,768]{2,1,0:T(8,128)(2,1)} %all-to-all-done.4.first_ref, bf16[4,496,768]{2,1,0:T(8,128)(2,1)} %all-to-all-done.5.second_ref, s32[2048,128]{1,0:T(8,128)S(1)} %pad.42.rank_ref, f32[2048,128]{1,0:T(8,128)S(1)} %get-tuple-element.99.info_ref), custom_call_target="tpu_custom_call" | custom-call | flops 1000 | bytes 1000 | tf_op jit(solution)/shard_map/combine_grads/pallas_call | solution.py:504
  401.3 10.6 %collective-permute-done.23 = bf16[512,768]{1,0:T(8,128)(2,1)} collective-permute-done((bf16[512,768]{1,0:T(8,128)(2,1)}, bf16[512,768]{1,0:T(8,128)(2,1)}, u32[]{:S(2)}, u32[]{:S(2)}) %collective-permute-start.23) | collective-permute-done | bytes 786464 | tf_op jit(solution)/shard_map/ppermute | solution.py:809
  438.4 20.1 %combine_out.1 = bf16[2048,768]{1,0:T(8,128)(2,1)} custom-call(s32[72]{0:T(128)S(1)} %copy-done.77, bf16[4,480,768]{2,1,0:T(8,128)(2,1)} %all-to-all-done.6.first_ref, bf16[4,480,768]{2,1,0:T(8,128)(2,1)} %all-to-all-done.7.second_ref, s32[2048,128]{1,0:T(8,128)S(1)} %pad.42.rank_ref, f32[2048,128]{1,0:T(8,128)S(1)} %get-tuple-element.99.info_ref), custom_call_target="tpu_custom_call" | custom-call | flops 1000 | bytes 1000 | tf_op jit(solution)/shard_map/combine_out/pallas_call | solution.py:504
  461.8 10.4 %collective-permute-done.25 = bf16[512,768]{1,0:T(8,128)(2,1)} collective-permute-done((bf16[512,768]{1,0:T(8,128)(2,1)}, bf16[512,768]{1,0:T(8,128)(2,1)}, u32[]{:S(2)}, u32[]{:S(2)}) %collective-permute-start.25) | collective-permute-done | bytes 786464 | tf_op jit(solution)/shard_map/ppermute | solution.py:818
  473.5 16.2 %collective-permute-done.22 = bf16[528,768]{1,0:T(8,128)(2,1)} collective-permute-done((bf16[528,768]{1,0:T(8,128)(2,1)}, bf16[528,768]{1,0:T(8,128)(2,1)}, u32[]{:S(2)}, u32[]{:S(2)}) %collective-permute-start.22) | collective-permute-done | bytes 811040 | tf_op jit(solution)/shard_map/ppermute | solution.py:818
  492.6 15.8 %route_norm_back.2 = (f32[1024,768]{1,0:T(8,128)}, bf16[1024,768]{1,0:T(8,128)(2,1)S(1)}, bf16[1,1024,256]{2,1,0:T(8,128)(2,1)S(1)}, bf16[3,1024,256]{2,1,0:T(8,128)(2,1)}, f32[24,768]{1,0:T(8,128)S(1)}) custom-call(s32[2]{0:T(128)S(1)} %copy-done.69, f32[2048,768]{1,0:T(8,128)} %get-tuple-element.91.after_ref, bf16[2048,768]{1,0:T(8,128)(2,1)} %cot_ref.5, ...), custom_call_target="tpu_custom_call" | custom-call | flops 1000 | bytes 1000 | tf_op jit(solution)/shard_map/route_norm_back/pallas_call | solution.py:669
  508.3 23.0 %collective-permute-start.38 = (bf16[512,768]{1,0:T(8,128)(2,1)S(1)}, bf16[512,768]{1,0:T(8,128)(2,1)}, u32[]{:S(2)}, u32[]{:S(2)}) collective-permute-start(bf16[512,768]{1,0:T(8,128)(2,1)S(1)} %get-tuple-element.131), channel_id=1, source_target_pairs={{0,1},{3,2},{4,5},{7,6},{8,9},{11,10},{12,13},{15,14},{16,17},{19,... | collective-permute-start | bytes 2359304 | tf_op jit(solution)/shard_map/ppermute | solution.py:809
  543.0 26.5 %attend_back.5.rest_ref = bf16[3,1024,768]{2,1,0:T(8,128)(2,1)} custom-call(s32[8]{0:T(128)S(1)} %copy-done.72, bf16[3,2048,768]{2,1,0:T(8,128)(2,1)} %project_rest.1.x_ref, s32[2,1,1024]{2,1,0:T(1,128)S(1)} %copy-done.59, bf16[3,1024,256]{2,1,0:T(8,128)(2,1)S(1)} %copy-done.45, bf16[3,2048,256]{2,1,0:T(8,128)(2,1)S(1)} %copy-done.5, ...), custom_call_target="tpu_custom_call" | custom-call | flops 1000 | bytes 1000 | tf_op jit(solution)/shard_map/attend_back/pallas_call | solution.py:313
  569.6 10.0 %attend_back.4.first_ref = bf16[1,1024,768]{2,1,0:T(8,128)(2,1)S(1)} custom-call(s32[8]{0:T(128)S(1)} %copy-done.72, bf16[1,2048,768]{2,1,0:T(8,128)(2,1)} %get-tuple-element.82.x_ref, s32[2,1,1024]{2,1,0:T(1,128)S(1)} %copy-done.59, bf16[1,1024,256]{2,1,0:T(8,128)(2,1)S(1)} %get-tuple-element.111.do_ref, bf16[1,2048,256]{2,1,0:T(8,128)(2,1)S(1)} %copy-done.15, ...), custom_call_target="tpu_custom_call" | custom-call | flops 1000 | bytes 1000 | tf_op jit(solution)/shard_map/attend_back/pallas_call | solution.py:313
  583.8 7.6 %collective-permute-done.29 = bf16[512,768]{1,0:T(8,128)(2,1)} collective-permute-done((bf16[512,768]{1,0:T(8,128)(2,1)S(1)}, bf16[512,768]{1,0:T(8,128)(2,1)}, u32[]{:S(2)}, u32[]{:S(2)}) %collective-permute-start.29) | collective-permute-done | bytes 786464 | tf_op jit(solution)/shard_map/ppermute | solution.py:809
  594.3 15.8 %route_norm_back.3 = (f32[1024,768]{1,0:T(8,128)}, bf16[1024,768]{1,0:T(8,128)(2,1)S(1)}, bf16[1,1024,256]{2,1,0:T(8,128)(2,1)S(1)}, bf16[3,1024,256]{2,1,0:T(8,128)(2,1)}, f32[24,768]{1,0:T(8,128)S(1)}) custom-call(s32[2]{0:T(128)S(1)} %copy-done.69, f32[2048,768]{1,0:T(8,128)} %get-tuple-element.91.after_ref, bf16[2048,768]{1,0:T(8,128)(2,1)} %cot_ref.5, ...), custom_call_target="tpu_custom_call" | custom-call | flops 1000 | bytes 1000 | tf_op jit(solution)/shard_map/route_norm_back/pallas_call | solution.py:669
  610.1 8.9 %attend_back.6.first_ref = bf16[1,1024,768]{2,1,0:T(8,128)(2,1)S(1)} custom-call(s32[8]{0:T(128)S(1)} %copy-done.72, bf16[1,2048,768]{2,1,0:T(8,128)(2,1)} %get-tuple-element.82.x_ref, s32[2,1,1024]{2,1,0:T(1,128)S(1)} %copy-done.59, bf16[1,1024,256]{2,1,0:T(8,128)(2,1)S(1)} %get-tuple-element.119.do_ref, bf16[1,2048,256]{2,1,0:T(8,128)(2,1)S(1)} %copy-done.15, ...), custom_call_target="tpu_custom_call" | custom-call | flops 1000 | bytes 1000 | tf_op jit(solution)/shard_map/attend_back/pallas_call | solution.py:313
  648.6 23.6 %attend_back.7.rest_ref = bf16[3,1024,768]{2,1,0:T(8,128)(2,1)} custom-call(s32[8]{0:T(128)S(1)} %copy-done.72, bf16[3,2048,768]{2,1,0:T(8,128)(2,1)} %project_rest.1.x_ref, s32[2,1,1024]{2,1,0:T(1,128)S(1)} %copy-done.59, bf16[3,1024,256]{2,1,0:T(8,128)(2,1)S(1)} %copy-done.44, bf16[3,2048,256]{2,1,0:T(8,128)(2,1)S(1)} %copy-done.6, ...), custom_call_target="tpu_custom_call" | custom-call | flops 1000 | bytes 1000 | tf_op jit(solution)/shard_map/attend_back/pallas_call | solution.py:313
  679.8 12.3 %norm_back.2 = (f32[2048,768]{1,0:T(8,128)}, f32[8,768]{1,0:T(8,128)S(1)}) custom-call(s32[2]{0:T(128)S(1)} %copy-done.69, bf16[1,1024,768]{2,1,0:T(8,128)(2,1)S(1)} %copy-done.20, bf16[3,1024,768]{2,1,0:T(8,128)(2,1)} %attend_back.5.rest_ref, bf16[2048,768]{1,0:T(8,128)(2,1)} %x_ref.7, f32[1,768]{1,0:T(1,128)S(1)} %copy-done.67, ...), custom_call_target="tpu_custom_call" | custom-call | flops 1000 | bytes 1000 | tf_op jit(solution)/shard_map/norm_back/pallas_call | solution.py:739
  694.7 12.3 %norm_back.3 = (f32[2048,768]{1,0:T(8,128)}, f32[8,768]{1,0:T(8,128)S(1)}) custom-call(s32[2]{0:T(128)S(1)} %copy-done.69, bf16[1,1024,768]{2,1,0:T(8,128)(2,1)S(1)} %copy-done.22, bf16[3,1024,768]{2,1,0:T(8,128)(2,1)} %attend_back.7.rest_ref, bf16[2048,768]{1,0:T(8,128)(2,1)} %x_ref.7, f32[1,768]{1,0:T(1,128)S(1)} %copy-done.67, ...), custom_call_target="tpu_custom_call", output_to_operand_aliasing={{0}: (14, {})} | custom-call | flops 1000 | bytes 1000 | tf_op jit(solution)/shard_map/norm_back/pallas_call | solution.py:739
  717.5 13.7 %collective-permute-done.40 = bf16[512,768]{1,0:T(8,128)(2,1)S(1)} collective-permute-done((bf16[512,768]{1,0:T(8,128)(2,1)S(1)}, bf16[512,768]{1,0:T(8,128)(2,1)S(1)}, u32[]{:S(2)}, u32[]{:S(2)}) %collective-permute-start.40) | collective-permute-done | bytes 786464 | tf_op jit(solution)/shard_map/ppermute | solution.py:818
  733.8 16.1 %collective-permute-done.42 = bf16[512,768]{1,0:T(8,128)(2,1)S(1)} collective-permute-done((bf16[512,768]{1,0:T(8,128)(2,1)S(1)}, bf16[512,768]{1,0:T(8,128)(2,1)S(1)}, u32[]{:S(2)}, u32[]{:S(2)}) %collective-permute-start.42) | collective-permute-done | bytes 786464 | tf_op jit(solution)/shard_map/ppermute | solution.py:818
  750.7 10.2 %output.1 = f32[2048,768]{1,0:T(8,128)} custom-call(f32[2048,768]{1,0:T(8,128)} %get-tuple-element.91.after_ref, bf16[2048,768]{1,0:T(8,128)(2,1)S(1)} %pad_maximum_fusion.moe_ref, f32[2048,128]{1,0:T(8,128)S(1)} %get-tuple-element.99.info_ref, s32[2048,2]{1,0:T(8,128)S(1)} %copy.97.routes_ref, f32[1,768]{1,0:T(1,128)S(1)} %copy-done.65, f32[2,768]{1,0:T(2,128)S(1)} %copy-done.70), custom_call_target="tpu_custom_call" | custom-call | flops 1000 | bytes 1000 | tf_op jit(solution)/shard_map/output/pallas_call | solution.py:581
  (511 shorter events, 304.1 us)
Async XLA Ops:
  11.0 49.8 %all-to-all-start = ((bf16[4,480,768]{2,1,0:T(8,128)(2,1)}), bf16[4,480,768]{2,1,0:T(8,128)(2,1)}, u32[]{:S(2)}, u32[]{:S(2)}) async-start(bf16[4,480,768]{2,1,0:T(8,128)(2,1)} %send_cot.2), calls=%async_computation | async-start | bytes 5898240 | tf_op jit(solution)/shard_map/all_to_all | solution.py:840
  60.8 84.8 %all-to-all-start.1 = ((bf16[4,480,768]{2,1,0:T(8,128)(2,1)}), bf16[4,480,768]{2,1,0:T(8,128)(2,1)}, u32[]{:S(2)}, u32[]{:S(2)}) async-start(bf16[4,480,768]{2,1,0:T(8,128)(2,1)} %send_cot.3), calls=%async_computation.1 | async-start | bytes 5898240 | tf_op jit(solution)/shard_map/all_to_all | solution.py:840
  89.6 39.1 %collective-permute-start.8 = (bf16[192,384]{1,0:T(8,128)(2,1)S(1)}, bf16[192,384]{1,0:T(8,128)(2,1)S(1)}, u32[]{:S(2)}, u32[]{:S(2)}) collective-permute-start(bf16[192,384]{1,0:T(8,128)(2,1)S(1)} %convert_element_type.339.refs_0_), channel_id=1, source_target_pairs={{0,16},{16,0},{1,17},{17,1},{2,18},{18,2},{3,19},{19,3},{4,20},{20... | collective-permute-start | bytes 442376 | tf_op jit(solution)/shard_map/ppermute | solution.py:800
  90.2 38.5 %collective-permute-start.10 = (bf16[192,384]{1,0:T(8,128)(2,1)}, bf16[192,384]{1,0:T(8,128)(2,1)S(1)}, u32[]{:S(2)}, u32[]{:S(2)}) collective-permute-start(bf16[192,384]{1,0:T(8,128)(2,1)} %collective-permute-done.9.refs_2_), channel_id=1, source_target_pairs={{0,16},{16,0},{1,17},{17,1},{2,18},{18,2},{3,19},{19,3},{4,20},{20... | collective-permute-start | bytes 442376 | tf_op jit(solution)/shard_map/ppermute | solution.py:800
  90.2 38.5 %collective-permute-start.12 = (bf16[192,384]{1,0:T(8,128)(2,1)S(1)}, bf16[192,384]{1,0:T(8,128)(2,1)S(1)}, u32[]{:S(2)}, u32[]{:S(2)}) collective-permute-start(bf16[192,384]{1,0:T(8,128)(2,1)S(1)} %collective-permute-done.11.refs_4_), channel_id=1, source_target_pairs={{0,16},{16,0},{1,17},{17,1},{2,18},{18,2},{3,19},{19,3},{4,20},{20... | collective-permute-start | bytes 442376 | tf_op jit(solution)/shard_map/ppermute | solution.py:800
  90.7 38.0 %collective-permute-start.14 = (bf16[192,384]{1,0:T(8,128)(2,1)S(1)}, bf16[192,384]{1,0:T(8,128)(2,1)S(1)}, u32[]{:S(2)}, u32[]{:S(2)}) collective-permute-start(bf16[192,384]{1,0:T(8,128)(2,1)S(1)} %collective-permute-done.13.refs_6_), channel_id=1, source_target_pairs={{0,16},{16,0},{1,17},{17,1},{2,18},{18,2},{3,19},{19,3},{4,20},{20... | collective-permute-start | bytes 442376 | tf_op jit(solution)/shard_map/ppermute | solution.py:800
  154.6 37.9 %all-to-all-start.3 = ((bf16[4,480,768]{2,1,0:T(8,128)(2,1)}), bf16[4,480,768]{2,1,0:T(8,128)(2,1)}, u32[]{:S(2)}, u32[]{:S(2)}) async-start(bf16[4,480,768]{2,1,0:T(8,128)(2,1)} %copy-done.13), calls=%async_computation.3 | async-start | bytes 5898240 | tf_op jit(solution)/shard_map/all_to_all | solution.py:840
  192.5 38.5 %all-to-all-start.2 = ((bf16[4,480,768]{2,1,0:T(8,128)(2,1)}), bf16[4,480,768]{2,1,0:T(8,128)(2,1)}, u32[]{:S(2)}, u32[]{:S(2)}) async-start(bf16[4,480,768]{2,1,0:T(8,128)(2,1)} %copy-done.12), calls=%async_computation.2 | async-start | bytes 5898240 | tf_op jit(solution)/shard_map/all_to_all | solution.py:840
  231.0 39.4 %all-to-all-start.5 = ((bf16[4,496,768]{2,1,0:T(8,128)(2,1)}), bf16[4,496,768]{2,1,0:T(8,128)(2,1)}, u32[]{:S(2)}, u32[]{:S(2)}) async-start(bf16[4,496,768]{2,1,0:T(8,128)(2,1)} %get-tuple-element.101), calls=%async_computation.5 | async-start | bytes 6094848 | tf_op jit(solution)/shard_map/all_to_all | solution.py:840
  270.4 39.6 %all-to-all-start.4 = ((bf16[4,496,768]{2,1,0:T(8,128)(2,1)}), bf16[4,496,768]{2,1,0:T(8,128)(2,1)}, u32[]{:S(2)}, u32[]{:S(2)}) async-start(bf16[4,496,768]{2,1,0:T(8,128)(2,1)} %get-tuple-element.100), calls=%async_computation.4 | async-start | bytes 6094848 | tf_op jit(solution)/shard_map/all_to_all | solution.py:840
  310.0 52.4 %collective-permute-start.50 = (f32[2,480]{1,0:T(2,128)S(1)}, f32[2,480]{1,0:T(2,128)S(1)}, u32[]{:S(2)}, u32[]{:S(2)}) collective-permute-start(f32[2,480]{1,0:T(2,128)S(1)} %get-tuple-element.193), channel_id=1, source_target_pairs={{0,4},{4,0},{8,12},{12,8},{1,5},{5,1},{9,13},{13,9},{2,6},{6,2},{1... | collective-permute-start | bytes 11528 | tf_op jit(solution)/shard_map/ppermute | solution.py:827
  311.4 53.1 %collective-permute-start.51 = (f32[2,480]{1,0:T(2,128)S(1)}, f32[2,480]{1,0:T(2,128)S(1)}, u32[]{:S(2)}, u32[]{:S(2)}) collective-permute-start(f32[2,480]{1,0:T(2,128)S(1)} %get-tuple-element.192), channel_id=1, source_target_pairs={{0,8},{4,12},{8,0},{12,4},{1,9},{5,13},{9,1},{13,5},{2,10},{6,14},... | collective-permute-start | bytes 11528 | tf_op jit(solution)/shard_map/ppermute | solution.py:827
  312.0 54.9 %collective-permute-start.52 = (f32[2,480]{1,0:T(2,128)S(1)}, f32[2,480]{1,0:T(2,128)S(1)}, u32[]{:S(2)}, u32[]{:S(2)}) collective-permute-start(f32[2,480]{1,0:T(2,128)S(1)} %get-tuple-element.191), channel_id=1, source_target_pairs={{0,12},{4,8},{8,4},{12,0},{1,13},{5,9},{9,5},{13,1},{2,14},{6,10},... | collective-permute-start | bytes 11528 | tf_op jit(solution)/shard_map/ppermute | solution.py:827
  349.6 47.0 %all-to-all-start.6 = ((bf16[4,480,768]{2,1,0:T(8,128)(2,1)}), bf16[4,480,768]{2,1,0:T(8,128)(2,1)}, u32[]{:S(2)}, u32[]{:S(2)}) async-start(bf16[4,480,768]{2,1,0:T(8,128)(2,1)} %convolution_convert_fusion.1), calls=%async_computation.6 | async-start | bytes 5898240 | tf_op jit(solution)/shard_map/all_to_all | solution.py:840
  354.4 39.8 %collective-permute-start.17 = (bf16[512,768]{1,0:T(8,128)(2,1)}, bf16[512,768]{1,0:T(8,128)(2,1)}, u32[]{:S(2)}, u32[]{:S(2)}) collective-permute-start(bf16[512,768]{1,0:T(8,128)(2,1)} %slice.192), channel_id=1, source_target_pairs={{0,1},{3,2},{4,5},{7,6},{8,9},{11,10},{12,13},{15,14},{16,17},{19,... | collective-permute-start | bytes 2359304 | tf_op jit(solution)/shard_map/ppermute | solution.py:809
  360.2 57.5 %collective-permute-start.20 = (bf16[528,768]{1,0:T(8,128)(2,1)}, bf16[528,768]{1,0:T(8,128)(2,1)}, u32[]{:S(2)}, u32[]{:S(2)}) collective-permute-start(bf16[528,768]{1,0:T(8,128)(2,1)} %slice.193), channel_id=1, source_target_pairs={{0,1},{3,2},{4,5},{7,6},{8,9},{11,10},{12,13},{15,14},{16,17},{19,... | collective-permute-start | bytes 2433032 | tf_op jit(solution)/shard_map/ppermute | solution.py:809
  362.4 49.5 %collective-permute-start.23 = (bf16[512,768]{1,0:T(8,128)(2,1)}, bf16[512,768]{1,0:T(8,128)(2,1)}, u32[]{:S(2)}, u32[]{:S(2)}) collective-permute-start(bf16[512,768]{1,0:T(8,128)(2,1)} %slice.194), channel_id=1, source_target_pairs={{0,1},{3,2},{4,5},{7,6},{8,9},{11,10},{12,13},{15,14},{16,17},{19,... | collective-permute-start | bytes 2359304 | tf_op jit(solution)/shard_map/ppermute | solution.py:809
  364.6 61.8 %collective-permute-start.26 = (bf16[528,768]{1,0:T(8,128)(2,1)}, bf16[528,768]{1,0:T(8,128)(2,1)}, u32[]{:S(2)}, u32[]{:S(2)}) collective-permute-start(bf16[528,768]{1,0:T(8,128)(2,1)} %slice.195), channel_id=1, source_target_pairs={{0,1},{3,2},{4,5},{7,6},{8,9},{11,10},{12,13},{15,14},{16,17},{19,... | collective-permute-start | bytes 2433032 | tf_op jit(solution)/shard_map/ppermute | solution.py:809
  394.2 241.8 %collective-permute-start.53 = (bf16[2,384,1024]{2,1,0:T(8,128)(2,1)}, bf16[2,384,1024]{2,1,0:T(8,128)(2,1)}, u32[]{:S(2)}, u32[]{:S(2)}) collective-permute-start(bf16[2,384,1024]{2,1,0:T(8,128)(2,1)} %fusion.5), channel_id=1, source_target_pairs={{0,16},{16,0},{1,17},{17,1},{2,18},{18,2},{3,19},{19,3},{4,20},{20... | collective-permute-start | bytes 4718600 | tf_op jit(solution)/shard_map/ppermute | solution.py:777
  396.6 41.8 %all-to-all-start.7 = ((bf16[4,480,768]{2,1,0:T(8,128)(2,1)}), bf16[4,480,768]{2,1,0:T(8,128)(2,1)}, u32[]{:S(2)}, u32[]{:S(2)}) async-start(bf16[4,480,768]{2,1,0:T(8,128)(2,1)} %convolution_convert_fusion), calls=%async_computation.7 | async-start | bytes 5898240 | tf_op jit(solution)/shard_map/all_to_all | solution.py:840
  432.3 40.0 %collective-permute-start.25 = (bf16[512,768]{1,0:T(8,128)(2,1)}, bf16[512,768]{1,0:T(8,128)(2,1)}, u32[]{:S(2)}, u32[]{:S(2)}) collective-permute-start(bf16[512,768]{1,0:T(8,128)(2,1)} %add_convert_fusion.12), channel_id=1, source_target_pairs={{1,0},{2,3},{5,4},{6,7},{9,8},{10,11},{13,12},{14,15},{17,16},{18,... | collective-permute-start | bytes 2359304 | tf_op jit(solution)/shard_map/ppermute | solution.py:818
  434.7 54.9 %collective-permute-start.22 = (bf16[528,768]{1,0:T(8,128)(2,1)}, bf16[528,768]{1,0:T(8,128)(2,1)}, u32[]{:S(2)}, u32[]{:S(2)}) collective-permute-start(bf16[528,768]{1,0:T(8,128)(2,1)} %add_convert_fusion.2), channel_id=1, source_target_pairs={{1,0},{2,3},{5,4},{6,7},{9,8},{10,11},{13,12},{14,15},{17,16},{18,... | collective-permute-start | bytes 2433032 | tf_op jit(solution)/shard_map/ppermute | solution.py:818
  437.1 98.5 %collective-permute-start.28 = (bf16[528,768]{1,0:T(8,128)(2,1)}, bf16[528,768]{1,0:T(8,128)(2,1)}, u32[]{:S(2)}, u32[]{:S(2)}) collective-permute-start(bf16[528,768]{1,0:T(8,128)(2,1)} %add_convert_fusion), channel_id=1, source_target_pairs={{1,0},{2,3},{5,4},{6,7},{9,8},{10,11},{13,12},{14,15},{17,16},{18,... | collective-permute-start | bytes 2433032 | tf_op jit(solution)/shard_map/ppermute | solution.py:818
  508.3 119.9 %collective-permute-start.38 = (bf16[512,768]{1,0:T(8,128)(2,1)S(1)}, bf16[512,768]{1,0:T(8,128)(2,1)}, u32[]{:S(2)}, u32[]{:S(2)}) collective-permute-start(bf16[512,768]{1,0:T(8,128)(2,1)S(1)} %get-tuple-element.131), channel_id=1, source_target_pairs={{0,1},{3,2},{4,5},{7,6},{8,9},{11,10},{12,13},{15,14},{16,17},{19,... | collective-permute-start | bytes 2359304 | tf_op jit(solution)/shard_map/ppermute | solution.py:809
  531.3 92.2 %collective-permute-start.32 = (bf16[512,768]{1,0:T(8,128)(2,1)S(1)}, bf16[512,768]{1,0:T(8,128)(2,1)}, u32[]{:S(2)}, u32[]{:S(2)}) collective-permute-start(bf16[512,768]{1,0:T(8,128)(2,1)S(1)} %get-tuple-element.123), channel_id=1, source_target_pairs={{0,1},{3,2},{4,5},{7,6},{8,9},{11,10},{12,13},{15,14},{16,17},{19,... | collective-permute-start | bytes 2359304 | tf_op jit(solution)/shard_map/ppermute | solution.py:809
  533.5 49.0 %collective-permute-start.30 = (bf16[512,768]{1,0:T(8,128)(2,1)S(1)}, bf16[512,768]{1,0:T(8,128)(2,1)}, u32[]{:S(2)}, u32[]{:S(2)}) collective-permute-start(bf16[512,768]{1,0:T(8,128)(2,1)S(1)} %get-tuple-element.117), channel_id=1, source_target_pairs={{0,1},{3,2},{4,5},{7,6},{8,9},{11,10},{12,13},{15,14},{16,17},{19,... | collective-permute-start | bytes 2359304 | tf_op jit(solution)/shard_map/ppermute | solution.py:809
  535.7 55.8 %collective-permute-start.29 = (bf16[512,768]{1,0:T(8,128)(2,1)S(1)}, bf16[512,768]{1,0:T(8,128)(2,1)}, u32[]{:S(2)}, u32[]{:S(2)}) collective-permute-start(bf16[512,768]{1,0:T(8,128)(2,1)S(1)} %get-tuple-element.116), channel_id=1, source_target_pairs={{0,1},{3,2},{4,5},{7,6},{8,9},{11,10},{12,13},{15,14},{16,17},{19,... | collective-permute-start | bytes 2359304 | tf_op jit(solution)/shard_map/ppermute | solution.py:809
  631.0 46.0 %collective-permute-start.33 = (bf16[512,768]{1,0:T(8,128)(2,1)}, bf16[512,768]{1,0:T(8,128)(2,1)}, u32[]{:S(2)}, u32[]{:S(2)}) collective-permute-start(bf16[512,768]{1,0:T(8,128)(2,1)} %add_convert_fusion.9), channel_id=1, source_target_pairs={{1,0},{2,3},{5,4},{6,7},{9,8},{10,11},{13,12},{14,15},{17,16},{18,... | collective-permute-start | bytes 2359304 | tf_op jit(solution)/shard_map/ppermute | solution.py:818
  634.8 40.6 %collective-permute-start.48 = (bf16[24,384]{1,0:T(8,128)(2,1)S(1)}, bf16[24,384]{1,0:T(8,128)(2,1)S(1)}, u32[]{:S(2)}, u32[]{:S(2)}) collective-permute-start(bf16[24,384]{1,0:T(8,128)(2,1)S(1)} %convert_add_fusion.3), channel_id=1, source_target_pairs={{0,4},{4,0},{8,12},{12,8},{1,5},{5,1},{9,13},{13,9},{2,6},{6,2},{1... | collective-permute-start | bytes 55304 | tf_op jit(solution)/shard_map/ppermute | solution.py:787
  674.1 42.3 %collective-permute-start.39 = (bf16[512,768]{1,0:T(8,128)(2,1)S(1)}, bf16[512,768]{1,0:T(8,128)(2,1)S(1)}, u32[]{:S(2)}, u32[]{:S(2)}) collective-permute-start(bf16[512,768]{1,0:T(8,128)(2,1)S(1)} %copy-done.87), channel_id=1, source_target_pairs={{1,0},{2,3},{5,4},{6,7},{9,8},{10,11},{13,12},{14,15},{17,16},{18,... | collective-permute-start | bytes 2359304 | tf_op jit(solution)/shard_map/ppermute | solution.py:818
  675.4 55.9 %collective-permute-start.40 = (bf16[512,768]{1,0:T(8,128)(2,1)S(1)}, bf16[512,768]{1,0:T(8,128)(2,1)S(1)}, u32[]{:S(2)}, u32[]{:S(2)}) collective-permute-start(bf16[512,768]{1,0:T(8,128)(2,1)S(1)} %add_convert_fusion.6), channel_id=1, source_target_pairs={{1,0},{2,3},{5,4},{6,7},{9,8},{10,11},{13,12},{14,15},{17,16},{18,... | collective-permute-start | bytes 2359304 | tf_op jit(solution)/shard_map/ppermute | solution.py:818
  708.1 41.8 %collective-permute-start.42 = (bf16[512,768]{1,0:T(8,128)(2,1)S(1)}, bf16[512,768]{1,0:T(8,128)(2,1)S(1)}, u32[]{:S(2)}, u32[]{:S(2)}) collective-permute-start(bf16[512,768]{1,0:T(8,128)(2,1)S(1)} %add_convert_fusion.4), channel_id=1, source_target_pairs={{1,0},{2,3},{5,4},{6,7},{9,8},{10,11},{13,12},{14,15},{17,16},{18,... | collective-permute-start | bytes 2359304 | tf_op jit(solution)/shard_map/ppermute | solution.py:818
  (150 other events, 2149.0 us)
